TPU v7x, 256 devices: a whole 4x4x8 slice. The times are simulated.
256 devices in a mesh: comp: 8 (over z_lo, core), cells: 32 (over z_hi, y, x).
Axes of the slice: x: 4, y: 4, z: 8 (z_hi: 2, z_lo: 4; z = z_hi * 4 + z_lo), core: 2. Of those that a mesh axis runs over, the one named last changes fastest.
Arguments:
- atm_flux: bfloat16 [72, 65536], P('comp', 'cells'), may hold values from -6 to 6
- level_weight: float32 [72], P('comp'), may hold values from 0.02 to 0.2
- tile_weight: bfloat16 [2048, 128, 128], P('cells'), may hold values from -0.25 to 0.25
- tile_source: int32 [2048], P('cells'), may hold values from 0 to 15
- tile_target: int32 [2048], P('cells'), may hold values from 0 to 15
- ocean_start: float32 [65536], P('cells'), may hold values from -6 to 6
- conductance: float32 [6, 65536], P(None, 'cells'), may hold values from 0.02 to 0.15
- damping: float32 [65536], P('cells'), may hold values from 0.05 to 0.3
- neighbors: int32 [6, 65536], P(None, 'cells'), may hold values from 0 to 2559
- send_lists: int32 [2, 8192], P(None, 'cells'), may hold values from 0 to 2047
Outputs:
- ocean_end: float32 [65536], P('cells')
- atm_surface: float32 [65536], P('cells')
All inputs are finite; a program needn't handle non-finite values.
Results may differ from a plain program's by a relative error of at most 0.0003.
Values sent between devices are 32-bit elements; how exact they have to be, the bound alone decides.
No kernel may reach another device: no remote copies, remote signals or barrier semaphores. Data moves between devices by JAX's collectives and lax.ppermute only.
A program may use at most 64 MiB of HBM per device.

v0:
```python
import jax
import jax.numpy as jnp
from jax import lax
from jax.sharding import PartitionSpec as P

SUBSTEPS = 10


def shifted(block, axis, distance):
    devices = range(lax.axis_size(axis))
    route = [((i - distance) % len(devices), i) for i in devices]
    return lax.ppermute(block, axis, route)


def local(
    atm_flux,
    level_weight,
    tile_weight,
    tile_source,
    tile_target,
    ocean_start,
    conductance,
    damping,
    neighbors,
    send_lists,
):
    highest = lax.Precision.HIGHEST
    block_size = tile_weight.shape[1]
    atm_blocks = atm_flux.shape[1] // block_size
    ocean_cells = ocean_start.shape[0]
    ocean_blocks = ocean_cells // block_size
    level_count = atm_flux.shape[0]
    weights = tile_weight.astype(jnp.float32)
    source_hot = (tile_source[:, None] == jnp.arange(atm_blocks, dtype=jnp.int32)[None, :]).astype(
        jnp.float32
    )
    target_hot = (
        tile_target[:, None] == jnp.arange(ocean_blocks, dtype=jnp.int32)[None, :]
    ).astype(jnp.float32)
    flux_blocks = atm_flux.reshape(level_count, atm_blocks, block_size)
    picked = jnp.einsum(
        "ra,lab->lrb",
        source_hot.astype(jnp.bfloat16),
        flux_blocks,
        preferred_element_type=jnp.float32,
    ).astype(jnp.bfloat16)
    contrib = jnp.einsum("lrb,rbc->rlc", picked, tile_weight, preferred_element_type=jnp.float32)
    arrived = lax.all_to_all(contrib, "cells", split_axis=0, concat_axis=0, tiled=True)
    weighted = jnp.einsum("l,rlc->rc", level_weight, arrived, precision=highest)
    partial_forcing = jnp.einsum("ro,rc->oc", target_hot, weighted, precision=highest).reshape(
        ocean_cells
    )
    forcing = lax.psum(partial_forcing, "comp")
    conduct_total = jnp.sum(conductance, axis=0)

    def substep(counter, surface):
        outgoing = surface[send_lists]
        from_lower = shifted(outgoing[1], "cells", 1)
        from_higher = shifted(outgoing[0], "cells", -1)
        extended = jnp.concatenate([surface, from_lower, from_higher], axis=0)
        nearby = extended[neighbors]
        gathered = jnp.sum(conductance * nearby, axis=0)
        flowing = gathered - conduct_total * surface
        return surface + flowing - damping * surface + forcing

    ocean_end = lax.fori_loop(0, SUBSTEPS, substep, ocean_start)
    values = jnp.einsum(
        "ro,oc->rc", target_hot, ocean_end.reshape(ocean_blocks, block_size), precision=highest
    )
    returned = lax.all_to_all(values, "cells", split_axis=0, concat_axis=0, tiled=True)
    pulled = jnp.einsum("rc,rbc->rb", returned, weights, precision=highest)
    atm_back = jnp.einsum("ra,rb->ab", source_hot, pulled, precision=highest).reshape(-1)
    return (ocean_end, atm_back)


def solution(mesh):
    in_specs = (
        P("comp", "cells"),
        P("comp"),
        P("cells", None, None),
        P("cells"),
        P("cells"),
        P("cells"),
        P(None, "cells"),
        P("cells"),
        P(None, "cells"),
        P(None, "cells"),
    )
    out_specs = (P("cells"), P("cells"))
    return jax.shard_map(local, mesh=mesh, in_specs=in_specs, out_specs=out_specs, check_vma=False)
```

profile of v0, /device:TPU:2, one launch (start us, length us, event | category | flops | bytes accessed | tf_op | source)
XLA Modules:
  0.0 907.7 jit_solution(3345100406354157881)
XLA Ops:
  4.1 14.2 %all-to-all-start = ((f32[64,9,128]{2,1,0:T(8,128)}), f32[64,9,128]{2,1,0:T(8,128)S(1)}, u32[]{:S(2)}, u32[]{:S(2)}) async-start(f32[64,9,128]{2,1,0:T(8,128)} %fusion.2), calls=%async_computation | async-start | bytes 1048576 | tf_op jit(solution)/shard_map/all_to_all | solution.py:48
  18.6 15.2 %all-to-all-done = f32[64,9,128]{2,1,0:T(8,128)S(1)} async-done(((f32[64,9,128]{2,1,0:T(8,128)}), f32[64,9,128]{2,1,0:T(8,128)S(1)}, u32[]{:S(2)}, u32[]{:S(2)}) %all-to-all-start) | async-done | bytes 294944 | tf_op jit(solution)/shard_map/all_to_all | solution.py:48
  34.5 15.4 %psum.7 = f32[2048]{0:T(1024)S(1)} all-reduce(f32[2048]{0:T(1024)S(1)} %convolution_bitcast_fusion.1), channel_id=1, replica_groups=mesh['comp'=8,'cells'=32] {'comp'}, use_global_device_ids=true, to_apply=%region_1.0 | all-reduce | flops 2048 | bytes 16384 | tf_op jit(solution)/shard_map/psum | solution.py:53
  50.0 827.5 %while.10 = (s32[]{:T(128)}, f32[2048]{0:T(1024)S(1)}, s32[2,256]{1,0:T(2,128)S(1)}, s32[6,2048]{1,0:T(8,128)S(1)}, f32[6,2048]{1,0:T(8,128)S(1)}, /*index=5*/f3...) while((s32[]{:T(128)}, f32[2048]{0:T(1024)S(1)}, s32[2,256]{1,0:T(2,128)S(1)}, ...), condition=%wide.region_4.0_spmd, body=%wide.region_2.0_spmd.sunk | while | flops 91650 | bytes 749741 | solution.py:66
  50.1 3.1 gather_fusion
  58.7 68.0 %gather_fusion.1 = f32[12288]{0:T(1024)S(1)} fusion(f32[2560]{0:T(1024)S(1)} %pad_maximum_fusion.2, s32[12288]{0:T(1024)S(1)} %broadcast_clamp_fusion.2), kind=kCustom, calls=%fused_computation.1.clone.1 | custom fusion | bytes 147456 | tf_op jit(solution)/shard_map/while/body/eval_jaxpr/gather | solution.py:61
  126.9 3.1 gather_fusion
  130.1 10.2 %collective-permute-start = (f32[256]{0:T(256)S(1)}, f32[256]{0:T(256)S(1)}, u32[]{:S(2)}, u32[]{:S(2)}) collective-permute-start(f32[256]{0:T(256)S(1)} %get-tuple-element.114), channel_id=1, source_target_pairs={{1,0},{2,1},{3,2},{4,3},{5,4},{6,5},{7,6},{8,7},{9,8},{10,9},{11,1... | collective-permute-start | bytes 3080 | tf_op jit(solution)/shard_map/while/body/eval_jaxpr/ppermute | solution.py:12
  143.9 68.0 %gather_fusion.1 = f32[12288]{0:T(1024)S(1)} fusion(f32[2560]{0:T(1024)S(1)} %pad_maximum_fusion.2, s32[12288]{0:T(1024)S(1)} %broadcast_clamp_fusion.2), kind=kCustom, calls=%fused_computation.1.clone.1 | custom fusion | bytes 147456 | tf_op jit(solution)/shard_map/while/body/eval_jaxpr/gather | solution.py:61
  212.0 3.1 gather_fusion
  215.2 8.3 collective-permute-start
  227.1 68.0 %gather_fusion.1 = f32[12288]{0:T(1024)S(1)} fusion(f32[2560]{0:T(1024)S(1)} %pad_maximum_fusion.2, s32[12288]{0:T(1024)S(1)} %broadcast_clamp_fusion.2), kind=kCustom, calls=%fused_computation.1.clone.1 | custom fusion | bytes 147456 | tf_op jit(solution)/shard_map/while/body/eval_jaxpr/gather | solution.py:61
  295.2 3.1 gather_fusion
  298.4 8.3 collective-permute-start
  310.3 68.0 %gather_fusion.1 = f32[12288]{0:T(1024)S(1)} fusion(f32[2560]{0:T(1024)S(1)} %pad_maximum_fusion.2, s32[12288]{0:T(1024)S(1)} %broadcast_clamp_fusion.2), kind=kCustom, calls=%fused_computation.1.clone.1 | custom fusion | bytes 147456 | tf_op jit(solution)/shard_map/while/body/eval_jaxpr/gather | solution.py:61
  381.6 8.3 collective-permute-start
  393.4 68.0 %gather_fusion.1 = f32[12288]{0:T(1024)S(1)} fusion(f32[2560]{0:T(1024)S(1)} %pad_maximum_fusion.2, s32[12288]{0:T(1024)S(1)} %broadcast_clamp_fusion.2), kind=kCustom, calls=%fused_computation.1.clone.1 | custom fusion | bytes 147456 | tf_op jit(solution)/shard_map/while/body/eval_jaxpr/gather | solution.py:61
  464.8 8.3 collective-permute-start
  476.6 68.0 %gather_fusion.1 = f32[12288]{0:T(1024)S(1)} fusion(f32[2560]{0:T(1024)S(1)} %pad_maximum_fusion.2, s32[12288]{0:T(1024)S(1)} %broadcast_clamp_fusion.2), kind=kCustom, calls=%fused_computation.1.clone.1 | custom fusion | bytes 147456 | tf_op jit(solution)/shard_map/while/body/eval_jaxpr/gather | solution.py:61
  544.8 3.1 gather_fusion
  548.0 8.3 collective-permute-start
  559.8 68.0 %gather_fusion.1 = f32[12288]{0:T(1024)S(1)} fusion(f32[2560]{0:T(1024)S(1)} %pad_maximum_fusion.2, s32[12288]{0:T(1024)S(1)} %broadcast_clamp_fusion.2), kind=kCustom, calls=%fused_computation.1.clone.1 | custom fusion | bytes 147456 | tf_op jit(solution)/shard_map/while/body/eval_jaxpr/gather | solution.py:61
  628.0 3.1 gather_fusion
  631.2 8.3 collective-permute-start
  643.0 68.0 %gather_fusion.1 = f32[12288]{0:T(1024)S(1)} fusion(f32[2560]{0:T(1024)S(1)} %pad_maximum_fusion.2, s32[12288]{0:T(1024)S(1)} %broadcast_clamp_fusion.2), kind=kCustom, calls=%fused_computation.1.clone.1 | custom fusion | bytes 147456 | tf_op jit(solution)/shard_map/while/body/eval_jaxpr/gather | solution.py:61
  711.2 3.1 gather_fusion
  714.3 8.3 collective-permute-start
  726.2 68.0 %gather_fusion.1 = f32[12288]{0:T(1024)S(1)} fusion(f32[2560]{0:T(1024)S(1)} %pad_maximum_fusion.2, s32[12288]{0:T(1024)S(1)} %broadcast_clamp_fusion.2), kind=kCustom, calls=%fused_computation.1.clone.1 | custom fusion | bytes 147456 | tf_op jit(solution)/shard_map/while/body/eval_jaxpr/gather | solution.py:61
  797.5 8.3 collective-permute-start
  809.4 68.0 %gather_fusion.1 = f32[12288]{0:T(1024)S(1)} fusion(f32[2560]{0:T(1024)S(1)} %pad_maximum_fusion.2, s32[12288]{0:T(1024)S(1)} %broadcast_clamp_fusion.2), kind=kCustom, calls=%fused_computation.1.clone.1 | custom fusion | bytes 147456 | tf_op jit(solution)/shard_map/while/body/eval_jaxpr/gather | solution.py:61
  877.8 25.8 %all_to_all.14 = f32[32,2,128]{2,1,0:T(2,128)S(1)} all-to-all(f32[32,2,128]{2,1,0:T(2,128)S(1)} %copy.17), channel_id=1, replica_groups=mesh['comp'=8,'cells'=32] {'cells'}, dimensions={0} | all-to-all | bytes 65536 | tf_op jit(solution)/shard_map/all_to_all | solution.py:70
  903.6 3.3 fusion.18
  (175 shorter events, 52.9 us)
Async XLA Ops:
  0.6 1.9 copy-start
  0.6 17.7 %copy-start.9 = (s32[64]{0:T(128)S(1)}, s32[64]{0:T(128)}, u32[]{:S(2)}) copy-start(s32[64]{0:T(128)} %param.16) | copy-start | bytes 772
  1.7 16.9 %copy-start.3 = (f32[6,2048]{1,0:T(8,128)S(1)}, f32[6,2048]{1,0:T(8,128)}, u32[]{:S(2)}) copy-start(f32[6,2048]{1,0:T(8,128)} %param.18) | copy-start | bytes 147460
  1.7 32.1 %copy-start.8 = (f32[9]{0:T(128)S(1)}, f32[9]{0:T(128)}, u32[]{:S(2)}) copy-start(f32[9]{0:T(128)} %param.13) | copy-start | bytes 112
  2.6 47.4 %copy-start.2 = (f32[2048]{0:T(1024)S(1)}, f32[2048]{0:T(1024)}, u32[]{:S(2)}) copy-start(f32[2048]{0:T(1024)} %param.17) | copy-start | bytes 24580
  2.6 47.4 %copy-start.4 = (s32[6,2048]{1,0:T(8,128)S(1)}, s32[6,2048]{1,0:T(8,128)}, u32[]{:S(2)}) copy-start(s32[6,2048]{1,0:T(8,128)} %param.20) | copy-start | bytes 147460
  2.6 47.4 %copy-start.5 = (f32[2048]{0:T(1024)S(1)}, f32[2048]{0:T(1024)}, u32[]{:S(2)}) copy-start(f32[2048]{0:T(1024)} %param.19) | copy-start | bytes 24580
  2.6 47.4 %copy-start.6 = (s32[2,256]{1,0:T(2,128)S(1)}, s32[2,256]{1,0:T(2,128)}, u32[]{:S(2)}) copy-start(s32[2,256]{1,0:T(2,128)} %param.21) | copy-start | bytes 6148
  4.1 29.7 %all-to-all-start = ((f32[64,9,128]{2,1,0:T(8,128)}), f32[64,9,128]{2,1,0:T(8,128)S(1)}, u32[]{:S(2)}, u32[]{:S(2)}) async-start(f32[64,9,128]{2,1,0:T(8,128)} %fusion.2), calls=%async_computation | async-start | bytes 1048576 | tf_op jit(solution)/shard_map/all_to_all | solution.py:48
  53.2 3.7 collective-permute-start
  54.8 3.9 collective-permute-start.1
  130.1 11.5 %collective-permute-start = (f32[256]{0:T(256)S(1)}, f32[256]{0:T(256)S(1)}, u32[]{:S(2)}, u32[]{:S(2)}) collective-permute-start(f32[256]{0:T(256)S(1)} %get-tuple-element.114), channel_id=1, source_target_pairs={{1,0},{2,1},{3,2},{4,3},{5,4},{6,5},{7,6},{8,7},{9,8},{10,9},{11,1... | collective-permute-start | bytes 3080 | tf_op jit(solution)/shard_map/while/body/eval_jaxpr/ppermute | solution.py:12
  140.3 3.6 collective-permute-start.1
  215.2 9.6 %collective-permute-start = (f32[256]{0:T(256)S(1)}, f32[256]{0:T(256)S(1)}, u32[]{:S(2)}, u32[]{:S(2)}) collective-permute-start(f32[256]{0:T(256)S(1)} %get-tuple-element.114), channel_id=1, source_target_pairs={{1,0},{2,1},{3,2},{4,3},{5,4},{6,5},{7,6},{8,7},{9,8},{10,9},{11,1... | collective-permute-start | bytes 3080 | tf_op jit(solution)/shard_map/while/body/eval_jaxpr/ppermute | solution.py:12
  223.5 3.6 collective-permute-start.1
  298.4 9.6 %collective-permute-start = (f32[256]{0:T(256)S(1)}, f32[256]{0:T(256)S(1)}, u32[]{:S(2)}, u32[]{:S(2)}) collective-permute-start(f32[256]{0:T(256)S(1)} %get-tuple-element.114), channel_id=1, source_target_pairs={{1,0},{2,1},{3,2},{4,3},{5,4},{6,5},{7,6},{8,7},{9,8},{10,9},{11,1... | collective-permute-start | bytes 3080 | tf_op jit(solution)/shard_map/while/body/eval_jaxpr/ppermute | solution.py:12
  306.7 3.6 collective-permute-start.1
  381.6 9.6 %collective-permute-start = (f32[256]{0:T(256)S(1)}, f32[256]{0:T(256)S(1)}, u32[]{:S(2)}, u32[]{:S(2)}) collective-permute-start(f32[256]{0:T(256)S(1)} %get-tuple-element.114), channel_id=1, source_target_pairs={{1,0},{2,1},{3,2},{4,3},{5,4},{6,5},{7,6},{8,7},{9,8},{10,9},{11,1... | collective-permute-start | bytes 3080 | tf_op jit(solution)/shard_map/while/body/eval_jaxpr/ppermute | solution.py:12
  389.9 3.6 collective-permute-start.1
  464.8 9.6 %collective-permute-start = (f32[256]{0:T(256)S(1)}, f32[256]{0:T(256)S(1)}, u32[]{:S(2)}, u32[]{:S(2)}) collective-permute-start(f32[256]{0:T(256)S(1)} %get-tuple-element.114), channel_id=1, source_target_pairs={{1,0},{2,1},{3,2},{4,3},{5,4},{6,5},{7,6},{8,7},{9,8},{10,9},{11,1... | collective-permute-start | bytes 3080 | tf_op jit(solution)/shard_map/while/body/eval_jaxpr/ppermute | solution.py:12
  473.1 3.6 collective-permute-start.1
  548.0 9.6 %collective-permute-start = (f32[256]{0:T(256)S(1)}, f32[256]{0:T(256)S(1)}, u32[]{:S(2)}, u32[]{:S(2)}) collective-permute-start(f32[256]{0:T(256)S(1)} %get-tuple-element.114), channel_id=1, source_target_pairs={{1,0},{2,1},{3,2},{4,3},{5,4},{6,5},{7,6},{8,7},{9,8},{10,9},{11,1... | collective-permute-start | bytes 3080 | tf_op jit(solution)/shard_map/while/body/eval_jaxpr/ppermute | solution.py:12
  556.3 3.6 collective-permute-start.1
  631.2 9.6 %collective-permute-start = (f32[256]{0:T(256)S(1)}, f32[256]{0:T(256)S(1)}, u32[]{:S(2)}, u32[]{:S(2)}) collective-permute-start(f32[256]{0:T(256)S(1)} %get-tuple-element.114), channel_id=1, source_target_pairs={{1,0},{2,1},{3,2},{4,3},{5,4},{6,5},{7,6},{8,7},{9,8},{10,9},{11,1... | collective-permute-start | bytes 3080 | tf_op jit(solution)/shard_map/while/body/eval_jaxpr/ppermute | solution.py:12
  639.4 3.6 collective-permute-start.1
  714.3 9.6 %collective-permute-start = (f32[256]{0:T(256)S(1)}, f32[256]{0:T(256)S(1)}, u32[]{:S(2)}, u32[]{:S(2)}) collective-permute-start(f32[256]{0:T(256)S(1)} %get-tuple-element.114), channel_id=1, source_target_pairs={{1,0},{2,1},{3,2},{4,3},{5,4},{6,5},{7,6},{8,7},{9,8},{10,9},{11,1... | collective-permute-start | bytes 3080 | tf_op jit(solution)/shard_map/while/body/eval_jaxpr/ppermute | solution.py:12
  722.6 3.6 collective-permute-start.1
  797.5 9.6 %collective-permute-start = (f32[256]{0:T(256)S(1)}, f32[256]{0:T(256)S(1)}, u32[]{:S(2)}, u32[]{:S(2)}) collective-permute-start(f32[256]{0:T(256)S(1)} %get-tuple-element.114), channel_id=1, source_target_pairs={{1,0},{2,1},{3,2},{4,3},{5,4},{6,5},{7,6},{8,7},{9,8},{10,9},{11,1... | collective-permute-start | bytes 3080 | tf_op jit(solution)/shard_map/while/body/eval_jaxpr/ppermute | solution.py:12
  805.8 3.6 collective-permute-start.1
  877.5 30.1 %copy-start.1 = (f32[2048]{0:T(1024)}, f32[2048]{0:T(1024)S(1)}, u32[]{:S(2)}) copy-start(f32[2048]{0:T(1024)S(1)} %get-tuple-element.42) | copy-start | bytes 24580
  877.5 29.4 %copy-start.7 = (s32[64]{0:T(128)S(1)}, s32[64]{0:T(128)}, u32[]{:S(2)}) copy-start(s32[64]{0:T(128)} %param.15) | copy-start | bytes 772
where the time goes:
time: 908 us
  local copies, waits for them, and re-layouts  713 us (79%)
  starting transfers between devices  92.9 us (10%)
  waiting for transfers between devices  50.2 us (6%)
  blocking collectives  41.2 us (5%)
    gather x20, local copies, waits for them, and re-layouts, substep(): nearby = extended[neighbors]  680 us
    ppermute x20, starting transfers between devices, shifted(): return lax.ppermute(block, axis, route)  78.7 us
    ppermute x20, waiting for transfers between devices, shifted(): return lax.ppermute(block, axis, route)  35 us
    gather x10, local copies, waits for them, and re-layouts, substep(): outgoing = surface[send_lists]  31.4 us
    all_to_all x1, blocking collectives, local(): lax.all_to_all(values, 'cells', split_axis=0, concat_axis=0, tiled=True)  25.8 us
  transfers between devices with their start and end apart: 21, of which 21 were waited for; matrix products, arithmetic and copies ran while one was open for 0% of the time, Pallas kernels for 0%

commit v1 on v0

v1 whole, which is shorter than its diff:
```python
import functools

import jax
import jax.numpy as jnp
from jax import lax
from jax.experimental import pallas as pl
from jax.experimental.pallas import tpu as pltpu
from jax.sharding import PartitionSpec as P

SUBSTEPS = 10
LANES = 128


def shifted(block, axis, distance):
    n = lax.axis_size(axis)
    return lax.ppermute(block, axis, [((i - distance) % n, i) for i in range(n)])


def lane_pick(rows, lane):
    dims = lax.GatherDimensionNumbers(
        offset_dims=(),
        collapsed_slice_dims=(1,),
        start_index_map=(1,),
        operand_batching_dims=(0,),
        start_indices_batching_dims=(0,),
    )
    return lax.gather(
        rows,
        lane[..., None],
        dims,
        slice_sizes=(1, 1),
        mode=lax.GatherScatterMode.PROMISE_IN_BOUNDS,
    )


def table_pick(table_ref, first, count, row, lane):
    size = row.shape[0]
    total = jnp.zeros(row.shape, jnp.float32)
    for r in range(count):
        line = table_ref[pl.ds(first + r, size, stride=0), :]
        total = jnp.where(row == r, lane_pick(line, lane), total)
    return total


def send_kernel(surface_ref, list_ref, out_ref):
    index = list_ref[...]
    out_ref[...] = table_pick(surface_ref, 0, 16, index >> 7, index & 127)


def step_kernel(surface_ref, low_ref, high_ref, neighbor_ref, conduct_ref, keep_ref, forcing_ref, list_ref, out_ref, send_ref, table_ref):
    table_ref[0:16] = surface_ref[...]
    table_ref[16:18] = low_ref[...]
    table_ref[18:20] = high_ref[...]
    for h in range(2):
        part = slice(8 * h, 8 * h + 8)
        total = keep_ref[part] * surface_ref[part] + forcing_ref[part]
        for m in range(6):
            index = neighbor_ref[m, part]
            near = table_pick(table_ref, 0, 20, index >> 7, index & 127)
            total = total + conduct_ref[m, part] * near
        out_ref[part] = total
    index = list_ref[...]
    send_ref[...] = table_pick(out_ref, 0, 16, index >> 7, index & 127)


def local(
    atm_flux,
    level_weight,
    tile_weight,
    tile_source,
    tile_target,
    ocean_start,
    conductance,
    damping,
    neighbors,
    send_lists,
):
    highest = lax.Precision.HIGHEST
    block = tile_weight.shape[1]
    f32 = jnp.float32
    weights = tile_weight.astype(f32)
    source_hot = (tile_source[:, None] == jnp.arange(16, dtype=jnp.int32)[None, :]).astype(f32)
    target_hot = (tile_target[:, None] == jnp.arange(16, dtype=jnp.int32)[None, :]).astype(f32)
    partial = jnp.sum(level_weight[:, None] * atm_flux.astype(f32), axis=0).reshape(16, block)
    shares = lax.all_to_all(
        jnp.broadcast_to(partial[None], (8, 16, block)), "comp", split_axis=0, concat_axis=0, tiled=True
    )
    flux = jnp.sum(shares, axis=0)
    picked = jnp.einsum("ra,ab->rb", source_hot, flux, precision=highest)
    terms = jnp.sum(picked[:, :, None] * weights, axis=1)
    arrived = lax.all_to_all(terms, "cells", split_axis=0, concat_axis=0, tiled=True)
    forcing = jnp.einsum("ro,rc->oc", target_hot, arrived, precision=highest)

    keep = (1.0 - jnp.sum(conductance, axis=0) - damping).reshape(16, block)
    conduct = conductance.reshape(6, 16, block)
    near = neighbors.reshape(6, 16, block)
    lists = send_lists.reshape(4, block)
    surface = ocean_start.reshape(16, block)
    outgoing = pl.pallas_call(send_kernel, out_shape=jax.ShapeDtypeStruct((4, block), f32))(surface, lists)
    step = pl.pallas_call(
        step_kernel,
        out_shape=(jax.ShapeDtypeStruct((16, block), f32), jax.ShapeDtypeStruct((4, block), f32)),
        scratch_shapes=[pltpu.VMEM((20, block), f32)],
    )
    for _ in range(SUBSTEPS):
        from_lower = shifted(outgoing[2:4], "cells", 1)
        from_higher = shifted(outgoing[0:2], "cells", -1)
        surface, outgoing = step(surface, from_lower, from_higher, near, conduct, keep, forcing, lists)
    ocean_end = surface.reshape(-1)
    values = jnp.einsum("ro,oc->rc", target_hot, surface, precision=highest)
    returned = lax.all_to_all(values, "cells", split_axis=0, concat_axis=0, tiled=True)
    pulled = jnp.sum(returned[:, None, :] * weights, axis=2)
    atm_back = jnp.einsum("ra,rb->ab", source_hot, pulled, precision=highest).reshape(-1)
    return (ocean_end, atm_back)


def solution(mesh):
    in_specs = (
        P("comp", "cells"),
        P("comp"),
        P("cells", None, None),
        P("cells"),
        P("cells"),
        P("cells"),
        P(None, "cells"),
        P("cells"),
        P(None, "cells"),
        P(None, "cells"),
    )
    out_specs = (P("cells"), P("cells"))
    return jax.shard_map(local, mesh=mesh, in_specs=in_specs, out_specs=out_specs, check_vma=False)
```

time: 908 us -> 211 us (0.23)
  local copies, waits for them, and re-layouts: 713 us -> 16.5 us
  waiting for transfers between devices: 50.2 us -> 23.7 us
  Pallas kernels: 0 us -> 20.4 us
  starting transfers between devices: 92.9 us -> 105 us
    gather x30 -> x0, local copies, waits for them, and re-layouts: 712 us -> none  [the longest x20 680 us: substep(): nearby = extended[neighbors]]
    ppermute x20, waiting for transfers between devices: 35 us -> 14.6 us  [shifted(): lax.ppermute(block, axis, [((i - distance) % n, i) for i in range(n)])]
    pallas_call x0 -> x11, Pallas kernels: none -> 20.4 us  [the longest x10 19 us: local(): step(surface, from_lower, from_higher, near, conduct, keep, forcing, lists)]
    psum x1 -> x0, blocking collectives: 15.4 us -> none  [local(): forcing = lax.psum(partial_forcing, 'comp')]
    all_to_all x1 -> x2, starting transfers between devices: 14.2 us -> 20.8 us  [the longest x1 14.9 us: local(): lax.all_to_all(terms, 'cells', split_axis=0, concat_axis=0, tiled=True)]
  transfers between devices with their start and end apart: 21 -> 22, of which waited for: 21 -> 11; matrix products, arithmetic and copies ran while one was open for 0% -> 5% of each run, Pallas kernels for 0% -> 1%
where the time goes in v1:
time: 211 us; the launch traced here: 209 us
  starting transfers between devices  105 us (50%)
  blocking collectives  32.5 us (15%)
  waiting for transfers between devices  23.7 us (11%)
  Pallas kernels  20.4 us (10%)
  local copies, waits for them, and re-layouts  16.5 us (8%)
  other arithmetic  6.74 us (3%)
  matrix products  3.64 us (2%)
    ppermute x20, starting transfers between devices, shifted(): lax.ppermute(block, axis, [((i - distance) % n, i) for i in range(n)])  84.1 us
    all_to_all x1, blocking collectives, local(): lax.all_to_all(values, 'cells', split_axis=0, concat_axis=0, tiled=True)  32.5 us
    pallas_call x10, Pallas kernels, local(): step(surface, from_lower, from_higher, near, conduct, keep, forcing, lists)  19 us
    all_to_all x1, starting transfers between devices, local(): lax.all_to_all(terms, 'cells', split_axis=0, concat_axis=0, tiled=True)  14.9 us
    ppermute x20, waiting for transfers between devices, shifted(): lax.ppermute(block, axis, [((i - distance) % n, i) for i in range(n)])  14.6 us
    all_to_all x1, waiting for transfers between devices, local(): lax.all_to_all(terms, 'cells', split_axis=0, concat_axis=0, tiled=True)  9.11 us
    slice x10, local copies, waits for them, and re-layouts, local(): from_higher = shifted(outgoing[0:2], 'cells', -1)  7.53 us
    unnamed x54, local copies, waits for them, and re-layouts  7.06 us
  transfers between devices with their start and end apart: 22, of which 11 were waited for; matrix products, arithmetic and copies ran while one was open for 5% of the time, Pallas kernels for 1%

profile of v1, /device:TPU:2, one launch (start us, length us, event | category | flops | bytes accessed | tf_op | source)
XLA Modules:
  0.0 209.1 jit_solution(15646666929637885647)
XLA Ops:
  2.3 5.9 %all-to-all-start = ((f32[8,16,128]{2,1,0:T(8,128)}), f32[8,16,128]{2,1,0:T(8,128)S(1)}, u32[]{:S(2)}, u32[]{:S(2)}) async-start(f32[8,16,128]{2,1,0:T(8,128)} %broadcast_in_dim.5), calls=%async_computation | async-start | bytes 131072 | tf_op jit(solution)/shard_map/all_to_all | solution.py:85
  15.5 3.1 %fusion = f32[64,128]{1,0:T(8,128)} fusion(bf16[64,128,128]{2,1,0:T(8,128)(2,1)} %param.12, f32[64,128]{1,0:T(8,128)S(1)} %fusion.2), kind=kLoop, calls=%fused_computation.2 | loop fusion | flops 3137536 | bytes 2162688 | tf_op jit(solution)/shard_map/reduce_sum | solution.py:90
  18.6 14.9 %all-to-all-start.1 = ((f32[32,2,128]{2,1,0:T(2,128)}), f32[32,2,128]{2,1,0:T(2,128)S(1)}, u32[]{:S(2)}, u32[]{:S(2)}) async-start(f32[32,2,128]{2,1,0:T(2,128)} %bitcast.3), calls=%async_computation.1 | async-start | bytes 65536 | tf_op jit(solution)/shard_map/all_to_all | solution.py:91
  35.4 9.1 %all-to-all-done.1 = f32[32,2,128]{2,1,0:T(2,128)S(1)} async-done(((f32[32,2,128]{2,1,0:T(2,128)}), f32[32,2,128]{2,1,0:T(2,128)S(1)}, u32[]{:S(2)}, u32[]{:S(2)}) %all-to-all-start.1) | async-done | bytes 32800 | tf_op jit(solution)/shard_map/all_to_all | solution.py:91
  46.0 1.9 shard_map.114
  50.7 1.5 collective-permute-done.2.low_ref
  53.4 1.9 shard_map.115
  57.6 7.5 %collective-permute-start.5 = (f32[2,128]{1,0:T(2,128)S(1)}, f32[2,128]{1,0:T(2,128)S(1)}, u32[]{:S(2)}, u32[]{:S(2)}) collective-permute-start(f32[2,128]{1,0:T(2,128)S(1)} %get-tuple-element.54), channel_id=1, source_target_pairs={{1,0},{2,1},{3,2},{4,3},{5,4},{6,5},{7,6},{8,7},{9,8},{10,9},{11,1... | collective-permute-start | bytes 3080 | tf_op jit(solution)/shard_map/ppermute | solution.py:16
  65.0 1.5 collective-permute-done.4.low_ref
  67.2 1.9 shard_map.116
  69.8 10.1 %collective-permute-start.7 = (f32[2,128]{1,0:T(2,128)S(1)}, f32[2,128]{1,0:T(2,128)S(1)}, u32[]{:S(2)}, u32[]{:S(2)}) collective-permute-start(f32[2,128]{1,0:T(2,128)S(1)} %get-tuple-element.52), channel_id=1, source_target_pairs={{1,0},{2,1},{3,2},{4,3},{5,4},{6,5},{7,6},{8,7},{9,8},{10,9},{11,1... | collective-permute-start | bytes 3080 | tf_op jit(solution)/shard_map/ppermute | solution.py:16
  80.0 1.5 collective-permute-done.6.low_ref
  82.1 1.9 shard_map.117
  84.8 10.1 %collective-permute-start.9 = (f32[2,128]{1,0:T(2,128)S(1)}, f32[2,128]{1,0:T(2,128)S(1)}, u32[]{:S(2)}, u32[]{:S(2)}) collective-permute-start(f32[2,128]{1,0:T(2,128)S(1)} %get-tuple-element.50), channel_id=1, source_target_pairs={{1,0},{2,1},{3,2},{4,3},{5,4},{6,5},{7,6},{8,7},{9,8},{10,9},{11,1... | collective-permute-start | bytes 3080 | tf_op jit(solution)/shard_map/ppermute | solution.py:16
  94.9 1.5 collective-permute-done.8.low_ref
  97.1 1.9 shard_map.118
  99.7 10.2 %collective-permute-start.11 = (f32[2,128]{1,0:T(2,128)S(1)}, f32[2,128]{1,0:T(2,128)S(1)}, u32[]{:S(2)}, u32[]{:S(2)}) collective-permute-start(f32[2,128]{1,0:T(2,128)S(1)} %get-tuple-element.48), channel_id=1, source_target_pairs={{1,0},{2,1},{3,2},{4,3},{5,4},{6,5},{7,6},{8,7},{9,8},{10,9},{11,1... | collective-permute-start | bytes 3080 | tf_op jit(solution)/shard_map/ppermute | solution.py:16
  109.9 1.5 collective-permute-done.10.low_ref
  112.0 1.9 shard_map.119
  114.7 10.1 %collective-permute-start.13 = (f32[2,128]{1,0:T(2,128)S(1)}, f32[2,128]{1,0:T(2,128)S(1)}, u32[]{:S(2)}, u32[]{:S(2)}) collective-permute-start(f32[2,128]{1,0:T(2,128)S(1)} %get-tuple-element.46), channel_id=1, source_target_pairs={{1,0},{2,1},{3,2},{4,3},{5,4},{6,5},{7,6},{8,7},{9,8},{10,9},{11,1... | collective-permute-start | bytes 3080 | tf_op jit(solution)/shard_map/ppermute | solution.py:16
  124.8 1.5 collective-permute-done.12.low_ref
  126.9 1.9 shard_map.120
  129.6 10.1 %collective-permute-start.15 = (f32[2,128]{1,0:T(2,128)S(1)}, f32[2,128]{1,0:T(2,128)S(1)}, u32[]{:S(2)}, u32[]{:S(2)}) collective-permute-start(f32[2,128]{1,0:T(2,128)S(1)} %get-tuple-element.44), channel_id=1, source_target_pairs={{1,0},{2,1},{3,2},{4,3},{5,4},{6,5},{7,6},{8,7},{9,8},{10,9},{11,1... | collective-permute-start | bytes 3080 | tf_op jit(solution)/shard_map/ppermute | solution.py:16
  139.7 1.5 collective-permute-done.14.low_ref
  141.9 1.9 shard_map.121
  144.5 10.1 %collective-permute-start.17 = (f32[2,128]{1,0:T(2,128)S(1)}, f32[2,128]{1,0:T(2,128)S(1)}, u32[]{:S(2)}, u32[]{:S(2)}) collective-permute-start(f32[2,128]{1,0:T(2,128)S(1)} %get-tuple-element.42), channel_id=1, source_target_pairs={{1,0},{2,1},{3,2},{4,3},{5,4},{6,5},{7,6},{8,7},{9,8},{10,9},{11,1... | collective-permute-start | bytes 3080 | tf_op jit(solution)/shard_map/ppermute | solution.py:16
  154.7 1.5 collective-permute-done.16.low_ref
  156.8 1.9 shard_map.122
  159.5 10.1 %collective-permute-start.19 = (f32[2,128]{1,0:T(2,128)S(1)}, f32[2,128]{1,0:T(2,128)S(1)}, u32[]{:S(2)}, u32[]{:S(2)}) collective-permute-start(f32[2,128]{1,0:T(2,128)S(1)} %get-tuple-element.40), channel_id=1, source_target_pairs={{1,0},{2,1},{3,2},{4,3},{5,4},{6,5},{7,6},{8,7},{9,8},{10,9},{11,1... | collective-permute-start | bytes 3080 | tf_op jit(solution)/shard_map/ppermute | solution.py:16
  169.6 1.5 collective-permute-done.18.low_ref
  171.7 1.9 shard_map.123
  174.5 32.5 %all_to_all.26 = f32[32,2,128]{2,1,0:T(2,128)S(1)} all-to-all(f32[32,2,128]{2,1,0:T(2,128)S(1)} %bitcast.50), channel_id=1, replica_groups=mesh['comp'=8,'cells'=32] {'cells'}, dimensions={0} | all-to-all | bytes 65536 | tf_op jit(solution)/shard_map/all_to_all | solution.py:111
  (100 shorter events, 31.3 us)
Async XLA Ops:
  0.6 33.5 %copy-start.1 = (f32[6,2048]{1,0:T(8,128)S(1)}, f32[6,2048]{1,0:T(8,128)}, u32[]{:S(2)}) copy-start(f32[6,2048]{1,0:T(8,128)} %param.16) | copy-start | bytes 147460
  0.6 32.9 %copy-start.3 = (f32[2048]{0:T(1024)S(1)}, f32[2048]{0:T(1024)}, u32[]{:S(2)}) copy-start(f32[2048]{0:T(1024)} %param.17) | copy-start | bytes 24580
  0.7 34.1 %copy-start.2 = (s32[6,2048]{1,0:T(8,128)S(1)}, s32[6,2048]{1,0:T(8,128)}, u32[]{:S(2)}) copy-start(s32[6,2048]{1,0:T(8,128)} %param.18) | copy-start | bytes 147460
  0.7 43.9 %copy-start.24 = (s32[64]{0:T(128)S(1)}, s32[64]{0:T(128)}, u32[]{:S(2)}) copy-start(s32[64]{0:T(128)} %param.14) | copy-start | bytes 772
  2.3 12.2 %all-to-all-start = ((f32[8,16,128]{2,1,0:T(8,128)}), f32[8,16,128]{2,1,0:T(8,128)S(1)}, u32[]{:S(2)}, u32[]{:S(2)}) async-start(f32[8,16,128]{2,1,0:T(8,128)} %broadcast_in_dim.5), calls=%async_computation | async-start | bytes 131072 | tf_op jit(solution)/shard_map/all_to_all | solution.py:85
  11.6 33.8 %collective-permute-start = (f32[2,128]{1,0:T(2,128)S(1)}, f32[2,128]{1,0:T(2,128)S(1)}, u32[]{:S(2)}, u32[]{:S(2)}) collective-permute-start(f32[2,128]{1,0:T(2,128)S(1)} %get-tuple-element.59), channel_id=1, source_target_pairs={{31,0},{0,1},{1,2},{2,3},{3,4},{4,5},{5,6},{6,7},{7,8},{8,9},{9,10... | collective-permute-start | bytes 3080 | tf_op jit(solution)/shard_map/ppermute | solution.py:16
  13.1 32.3 %collective-permute-start.1 = (f32[2,128]{1,0:T(2,128)S(1)}, f32[2,128]{1,0:T(2,128)S(1)}, u32[]{:S(2)}, u32[]{:S(2)}) collective-permute-start(f32[2,128]{1,0:T(2,128)S(1)} %get-tuple-element.58), channel_id=1, source_target_pairs={{1,0},{2,1},{3,2},{4,3},{5,4},{6,5},{7,6},{8,7},{9,8},{10,9},{11,1... | collective-permute-start | bytes 3080 | tf_op jit(solution)/shard_map/ppermute | solution.py:16
  14.5 192.6 %copy-start = (bf16[64,128,128]{2,1,0:T(8,128)(2,1)S(1)}, bf16[64,128,128]{2,1,0:T(8,128)(2,1)}, u32[]{:S(2)}) copy-start(bf16[64,128,128]{2,1,0:T(8,128)(2,1)} %param.12) | copy-start | bytes 6291460
  18.6 189.6 %copy-start.25 = (s32[64]{0:T(128)S(1)}, s32[64]{0:T(128)}, u32[]{:S(2)}) copy-start(s32[64]{0:T(128)} %param.13) | copy-start | bytes 772
  18.6 25.9 %all-to-all-start.1 = ((f32[32,2,128]{2,1,0:T(2,128)}), f32[32,2,128]{2,1,0:T(2,128)S(1)}, u32[]{:S(2)}, u32[]{:S(2)}) async-start(f32[32,2,128]{2,1,0:T(2,128)} %bitcast.3), calls=%async_computation.1 | async-start | bytes 65536 | tf_op jit(solution)/shard_map/all_to_all | solution.py:91
  45.4 0.6 copy-start.4
  45.4 0.6 copy-start.5
  48.6 3.6 %collective-permute-start.2 = (f32[2,128]{1,0:T(2,128)S(1)}, f32[2,128]{1,0:T(2,128)S(1)}, u32[]{:S(2)}, u32[]{:S(2)}) collective-permute-start(f32[2,128]{1,0:T(2,128)S(1)} %get-tuple-element.57), channel_id=1, source_target_pairs={{31,0},{0,1},{1,2},{2,3},{3,4},{4,5},{5,6},{6,7},{7,8},{8,9},{9,10... | collective-permute-start | bytes 3080 | tf_op jit(solution)/shard_map/ppermute | solution.py:16
  49.3 3.6 %collective-permute-start.3 = (f32[2,128]{1,0:T(2,128)S(1)}, f32[2,128]{1,0:T(2,128)S(1)}, u32[]{:S(2)}, u32[]{:S(2)}) collective-permute-start(f32[2,128]{1,0:T(2,128)S(1)} %get-tuple-element.56), channel_id=1, source_target_pairs={{1,0},{2,1},{3,2},{4,3},{5,4},{6,5},{7,6},{8,7},{9,8},{10,9},{11,1... | collective-permute-start | bytes 3080 | tf_op jit(solution)/shard_map/ppermute | solution.py:16
  52.2 0.6 copy-start.8
  56.1 10.5 %collective-permute-start.4 = (f32[2,128]{1,0:T(2,128)S(1)}, f32[2,128]{1,0:T(2,128)S(1)}, u32[]{:S(2)}, u32[]{:S(2)}) collective-permute-start(f32[2,128]{1,0:T(2,128)S(1)} %get-tuple-element.55), channel_id=1, source_target_pairs={{31,0},{0,1},{1,2},{2,3},{3,4},{4,5},{5,6},{6,7},{7,8},{8,9},{9,10... | collective-permute-start | bytes 3080 | tf_op jit(solution)/shard_map/ppermute | solution.py:16
  57.6 9.0 %collective-permute-start.5 = (f32[2,128]{1,0:T(2,128)S(1)}, f32[2,128]{1,0:T(2,128)S(1)}, u32[]{:S(2)}, u32[]{:S(2)}) collective-permute-start(f32[2,128]{1,0:T(2,128)S(1)} %get-tuple-element.54), channel_id=1, source_target_pairs={{1,0},{2,1},{3,2},{4,3},{5,4},{6,5},{7,6},{8,7},{9,8},{10,9},{11,1... | collective-permute-start | bytes 3080 | tf_op jit(solution)/shard_map/ppermute | solution.py:16
  69.8 11.7 %collective-permute-start.6 = (f32[2,128]{1,0:T(2,128)S(1)}, f32[2,128]{1,0:T(2,128)S(1)}, u32[]{:S(2)}, u32[]{:S(2)}) collective-permute-start(f32[2,128]{1,0:T(2,128)S(1)} %get-tuple-element.53), channel_id=1, source_target_pairs={{31,0},{0,1},{1,2},{2,3},{3,4},{4,5},{5,6},{6,7},{7,8},{8,9},{9,10... | collective-permute-start | bytes 3080 | tf_op jit(solution)/shard_map/ppermute | solution.py:16
  69.8 11.7 %collective-permute-start.7 = (f32[2,128]{1,0:T(2,128)S(1)}, f32[2,128]{1,0:T(2,128)S(1)}, u32[]{:S(2)}, u32[]{:S(2)}) collective-permute-start(f32[2,128]{1,0:T(2,128)S(1)} %get-tuple-element.52), channel_id=1, source_target_pairs={{1,0},{2,1},{3,2},{4,3},{5,4},{6,5},{7,6},{8,7},{9,8},{10,9},{11,1... | collective-permute-start | bytes 3080 | tf_op jit(solution)/shard_map/ppermute | solution.py:16
  84.8 11.7 %collective-permute-start.8 = (f32[2,128]{1,0:T(2,128)S(1)}, f32[2,128]{1,0:T(2,128)S(1)}, u32[]{:S(2)}, u32[]{:S(2)}) collective-permute-start(f32[2,128]{1,0:T(2,128)S(1)} %get-tuple-element.51), channel_id=1, source_target_pairs={{31,0},{0,1},{1,2},{2,3},{3,4},{4,5},{5,6},{6,7},{7,8},{8,9},{9,10... | collective-permute-start | bytes 3080 | tf_op jit(solution)/shard_map/ppermute | solution.py:16
  84.8 11.7 %collective-permute-start.9 = (f32[2,128]{1,0:T(2,128)S(1)}, f32[2,128]{1,0:T(2,128)S(1)}, u32[]{:S(2)}, u32[]{:S(2)}) collective-permute-start(f32[2,128]{1,0:T(2,128)S(1)} %get-tuple-element.50), channel_id=1, source_target_pairs={{1,0},{2,1},{3,2},{4,3},{5,4},{6,5},{7,6},{8,7},{9,8},{10,9},{11,1... | collective-permute-start | bytes 3080 | tf_op jit(solution)/shard_map/ppermute | solution.py:16
  99.7 11.7 %collective-permute-start.10 = (f32[2,128]{1,0:T(2,128)S(1)}, f32[2,128]{1,0:T(2,128)S(1)}, u32[]{:S(2)}, u32[]{:S(2)}) collective-permute-start(f32[2,128]{1,0:T(2,128)S(1)} %get-tuple-element.49), channel_id=1, source_target_pairs={{31,0},{0,1},{1,2},{2,3},{3,4},{4,5},{5,6},{6,7},{7,8},{8,9},{9,10... | collective-permute-start | bytes 3080 | tf_op jit(solution)/shard_map/ppermute | solution.py:16
  99.7 11.7 %collective-permute-start.11 = (f32[2,128]{1,0:T(2,128)S(1)}, f32[2,128]{1,0:T(2,128)S(1)}, u32[]{:S(2)}, u32[]{:S(2)}) collective-permute-start(f32[2,128]{1,0:T(2,128)S(1)} %get-tuple-element.48), channel_id=1, source_target_pairs={{1,0},{2,1},{3,2},{4,3},{5,4},{6,5},{7,6},{8,7},{9,8},{10,9},{11,1... | collective-permute-start | bytes 3080 | tf_op jit(solution)/shard_map/ppermute | solution.py:16
  111.4 0.6 copy-start.20
  114.6 11.7 %collective-permute-start.12 = (f32[2,128]{1,0:T(2,128)S(1)}, f32[2,128]{1,0:T(2,128)S(1)}, u32[]{:S(2)}, u32[]{:S(2)}) collective-permute-start(f32[2,128]{1,0:T(2,128)S(1)} %get-tuple-element.47), channel_id=1, source_target_pairs={{31,0},{0,1},{1,2},{2,3},{3,4},{4,5},{5,6},{6,7},{7,8},{8,9},{9,10... | collective-permute-start | bytes 3080 | tf_op jit(solution)/shard_map/ppermute | solution.py:16
  114.7 11.7 %collective-permute-start.13 = (f32[2,128]{1,0:T(2,128)S(1)}, f32[2,128]{1,0:T(2,128)S(1)}, u32[]{:S(2)}, u32[]{:S(2)}) collective-permute-start(f32[2,128]{1,0:T(2,128)S(1)} %get-tuple-element.46), channel_id=1, source_target_pairs={{1,0},{2,1},{3,2},{4,3},{5,4},{6,5},{7,6},{8,7},{9,8},{10,9},{11,1... | collective-permute-start | bytes 3080 | tf_op jit(solution)/shard_map/ppermute | solution.py:16
  129.6 11.7 %collective-permute-start.14 = (f32[2,128]{1,0:T(2,128)S(1)}, f32[2,128]{1,0:T(2,128)S(1)}, u32[]{:S(2)}, u32[]{:S(2)}) collective-permute-start(f32[2,128]{1,0:T(2,128)S(1)} %get-tuple-element.45), channel_id=1, source_target_pairs={{31,0},{0,1},{1,2},{2,3},{3,4},{4,5},{5,6},{6,7},{7,8},{8,9},{9,10... | collective-permute-start | bytes 3080 | tf_op jit(solution)/shard_map/ppermute | solution.py:16
  129.6 11.7 %collective-permute-start.15 = (f32[2,128]{1,0:T(2,128)S(1)}, f32[2,128]{1,0:T(2,128)S(1)}, u32[]{:S(2)}, u32[]{:S(2)}) collective-permute-start(f32[2,128]{1,0:T(2,128)S(1)} %get-tuple-element.44), channel_id=1, source_target_pairs={{1,0},{2,1},{3,2},{4,3},{5,4},{6,5},{7,6},{8,7},{9,8},{10,9},{11,1... | collective-permute-start | bytes 3080 | tf_op jit(solution)/shard_map/ppermute | solution.py:16
  144.5 11.7 %collective-permute-start.16 = (f32[2,128]{1,0:T(2,128)S(1)}, f32[2,128]{1,0:T(2,128)S(1)}, u32[]{:S(2)}, u32[]{:S(2)}) collective-permute-start(f32[2,128]{1,0:T(2,128)S(1)} %get-tuple-element.43), channel_id=1, source_target_pairs={{31,0},{0,1},{1,2},{2,3},{3,4},{4,5},{5,6},{6,7},{7,8},{8,9},{9,10... | collective-permute-start | bytes 3080 | tf_op jit(solution)/shard_map/ppermute | solution.py:16
  144.5 11.7 %collective-permute-start.17 = (f32[2,128]{1,0:T(2,128)S(1)}, f32[2,128]{1,0:T(2,128)S(1)}, u32[]{:S(2)}, u32[]{:S(2)}) collective-permute-start(f32[2,128]{1,0:T(2,128)S(1)} %get-tuple-element.42), channel_id=1, source_target_pairs={{1,0},{2,1},{3,2},{4,3},{5,4},{6,5},{7,6},{8,7},{9,8},{10,9},{11,1... | collective-permute-start | bytes 3080 | tf_op jit(solution)/shard_map/ppermute | solution.py:16
  159.5 11.7 %collective-permute-start.18 = (f32[2,128]{1,0:T(2,128)S(1)}, f32[2,128]{1,0:T(2,128)S(1)}, u32[]{:S(2)}, u32[]{:S(2)}) collective-permute-start(f32[2,128]{1,0:T(2,128)S(1)} %get-tuple-element.41), channel_id=1, source_target_pairs={{31,0},{0,1},{1,2},{2,3},{3,4},{4,5},{5,6},{6,7},{7,8},{8,9},{9,10... | collective-permute-start | bytes 3080 | tf_op jit(solution)/shard_map/ppermute | solution.py:16
  159.5 11.7 %collective-permute-start.19 = (f32[2,128]{1,0:T(2,128)S(1)}, f32[2,128]{1,0:T(2,128)S(1)}, u32[]{:S(2)}, u32[]{:S(2)}) collective-permute-start(f32[2,128]{1,0:T(2,128)S(1)} %get-tuple-element.40), channel_id=1, source_target_pairs={{1,0},{2,1},{3,2},{4,3},{5,4},{6,5},{7,6},{8,7},{9,8},{10,9},{11,1... | collective-permute-start | bytes 3080 | tf_op jit(solution)/shard_map/ppermute | solution.py:16
  (16 other events, 9.1 us)

commit v2 on v1

v2 whole, which is shorter than its diff:
```python
import functools

import jax
import jax.numpy as jnp
from jax import lax
from jax.experimental import pallas as pl
from jax.experimental.pallas import tpu as pltpu
from jax.sharding import PartitionSpec as P

LANES = 128
OWNERS = 32
HALF = 16
BLOCKS = 16
REACH = 4
STEPS = 5
WINDOW = 2 * REACH + 1
PART = 232
CONDUCT, KEEP, START, LISTS, TARGET = 96, 192, 208, 224, 228
TABLE = 24
SENT = 24
BOTH = ("comp", "cells")
HIGHEST = lax.Precision.HIGHEST
F32 = jnp.float32


def device_of(owner, copy, core):
    z_low = copy if owner < HALF else (copy + 2) % 4
    return (2 * z_low + core) * OWNERS + owner


COPIES = [(copy, core) for copy in range(4) for core in range(2)]
GROUPS = [[device_of(owner, *copy) for owner in range(OWNERS)] for copy in COPIES]


def from_owner(block, offset):
    route = [
        (device_of((owner + offset) % OWNERS, *copy), device_of(owner, *copy))
        for copy in COPIES
        for owner in range(OWNERS)
    ]
    return lax.ppermute(block, BOTH, route)


def between_owners(blocks):
    return lax.all_to_all(
        blocks, BOTH, split_axis=0, concat_axis=0, tiled=True, axis_index_groups=GROUPS
    )


def lane_pick(rows, lane):
    dims = lax.GatherDimensionNumbers(
        offset_dims=(),
        collapsed_slice_dims=(1,),
        start_index_map=(1,),
        operand_batching_dims=(0,),
        start_indices_batching_dims=(0,),
    )
    return lax.gather(
        rows,
        lane[..., None],
        dims,
        slice_sizes=(1, 1),
        mode=lax.GatherScatterMode.PROMISE_IN_BOUNDS,
    )


def table_pick(table_ref, count, index):
    row, lane = index >> 7, index & 127
    total = None
    for r in range(count):
        line = table_ref[pl.ds(r, index.shape[0], stride=0), :]
        near = lane_pick(line, lane)
        total = near if total is None else jnp.where(row == r, near, total)
    return total


def terms_kernel(shares_ref, source_ref, weight_ref, out_ref, parts_ref, terms_ref):
    flux = jnp.sum(shares_ref[...], axis=0)
    tiles = lax.broadcasted_iota(jnp.int32, (64, BLOCKS), 1)
    hot = (source_ref[...] == tiles).astype(F32)
    picked = jnp.dot(hot, flux, precision=HIGHEST, preferred_element_type=F32)
    high = picked.astype(jnp.bfloat16).astype(F32)
    rest = picked - high
    middle = rest.astype(jnp.bfloat16).astype(F32)
    parts_ref[...] = jnp.zeros_like(parts_ref)
    parts_ref[:, 0, :] = high
    parts_ref[:, 1, :] = middle
    parts_ref[:, 2, :] = rest - middle
    for t in range(64):
        left = parts_ref[t].astype(jnp.bfloat16)
        three = jnp.dot(left, weight_ref[t], preferred_element_type=F32)
        term = jnp.sum(three, axis=0, keepdims=True)
        place = (t + 2 * REACH) % 64
        while place < 64 + SENT:
            terms_ref[place : place + 1] = term
            place += 64
    for p in range(OWNERS):
        out_ref[p] = terms_ref[2 * p : 2 * p + SENT]


def send(table_ref, slot, lists_ref):
    index = lists_ref[pl.ds(pl.multiple_of((slot - 1) * 8, 8), 8), :].astype(jnp.int32)
    values = table_pick(table_ref.at[slot], 16, index)
    table_ref[slot - 1, 18:20] = values[0:2]
    table_ref[slot + 1, 16:18] = values[2:4]


def run_steps(tables, part_ref, lists_ref, forcing_ref):
    def first(slot, carry):
        send(tables[0], slot, lists_ref)
        return carry

    lax.fori_loop(1, WINDOW + 3, first, 0)
    for step in range(STEPS):
        left = STEPS - 1 - step
        old, new = tables[step % 2], tables[(step + 1) % 2]

        def advance(slot, carry, old=old, new=new, left=left):
            base = pl.multiple_of((slot - 2) * PART, 8)
            force = pl.multiple_of((slot - 2) * 16, 8)
            for h in range(2):
                own = old[slot, 8 * h : 8 * h + 8]
                total = part_ref[pl.ds(base + KEEP + 8 * h, 8), :] * own + forcing_ref[pl.ds(force + 8 * h, 8), :]
                for m in range(6):
                    index = part_ref[pl.ds(base + 16 * m + 8 * h, 8), :].astype(jnp.int32)
                    near = table_pick(old.at[slot], 20, index)
                    total = total + part_ref[pl.ds(base + CONDUCT + 16 * m + 8 * h, 8), :] * near
                new[slot, 8 * h : 8 * h + 8] = total
            if left:
                send(new, slot, lists_ref)
            return carry

        lax.fori_loop(REACH + 2 - left, REACH + 3 + left, advance, 0)
    return tables[STEPS % 2][REACH + 2, 0:16]


def first_kernel(arrived_ref, key_ref, part_ref, lists_ref, start_ref, forcing_ref, out_ref, table0, table1):
    owners = lax.broadcasted_iota(jnp.int32, (16 * WINDOW, OWNERS * SENT), 0)
    hot = (owners == key_ref[...]).astype(F32)
    terms = arrived_ref[...].reshape(OWNERS * SENT, LANES)
    forcing_ref[...] = jnp.dot(hot, terms, precision=HIGHEST, preferred_element_type=F32)
    for slot in range(1, WINDOW + 3):
        table0[slot, 0:16] = start_ref[16 * (slot - 1) : 16 * slot]
    surface = run_steps((table0, table1), part_ref, lists_ref, forcing_ref)
    out_ref[...] = jnp.broadcast_to(surface[None], out_ref.shape)


def last_kernel(owner_ref, surfaces_ref, target_ref, part_ref, lists_ref, forcing_ref, out_ref, values_ref, table0, table1):
    for slot in range(1, WINDOW + 3):
        owner = (owner_ref[0] + (slot - REACH - 2 + OWNERS)) % OWNERS
        table0[slot, 0:16] = surfaces_ref[owner]
    surface = run_steps((table0, table1), part_ref, lists_ref, forcing_ref)
    out_ref[...] = surface
    blocks = lax.broadcasted_iota(jnp.int32, (64, BLOCKS), 1)
    hot = (target_ref[...] == blocks).astype(F32)
    values_ref[...] = jnp.dot(hot, surface, precision=HIGHEST, preferred_element_type=F32)


def shape(*dims):
    return jax.ShapeDtypeStruct(dims, F32)


def local(
    atm_flux,
    level_weight,
    tile_weight,
    tile_source,
    tile_target,
    ocean_start,
    conductance,
    damping,
    neighbors,
    send_lists,
):
    tables = [pltpu.VMEM((WINDOW + 4, TABLE, LANES), F32)] * 2

    keep = 1.0 - jnp.sum(conductance, axis=0) - damping
    target_row = jnp.pad(tile_target.astype(F32), (0, 64)).reshape(1, LANES)
    packed = jnp.concatenate(
        [
            neighbors.astype(F32).reshape(96, LANES),
            conductance.reshape(96, LANES),
            keep.reshape(16, LANES),
            ocean_start.reshape(16, LANES),
            send_lists.astype(F32).reshape(4, LANES),
            target_row,
            jnp.zeros((3, LANES), F32),
        ],
        axis=0,
    )
    three = jnp.concatenate([from_owner(packed, -1), packed, from_owner(packed, 1)], axis=0)
    outer = packed[START : START + 24]
    below, above = from_owner(outer, -STEPS), from_owner(outer, STEPS)
    parts = jnp.concatenate([from_owner(three, -3), three, from_owner(three, 3)], axis=0)
    by_owner = parts.reshape(WINDOW, PART, LANES)
    starts = jnp.concatenate([below[:16], by_owner[:, START:LISTS].reshape(-1, LANES), above[:16]], axis=0)
    lists = jnp.concatenate([below[16:24], by_owner[:, LISTS:PART].reshape(-1, LANES), above[16:24]], axis=0)
    targets = by_owner[:, TARGET, :64].astype(jnp.int32) + 16 * jnp.arange(WINDOW, dtype=jnp.int32)[:, None]
    key = jnp.pad(
        targets.reshape(WINDOW, OWNERS, 2).transpose(1, 0, 2).reshape(OWNERS, 2 * WINDOW),
        ((0, 0), (0, SENT - 2 * WINDOW)),
        constant_values=-1,
    ).reshape(1, OWNERS * SENT)

    partial = jnp.sum(level_weight[:, None] * atm_flux.astype(F32), axis=0).reshape(BLOCKS, LANES)
    shares = lax.all_to_all(
        jnp.broadcast_to(partial[None], (8, BLOCKS, LANES)), "comp", split_axis=0, concat_axis=0, tiled=True
    )
    terms = pl.pallas_call(
        terms_kernel,
        out_shape=shape(OWNERS, SENT, LANES),
        scratch_shapes=[pltpu.VMEM((64, 8, LANES), F32), pltpu.VMEM((64 + SENT, LANES), F32)],
    )(shares, tile_source[:, None], tile_weight)
    arrived = between_owners(terms)

    forcing, surface = pl.pallas_call(
        first_kernel,
        out_shape=(shape(16 * WINDOW, LANES), shape(OWNERS, 16, LANES)),
        scratch_shapes=tables,
    )(arrived, key, parts, lists, starts)
    surfaces = between_owners(surface)
    owner = lax.axis_index("cells").astype(jnp.int32).reshape(1)
    vmem = pl.BlockSpec(memory_space=pltpu.VMEM)
    ocean_end, values = pl.pallas_call(
        last_kernel,
        out_shape=(shape(16, LANES), shape(64, LANES)),
        in_specs=[pl.BlockSpec(memory_space=pltpu.SMEM)] + [vmem] * 5,
        scratch_shapes=tables,
    )(owner, surfaces, tile_target[:, None], parts, lists, forcing)

    returned = between_owners(values.reshape(OWNERS, 2, LANES)).reshape(64, LANES)
    pulled = jnp.sum(returned[:, None, :] * tile_weight.astype(F32), axis=2)
    source_hot = (tile_source[:, None] == jnp.arange(BLOCKS, dtype=jnp.int32)[None, :]).astype(F32)
    atm_back = jnp.einsum("ra,rb->ab", source_hot, pulled, precision=HIGHEST).reshape(-1)
    return (ocean_end.reshape(-1), atm_back)


def solution(mesh):
    in_specs = (
        P("comp", "cells"),
        P("comp"),
        P("cells", None, None),
        P("cells"),
        P("cells"),
        P("cells"),
        P(None, "cells"),
        P("cells"),
        P(None, "cells"),
        P(None, "cells"),
    )
    out_specs = (P("cells"), P("cells"))
    return jax.shard_map(local, mesh=mesh, in_specs=in_specs, out_specs=out_specs, check_vma=False)
```

time: 211 us -> 137 us (0.65)
  starting transfers between devices: 105 us -> 48.9 us
  blocking collectives: 32.5 us -> 16.6 us
  Pallas kernels: 20.4 us -> 32.4 us
  local copies, waits for them, and re-layouts: 16.5 us -> 8.42 us
  waiting for transfers between devices: 23.7 us -> 20.6 us
  matrix products: 3.64 us -> 0.87 us
    ppermute x20 -> x6, starting transfers between devices: 84.1 us -> 22.3 us  [from_owner(): return lax.ppermute(block, BOTH, route)]
    all_to_all x1, blocking collectives: 32.5 us -> 16.6 us  [between_owners(): lax.all_to_all(blocks, BOTH, split_axis=0, concat_axis=0, tiled=True, axi...]
    pallas_call x11 -> x3, Pallas kernels: 20.4 us -> 32.4 us  [the longest x1 14.7 us: local(): pl.pallas_call(first_kernel, out_shape=(shape(16 * WINDOW, LANES), shape(...]
    ppermute x20 -> x6, waiting for transfers between devices: 14.6 us -> 4 us  [from_owner(): return lax.ppermute(block, BOTH, route)]
    slice x10 -> x6, local copies, waits for them, and re-layouts: 7.53 us -> 0.02 us  [the longest x1 0.01 us: local(): by_owner[:, START:LISTS].reshape(-1, LANES)]
    all_to_all x2 -> x3, waiting for transfers between devices: 9.11 us -> 16.6 us  [the longest x2 16.6 us: between_owners(): lax.all_to_all(blocks, BOTH, split_axis=0, concat_axis=0, tiled=True, axi...]
    all_to_all x2 -> x3, starting transfers between devices: 20.8 us -> 26.6 us  [the longest x2 23 us: between_owners(): lax.all_to_all(blocks, BOTH, split_axis=0, concat_axis=0, tiled=True, axi...]
    unnamed x54 -> x16, local copies, waits for them, and re-layouts: 7.06 us -> 1.55 us
  transfers between devices with their start and end apart: 22 -> 9, of which waited for: 11 -> 4; matrix products, arithmetic and copies ran while one was open for 5% -> 6% of each run, Pallas kernels for 1% -> 2%
where the time goes in v2:
time: 137 us; the launch traced here: 136 us
  starting transfers between devices  48.9 us (36%)
  Pallas kernels  32.4 us (24%)
  waiting for transfers between devices  20.6 us (15%)
  blocking collectives  16.6 us (12%)
  local copies, waits for them, and re-layouts  8.42 us (6%)
  other arithmetic  7.87 us (6%)
    all_to_all x2, starting transfers between devices, between_owners(): lax.all_to_all(blocks, BOTH, split_axis=0, concat_axis=0, tiled=True, axi...  23 us
    ppermute x6, starting transfers between devices, from_owner(): return lax.ppermute(block, BOTH, route)  22.3 us
    all_to_all x1, blocking collectives, between_owners(): lax.all_to_all(blocks, BOTH, split_axis=0, concat_axis=0, tiled=True, axi...  16.6 us
    all_to_all x2, waiting for transfers between devices, between_owners(): lax.all_to_all(blocks, BOTH, split_axis=0, concat_axis=0, tiled=True, axi...  16.6 us
    pallas_call x1, Pallas kernels, local(): pl.pallas_call(first_kernel, out_shape=(shape(16 * WINDOW, LANES), shape(...  14.7 us
    pallas_call x1, Pallas kernels, local(): pl.pallas_call(last_kernel, out_shape=(shape(16, LANES), shape(64, LANES)...  14.3 us
    ppermute x6, waiting for transfers between devices, from_owner(): return lax.ppermute(block, BOTH, route)  4 us
    all_to_all x1, starting transfers between devices, local(): lax.all_to_all(jnp.broadcast_to(partial[None], (8, BLOCKS, LANES)), 'comp...  3.57 us
  transfers between devices with their start and end apart: 9, of which 4 were waited for; matrix products, arithmetic and copies ran while one was open for 6% of the time, Pallas kernels for 2%

profile of v2, /device:TPU:2, one launch (start us, length us, event | category | flops | bytes accessed | tf_op | source)
XLA Modules:
  0.0 136.5 jit_solution(10194282663275978902)
XLA Ops:
  0.6 0.7 convert_element_type.27
  2.0 0.8 convert_element_type.26
  2.9 0.9 reshape.68
  3.7 0.9 reduce_sum.28
  4.6 0.7 subtract_bitcast_fusion
  5.3 0.7 concatenate.20
  6.0 1.6 %collective-permute-start = (f32[232,128]{1,0:T(8,128)S(1)}, f32[232,128]{1,0:T(8,128)S(1)}, u32[]{:S(2)}, u32[]{:S(2)}) collective-permute-start(f32[232,128]{1,0:T(8,128)S(1)} %concatenate.20), channel_id=1, source_target_pairs={{159,0},{0,1},{1,2},{2,3},{3,4},{4,5},{5,6},{6,7},{7,8},{8,9},{9,1... | collective-permute-start | bytes 356360 | tf_op jit(solution)/shard_map/ppermute | solution.py:41
  7.6 0.8 collective-permute-start.1
  8.4 2.7 %collective-permute-done = f32[232,128]{1,0:T(8,128)S(1)} collective-permute-done((f32[232,128]{1,0:T(8,128)S(1)}, f32[232,128]{1,0:T(8,128)S(1)}, u32[]{:S(2)}, u32[]{:S(2)}) %collective-permute-start) | collective-permute-done | bytes 118816 | tf_op jit(solution)/shard_map/ppermute | solution.py:41
  11.2 1.3 collective-permute-done.1
  12.4 0.7 concatenate.21
  13.2 2.4 %collective-permute-start.2 = (f32[696,128]{1,0:T(8,128)S(1)}, f32[696,128]{1,0:T(8,128)S(1)}, u32[]{:S(2)}, u32[]{:S(2)}) collective-permute-start(f32[696,128]{1,0:T(8,128)S(1)} %concatenate.21), channel_id=1, source_target_pairs={{157,0},{158,1},{159,2},{0,3},{1,4},{2,5},{3,6},{4,7},{5,8},{6,9},... | collective-permute-start | bytes 1069064 | tf_op jit(solution)/shard_map/ppermute | solution.py:41
  15.5 7.2 %collective-permute-start.3 = (f32[696,128]{1,0:T(8,128)S(1)}, f32[696,128]{1,0:T(8,128)S(1)}, u32[]{:S(2)}, u32[]{:S(2)}) collective-permute-start(f32[696,128]{1,0:T(8,128)S(1)} %concatenate.21), channel_id=1, source_target_pairs={{3,0},{4,1},{5,2},{6,3},{7,4},{8,5},{9,6},{10,7},{11,8},{12,9},{13... | collective-permute-start | bytes 1069064 | tf_op jit(solution)/shard_map/ppermute | solution.py:41
  22.7 0.9 multiply_reduce_fusion.1
  24.3 3.6 %all-to-all-start = ((f32[8,16,128]{2,1,0:T(8,128)}), f32[8,16,128]{2,1,0:T(8,128)S(1)}, u32[]{:S(2)}, u32[]{:S(2)}) async-start(f32[8,16,128]{2,1,0:T(8,128)} %broadcast_in_dim.21), calls=%async_computation | async-start | bytes 131072 | tf_op jit(solution)/shard_map/all_to_all | solution.py:206
  27.9 0.7 pad_maximum_fusion.2
  28.6 10.3 %collective-permute-start.5 = (f32[24,128]{1,0:T(8,128)S(1)}, f32[24,128]{1,0:T(8,128)S(1)}, u32[]{:S(2)}, u32[]{:S(2)}) collective-permute-start(f32[24,128]{1,0:T(8,128)S(1)} %pad_maximum_fusion.2), channel_id=1, source_target_pairs={{5,0},{6,1},{7,2},{8,3},{9,4},{10,5},{11,6},{12,7},{13,8},{14,9},{... | collective-permute-start | bytes 36872 | tf_op jit(solution)/shard_map/ppermute | solution.py:41
  38.9 1.3 copy.15.source_ref
  40.9 3.4 %shard_map.113 = f32[32,24,128]{2,1,0:T(8,128)} custom-call(f32[8,16,128]{2,1,0:T(8,128)} %copy-done.3, s32[64,1]{1,0:T(8,128)} %copy.15.source_ref, bf16[64,128,128]{2,1,0:T(8,128)(2,1)} %weight_ref.1), custom_call_target="tpu_custom_call" | custom-call | tf_op jit(solution)/shard_map/pallas_call | solution.py:209
  44.3 13.5 %all-to-all-start.1 = ((f32[32,24,128]{2,1,0:T(8,128)}), f32[32,24,128]{2,1,0:T(8,128)}, u32[]{:S(2)}, u32[]{:S(2)}) async-start(f32[32,24,128]{2,1,0:T(8,128)} %shard_map.113), calls=%async_computation.1 | async-start | bytes 786432 | tf_op jit(solution)/shard_map/all_to_all | solution.py:45
  57.9 1.0 concatenate.22.part_ref
  59.3 0.7 reshape.75.key_ref
  61.2 7.5 %all-to-all-done.1.arrived_ref = f32[32,24,128]{2,1,0:T(8,128)} async-done(((f32[32,24,128]{2,1,0:T(8,128)}), f32[32,24,128]{2,1,0:T(8,128)}, u32[]{:S(2)}, u32[]{:S(2)}) %all-to-all-start.1) | async-done | bytes 393248 | tf_op jit(solution)/shard_map/all_to_all | solution.py:45
  68.7 14.7 %shard_map.114 = (f32[144,128]{1,0:T(8,128)}, f32[32,16,128]{2,1,0:T(8,128)}) custom-call(f32[32,24,128]{2,1,0:T(8,128)} %all-to-all-done.1.arrived_ref, s32[1,768]{1,0:T(1,128)} %reshape.75.key_ref, f32[2088,128]{1,0:T(8,128)} %copy-done, f32[88,128]{1,0:T(8,128)} %pad_maximum_fusion.1.lists_ref, f32[176,128]{1,0:T(8,128)} %pad_maximum_fusion.start_ref), custom_call_target="tpu_custom_call" | custom-call | tf_op jit(solution)/shard_map/pallas_call | solution.py:216
  83.4 9.5 %all-to-all-start.2 = ((f32[32,16,128]{2,1,0:T(8,128)}), f32[32,16,128]{2,1,0:T(8,128)S(1)}, u32[]{:S(2)}, u32[]{:S(2)}) async-start(f32[32,16,128]{2,1,0:T(8,128)} %get-tuple-element.6), calls=%async_computation.2 | async-start | bytes 524288 | tf_op jit(solution)/shard_map/all_to_all | solution.py:45
  93.0 0.7 copy.19.target_ref
  93.7 9.1 %all-to-all-done.2.surfaces_ref = f32[32,16,128]{2,1,0:T(8,128)S(1)} async-done(((f32[32,16,128]{2,1,0:T(8,128)}), f32[32,16,128]{2,1,0:T(8,128)S(1)}, u32[]{:S(2)}, u32[]{:S(2)}) %all-to-all-start.2) | async-done | bytes 262176 | tf_op jit(solution)/shard_map/all_to_all | solution.py:45
  102.8 0.7 copy-done.2
  103.5 14.3 %shard_map.115 = (f32[16,128]{1,0:T(8,128)}, f32[64,128]{1,0:T(8,128)}) custom-call(s32[1]{0:T(128)} %bitcast.owner_ref, f32[32,16,128]{2,1,0:T(8,128)} %copy-done.2, s32[64,1]{1,0:T(8,128)} %copy.19.target_ref, f32[2088,128]{1,0:T(8,128)} %copy-done, f32[88,128]{1,0:T(8,128)} %pad_maximum_fusion.1.lists_ref, f32[144,128]{1,0:T(8,128)} %get-tuple-element.7.forcing_ref), custom_call_target="tpu_custom_call" | custom-call | tf_op jit(solution)/shard_map/pallas_call | solution.py:224
  117.8 16.6 %all_to_all.20 = f32[32,2,128]{2,1,0:T(2,128)S(1)} all-to-all(f32[32,2,128]{2,1,0:T(2,128)} %bitcast.35), channel_id=1, replica_groups={{0,1,2,3,4,5,6,7,8,9,10,11,12,13,14,15,144,145,146,147,148,149,150,151,..., dimensions={0} | all-to-all | bytes 65536 | tf_op jit(solution)/shard_map/all_to_all | solution.py:45
  134.4 1.2 multiply_reduce_fusion
  135.6 0.9 convolution_bitcast_fusion
  (42 shorter events, 3.6 us)
Async XLA Ops:
  6.0 51.9 %copy-start.4 = (f32[2048]{0:T(1024)S(1)}, f32[2048]{0:T(1024)}, u32[]{:S(2)}) copy-start(f32[2048]{0:T(1024)} %param.15) | copy-start | bytes 24580
  6.0 5.1 %collective-permute-start = (f32[232,128]{1,0:T(8,128)S(1)}, f32[232,128]{1,0:T(8,128)S(1)}, u32[]{:S(2)}, u32[]{:S(2)}) collective-permute-start(f32[232,128]{1,0:T(8,128)S(1)} %concatenate.20), channel_id=1, source_target_pairs={{159,0},{0,1},{1,2},{2,3},{3,4},{4,5},{5,6},{6,7},{7,8},{8,9},{9,1... | collective-permute-start | bytes 356360 | tf_op jit(solution)/shard_map/ppermute | solution.py:41
  7.6 4.8 %collective-permute-start.1 = (f32[232,128]{1,0:T(8,128)S(1)}, f32[232,128]{1,0:T(8,128)S(1)}, u32[]{:S(2)}, u32[]{:S(2)}) collective-permute-start(f32[232,128]{1,0:T(8,128)S(1)} %concatenate.20), channel_id=1, source_target_pairs={{1,0},{2,1},{3,2},{4,3},{5,4},{6,5},{7,6},{8,7},{9,8},{10,9},{11,1... | collective-permute-start | bytes 356360 | tf_op jit(solution)/shard_map/ppermute | solution.py:41
  13.2 44.7 %collective-permute-start.2 = (f32[696,128]{1,0:T(8,128)S(1)}, f32[696,128]{1,0:T(8,128)S(1)}, u32[]{:S(2)}, u32[]{:S(2)}) collective-permute-start(f32[696,128]{1,0:T(8,128)S(1)} %concatenate.21), channel_id=1, source_target_pairs={{157,0},{158,1},{159,2},{0,3},{1,4},{2,5},{3,6},{4,7},{5,8},{6,9},... | collective-permute-start | bytes 1069064 | tf_op jit(solution)/shard_map/ppermute | solution.py:41
  15.5 42.3 %collective-permute-start.3 = (f32[696,128]{1,0:T(8,128)S(1)}, f32[696,128]{1,0:T(8,128)S(1)}, u32[]{:S(2)}, u32[]{:S(2)}) collective-permute-start(f32[696,128]{1,0:T(8,128)S(1)} %concatenate.21), channel_id=1, source_target_pairs={{3,0},{4,1},{5,2},{6,3},{7,4},{8,5},{9,6},{10,7},{11,8},{12,9},{13... | collective-permute-start | bytes 1069064 | tf_op jit(solution)/shard_map/ppermute | solution.py:41
  24.3 16.0 %all-to-all-start = ((f32[8,16,128]{2,1,0:T(8,128)}), f32[8,16,128]{2,1,0:T(8,128)S(1)}, u32[]{:S(2)}, u32[]{:S(2)}) async-start(f32[8,16,128]{2,1,0:T(8,128)} %broadcast_in_dim.21), calls=%async_computation | async-start | bytes 131072 | tf_op jit(solution)/shard_map/all_to_all | solution.py:206
  28.6 29.2 %collective-permute-start.4 = (f32[24,128]{1,0:T(8,128)S(1)}, f32[24,128]{1,0:T(8,128)S(1)}, u32[]{:S(2)}, u32[]{:S(2)}) collective-permute-start(f32[24,128]{1,0:T(8,128)S(1)} %pad_maximum_fusion.2), channel_id=1, source_target_pairs={{155,0},{156,1},{157,2},{158,3},{159,4},{0,5},{1,6},{2,7},{3,8},{4... | collective-permute-start | bytes 36872 | tf_op jit(solution)/shard_map/ppermute | solution.py:41
  28.6 29.2 %collective-permute-start.5 = (f32[24,128]{1,0:T(8,128)S(1)}, f32[24,128]{1,0:T(8,128)S(1)}, u32[]{:S(2)}, u32[]{:S(2)}) collective-permute-start(f32[24,128]{1,0:T(8,128)S(1)} %pad_maximum_fusion.2), channel_id=1, source_target_pairs={{5,0},{6,1},{7,2},{8,3},{9,4},{10,5},{11,6},{12,7},{13,8},{14,9},{... | collective-permute-start | bytes 36872 | tf_op jit(solution)/shard_map/ppermute | solution.py:41
  40.2 0.6 copy-start.3
  44.3 24.4 %all-to-all-start.1 = ((f32[32,24,128]{2,1,0:T(8,128)}), f32[32,24,128]{2,1,0:T(8,128)}, u32[]{:S(2)}, u32[]{:S(2)}) async-start(f32[32,24,128]{2,1,0:T(8,128)} %shard_map.113), calls=%async_computation.1 | async-start | bytes 786432 | tf_op jit(solution)/shard_map/all_to_all | solution.py:45
  57.8 35.2 %copy-start.5 = (s32[64]{0:T(128)S(1)}, s32[64]{0:T(128)}, u32[]{:S(2)}) copy-start(s32[64]{0:T(128)} %param.14) | copy-start | bytes 772
  58.9 9.8 %copy-start = (f32[2088,128]{1,0:T(8,128)}, f32[2088,128]{1,0:T(8,128)S(1)}, u32[]{:S(2)}) copy-start(f32[2088,128]{1,0:T(8,128)S(1)} %concatenate.22.part_ref) | copy-start | bytes 3207172
  59.2 75.3 %copy-start.1 = (bf16[64,128,128]{2,1,0:T(8,128)(2,1)S(1)}, bf16[64,128,128]{2,1,0:T(8,128)(2,1)}, u32[]{:S(2)}) copy-start(bf16[64,128,128]{2,1,0:T(8,128)(2,1)} %weight_ref.1) | copy-start | bytes 6291460
  83.4 52.2 %copy-start.6 = (s32[64]{0:T(128)S(1)}, s32[64]{0:T(128)}, u32[]{:S(2)}) copy-start(s32[64]{0:T(128)} %param.13) | copy-start | bytes 772
  83.4 19.4 %all-to-all-start.2 = ((f32[32,16,128]{2,1,0:T(8,128)}), f32[32,16,128]{2,1,0:T(8,128)S(1)}, u32[]{:S(2)}, u32[]{:S(2)}) async-start(f32[32,16,128]{2,1,0:T(8,128)} %get-tuple-element.6), calls=%async_computation.2 | async-start | bytes 524288 | tf_op jit(solution)/shard_map/all_to_all | solution.py:45
  102.8 0.7 copy-start.2

commit v3 on v1

v3 whole, which is shorter than its diff:
```python
import jax
import jax.numpy as jnp
from jax import lax
from jax.experimental import pallas as pl
from jax.experimental.pallas import tpu as pltpu
from jax.sharding import PartitionSpec as P

LANES = 128
OWNERS = 32
HALF = 16
TILES = 64
REACH = 4
STEPS = 5
WINDOW = 2 * REACH + 1
CENTER = REACH + 2
SLOTS = WINDOW + 4
PART = 232
CONDUCT, KEEP, START, LISTS, TARGET = 96, 192, 208, 224, 228
SENT = 40
TERMS = 22
BOTH = ("comp", "cells")
HIGHEST = lax.Precision.HIGHEST
F32, I32 = jnp.float32, jnp.int32
VMEM = pl.BlockSpec(memory_space=pltpu.VMEM)
SMEM = pl.BlockSpec(memory_space=pltpu.SMEM)


def device_of(owner, copy, core):
    z_low = copy if owner < HALF else 3 - copy
    return (2 * z_low + core) * OWNERS + owner


COPIES = [(copy, core) for copy in range(4) for core in range(2)]
ALL = [[device_of(owner, *copy) for owner in range(OWNERS)] for copy in COPIES]


def eights(first):
    return [
        [device_of((8 * g + first + i) % OWNERS, *copy) for i in range(8)] for copy in COPIES for g in range(4)
    ]


def exchange(blocks, groups):
    return lax.all_to_all(blocks, BOTH, split_axis=0, concat_axis=0, tiled=True, axis_index_groups=groups)


def lane_pick(rows, lane):
    dims = lax.GatherDimensionNumbers(
        offset_dims=(),
        collapsed_slice_dims=(1,),
        start_index_map=(1,),
        operand_batching_dims=(0,),
        start_indices_batching_dims=(0,),
    )
    return lax.gather(
        rows,
        lane[..., None],
        dims,
        slice_sizes=(1, 1),
        mode=lax.GatherScatterMode.PROMISE_IN_BOUNDS,
    )


def coded(index):
    row, lane = index >> 7, index & 127
    halo = row >= 16
    pair = jnp.where(halo, 8 + ((row >> 1) & 1), row & 7)
    half = jnp.where(halo, row & 1, row >> 3)
    return pair * 256 + half * 128 + lane


def pair_of(upper, lower):
    return (upper << 16) | (lower & 0xFFFF)


def pick(table_ref, count, code):
    lane, pair = code & 127, code >> 8
    total = None
    for r in range(count):
        line = table_ref[pl.ds(r, 8, stride=0), :]
        near = lane_pick(line, lane)
        total = near if total is None else jnp.where(pair == r, near, total)
    return jnp.where((code & 128) == 0, total, total << 16) >> 16


def prepare_kernel(weight_ref, flux_ref, neighbor_ref, conduct_ref, damping_ref, start_ref, lists_ref, target_ref, shares_ref, packed_ref, row_ref):
    for j in range(16):
        lanes = slice(LANES * j, LANES * j + LANES)
        block = flux_ref[:, lanes].astype(F32)
        row_ref[j : j + 1] = sum(weight_ref[level] * block[level : level + 1] for level in range(block.shape[0]))
    shares_ref[...] = jnp.broadcast_to(row_ref[...][None], shares_ref.shape)
    own = packed_ref.at[0]
    for j in range(16):
        lanes = slice(LANES * j, LANES * j + LANES)
        own[pl.ds(j, 6, stride=16), :] = coded(neighbor_ref[:, lanes]).astype(F32)
        conduct = conduct_ref[:, lanes]
        own[pl.ds(CONDUCT + j, 6, stride=16), :] = conduct
        own[KEEP + j : KEEP + j + 1] = 1.0 - jnp.sum(conduct, axis=0, keepdims=True) - damping_ref[j : j + 1]
    own[START:LISTS] = start_ref[...]
    for j in range(2):
        lanes = slice(LANES * j, LANES * j + LANES)
        lists = coded(lists_ref[:, lanes]).astype(F32)
        own[LISTS + j : LISTS + j + 1] = lists[0:1]
        own[LISTS + 2 + j : LISTS + 3 + j] = lists[1:2]
    own[TARGET:PART] = jnp.zeros((PART - TARGET, LANES), F32)
    own[TARGET : TARGET + 1, 0:TILES] = target_ref[...].astype(F32)
    for copy in range(1, 8):
        packed_ref[copy] = packed_ref[0]


def terms_kernel(source_ref, shares_ref, packed_ref, weight_ref, out_ref, parts_ref, terms_ref):
    flux = jnp.sum(shares_ref[...], axis=0)
    high = flux.astype(jnp.bfloat16).astype(F32)
    rest = flux - high
    middle = rest.astype(jnp.bfloat16).astype(F32)
    parts_ref[...] = jnp.zeros_like(parts_ref)
    parts_ref[:, 0, :] = high
    parts_ref[:, 1, :] = middle
    parts_ref[:, 2, :] = rest - middle
    for t in range(TILES):
        left = parts_ref[source_ref[t]].astype(jnp.bfloat16)
        three = jnp.dot(left, weight_ref[t], preferred_element_type=F32)
        term = jnp.sum(three, axis=0, keepdims=True)
        place = (t + 2 * REACH) % TILES
        while place < TILES + 2 * WINDOW:
            terms_ref[place : place + 1] = term
            place += TILES
    fixed = packed_ref[START : START + 24]
    for p in range(OWNERS):
        out_ref[p, 0:24] = fixed
        out_ref[p, TERMS:SENT] = terms_ref[2 * p : 2 * p + 2 * WINDOW]


def by_distance(left, work):
    work([CENTER])

    def pair(i, carry):
        work([CENTER - i, CENTER + i])
        return carry

    if left:
        lax.fori_loop(1, left + 1, pair, 0)


def load_window(owner_ref, group_ref, staggered_ref, window_ref):
    owner = owner_ref[0]
    for k in range(WINDOW):
        other = (owner + (k - REACH + OWNERS)) % OWNERS
        inside = other // 8 == owner // 8

        @pl.when(inside)
        def _(k=k, other=other):
            window_ref[k] = group_ref[other % 8]

        @pl.when(jnp.logical_not(inside))
        def _(k=k, other=other):
            window_ref[k] = staggered_ref[(other + 4) % 8]


def run_steps(window_ref, lists_ref, forcing_ref, surface_ref, table_ref, scale_ref):
    def spread(left):
        largest = jnp.max(jnp.max(scale_ref[0], axis=1, keepdims=True), axis=0, keepdims=True)
        largest = jnp.maximum(largest, 1e-30)
        scale_ref[1] = jnp.broadcast_to(32767.0 / largest, (8, LANES))
        scale_ref[2] = jnp.broadcast_to(largest * (1.0 / 32767.0), (8, LANES))
        scale_ref[0] = jnp.zeros((8, LANES), F32)

        def work(slots):
            for slot in slots:
                whole = []
                for h in range(2):
                    scaled = surface_ref[slot, 8 * h : 8 * h + 8] * scale_ref[1]
                    whole.append((scaled + jnp.where(scaled < 0, -0.5, 0.5)).astype(I32))
                table_ref[slot, 0:8] = pair_of(*whole)
            sent = []
            for slot in slots:
                value = pick(table_ref.at[slot], 8, lists_ref[slot].astype(I32))
                sent.append(pair_of(value, pltpu.roll(value, 7, 0)))
            for slot, pairs in zip(slots, sent):
                table_ref[slot - 1, 9:10] = pairs[0:1]
                table_ref[slot + 1, 8:9] = pairs[2:3]

        by_distance(left, work)

    def advance(left):
        def work(slots):
            totals = []
            for slot in slots:
                for h in range(2):
                    part = slice(8 * h, 8 * h + 8)
                    flow = None
                    for m in range(6):
                        rows = slice(16 * m + 8 * h, 16 * m + 8 * h + 8)
                        code = window_ref[slot - 2, rows].astype(I32)
                        near = pick(table_ref.at[slot], 10, code).astype(F32)
                        near = window_ref[slot - 2, CONDUCT + 16 * m + 8 * h : CONDUCT + 16 * m + 8 * h + 8] * near
                        flow = near if flow is None else flow + near
                    own = surface_ref[slot, part]
                    keep = window_ref[slot - 2, KEEP + 8 * h : KEEP + 8 * h + 8]
                    totals.append(keep * own + forcing_ref[slot - 2, part] + flow * scale_ref[2])
            largest = scale_ref[0]
            for i, slot in enumerate(slots):
                for h in range(2):
                    total = totals[2 * i + h]
                    surface_ref[slot, 8 * h : 8 * h + 8] = total
                    largest = jnp.maximum(largest, jnp.abs(total))
            scale_ref[0] = largest

        by_distance(left, work)

    largest = jnp.zeros((8, LANES), F32)
    for slot in range(1, WINDOW + 3):
        for h in range(2):
            largest = jnp.maximum(largest, jnp.abs(surface_ref[slot, 8 * h : 8 * h + 8]))
    scale_ref[0] = largest
    spread(REACH + 1)
    for step in range(STEPS):
        left = STEPS - 1 - step
        advance(left)
        if left:
            spread(left)


def first_kernel(owner_ref, arrived_ref, group_ref, staggered_ref, out_ref, lists_ref, forcing_ref, window_ref, terms_ref, surface_ref, table_ref, scale_ref):
    load_window(owner_ref, group_ref, staggered_ref, window_ref)
    owner = owner_ref[0]
    for slot in range(1, WINDOW + 3):
        other = (owner + (slot - CENTER + OWNERS)) % OWNERS
        surface_ref[slot] = arrived_ref[other, 0:16]
        lists_ref[slot] = arrived_ref[other, 16:24]
    for slot in range(1, WINDOW + 3):
        lists_ref[slot, 4:8] = jnp.zeros((4, LANES), F32)
    blocks = lax.broadcasted_iota(I32, (16, TILES), 0)
    for k in range(WINDOW):
        for j in range(2):
            terms_ref[pl.ds(j, OWNERS, stride=2), :] = arrived_ref[:, TERMS + 2 * k + j, :]
        target = window_ref[k, TARGET : TARGET + 1, 0:TILES].astype(I32)
        hot = (blocks == target).astype(F32)
        forcing_ref[k] = jnp.dot(hot, terms_ref[...], precision=HIGHEST, preferred_element_type=F32)
    run_steps(window_ref, lists_ref, forcing_ref, surface_ref, table_ref, scale_ref)
    out_ref[...] = jnp.broadcast_to(surface_ref[CENTER][None], out_ref.shape)


def last_kernel(owner_ref, target_ref, surfaces_ref, group_ref, staggered_ref, lists_ref, forcing_ref, out_ref, values_ref, window_ref, surface_ref, table_ref, scale_ref):
    load_window(owner_ref, group_ref, staggered_ref, window_ref)
    owner = owner_ref[0]
    for slot in range(1, WINDOW + 3):
        surface_ref[slot] = surfaces_ref[(owner + (slot - CENTER + OWNERS)) % OWNERS]
    run_steps(window_ref, lists_ref, forcing_ref, surface_ref, table_ref, scale_ref)
    out_ref[...] = surface_ref[CENTER]
    for t in range(TILES):
        values_ref[t // 2, t % 2 : t % 2 + 1] = surface_ref[CENTER, pl.ds(target_ref[t], 1), :]


def shape(*dims):
    return jax.ShapeDtypeStruct(dims, F32)


def local(
    atm_flux,
    level_weight,
    tile_weight,
    tile_source,
    tile_target,
    ocean_start,
    conductance,
    damping,
    neighbors,
    send_lists,
):
    owner = lax.axis_index("cells").astype(I32).reshape(1)
    window = pltpu.VMEM((WINDOW, PART, LANES), F32)
    scratch = [
        pltpu.VMEM((SLOTS, 16, LANES), F32),
        pltpu.VMEM((SLOTS, 16, LANES), I32),
        pltpu.VMEM((3, 8, LANES), F32),
    ]

    partials, packed = pl.pallas_call(
        prepare_kernel,
        out_shape=(shape(8, 16, LANES), shape(8, PART, LANES)),
        in_specs=[SMEM] + [VMEM] * 7,
        scratch_shapes=[pltpu.VMEM((16, LANES), F32)],
    )(
        level_weight,
        atm_flux,
        neighbors,
        conductance,
        damping.reshape(16, LANES),
        ocean_start.reshape(16, LANES),
        send_lists,
        tile_target.reshape(1, TILES),
    )
    shares = lax.all_to_all(partials, "comp", split_axis=0, concat_axis=0, tiled=True)
    group = exchange(packed, eights(0))
    staggered = exchange(packed, eights(4))
    terms = pl.pallas_call(
        terms_kernel,
        out_shape=shape(OWNERS, SENT, LANES),
        in_specs=[SMEM] + [VMEM] * 3,
        scratch_shapes=[pltpu.VMEM((16, 8, LANES), F32), pltpu.VMEM((TILES + 2 * WINDOW, LANES), F32)],
    )(tile_source, shares, packed[0], tile_weight)
    arrived = exchange(terms, ALL)
    surface, lists, forcing = pl.pallas_call(
        first_kernel,
        out_shape=(shape(OWNERS, 16, LANES), shape(SLOTS, 8, LANES), shape(WINDOW, 16, LANES)),
        in_specs=[SMEM] + [VMEM] * 3,
        scratch_shapes=[window, pltpu.VMEM((TILES, LANES), F32)] + scratch,
    )(owner, arrived, group, staggered)
    surfaces = exchange(surface, ALL)
    ocean_end, values = pl.pallas_call(
        last_kernel,
        out_shape=(shape(16, LANES), shape(OWNERS, 2, LANES)),
        in_specs=[SMEM] * 2 + [VMEM] * 5,
        scratch_shapes=[window] + scratch,
    )(owner, tile_target, surfaces, group, staggered, lists, forcing)
    returned = exchange(values, ALL).reshape(TILES, LANES)
    pulled = jnp.sum(returned[:, None, :] * tile_weight.astype(F32), axis=2)
    source_hot = (tile_source[:, None] == jnp.arange(16, dtype=I32)[None, :]).astype(F32)
    atm_back = jnp.einsum("ra,rb->ab", source_hot, pulled, precision=HIGHEST).reshape(-1)
    return (ocean_end.reshape(-1), atm_back)


def solution(mesh):
    in_specs = (
        P("comp", "cells"),
        P("comp"),
        P("cells", None, None),
        P("cells"),
        P("cells"),
        P("cells"),
        P(None, "cells"),
        P("cells"),
        P(None, "cells"),
        P(None, "cells"),
    )
    out_specs = (P("cells"), P("cells"))
    return jax.shard_map(local, mesh=mesh, in_specs=in_specs, out_specs=out_specs, check_vma=False)
```

time: 211 us -> 146 us (0.69)
  starting transfers between devices: 105 us -> 14.6 us
  blocking collectives: 32.5 us -> 71.9 us
  local copies, waits for them, and re-layouts: 16.5 us -> 2.59 us
  Pallas kernels: 20.4 us -> 26.8 us
  other arithmetic: 6.74 us -> 1.18 us
  waiting for transfers between devices: 23.7 us -> 26.9 us
  matrix products: 3.64 us -> 0.87 us
    ppermute x20 -> x0, starting transfers between devices: 84.1 us -> none  [shifted(): lax.ppermute(block, axis, [((i - distance) % n, i) for i in range(n)])]
    all_to_all x1 -> x4, blocking collectives: 32.5 us -> 71.9 us  [the longest x3 60 us: exchange(): lax.all_to_all(blocks, BOTH, split_axis=0, concat_axis=0, tiled=True, axi...]
    all_to_all x2, waiting for transfers between devices: 9.11 us -> 26.9 us  [exchange(): lax.all_to_all(blocks, BOTH, split_axis=0, concat_axis=0, tiled=True, axi...]
    ppermute x20 -> x0, waiting for transfers between devices: 14.6 us -> none  [shifted(): lax.ppermute(block, axis, [((i - distance) % n, i) for i in range(n)])]
    slice x10 -> x0, local copies, waits for them, and re-layouts: 7.53 us -> none  [local(): from_higher = shifted(outgoing[0:2], 'cells', -1)]
    pallas_call x11 -> x4, Pallas kernels: 20.4 us -> 26.8 us  [the longest x1 10.8 us: local(): pl.pallas_call(first_kernel, out_shape=(shape(OWNERS, 16, LANES), shape(S...]
    all_to_all x2, starting transfers between devices: 20.8 us -> 14.6 us  [exchange(): lax.all_to_all(blocks, BOTH, split_axis=0, concat_axis=0, tiled=True, axi...]
    unnamed x54 -> x8, local copies, waits for them, and re-layouts: 7.06 us -> 0.99 us
  transfers between devices with their start and end apart: 22 -> 2, of which waited for: 11 -> 2; matrix products, arithmetic and copies ran while one was open for 5% -> 1% of each run, Pallas kernels for 1% -> 2%
where the time goes in v3:
time: 146 us; the launch traced here: 145 us
  blocking collectives  71.9 us (49%)
  waiting for transfers between devices  26.9 us (18%)
  Pallas kernels  26.8 us (18%)
  starting transfers between devices  14.6 us (10%)
  local copies, waits for them, and re-layouts  2.59 us (2%)
    all_to_all x3, blocking collectives, exchange(): lax.all_to_all(blocks, BOTH, split_axis=0, concat_axis=0, tiled=True, axi...  60 us
    all_to_all x2, waiting for transfers between devices, exchange(): lax.all_to_all(blocks, BOTH, split_axis=0, concat_axis=0, tiled=True, axi...  26.9 us
    all_to_all x2, starting transfers between devices, exchange(): lax.all_to_all(blocks, BOTH, split_axis=0, concat_axis=0, tiled=True, axi...  14.6 us
    all_to_all x1, blocking collectives, local(): lax.all_to_all(partials, 'comp', split_axis=0, concat_axis=0, tiled=True)  11.9 us
    pallas_call x1, Pallas kernels, local(): pl.pallas_call(first_kernel, out_shape=(shape(OWNERS, 16, LANES), shape(S...  10.8 us
    pallas_call x1, Pallas kernels, local(): pl.pallas_call(last_kernel, out_shape=(shape(16, LANES), shape(OWNERS, 2,...  10.5 us
    pallas_call x1, Pallas kernels, local(): pl.pallas_call(terms_kernel, out_shape=shape(OWNERS, SENT, LANES), in_spe...  3.29 us
  transfers between devices with their start and end apart: 2, of which 2 were waited for; matrix products, arithmetic and copies ran while one was open for 1% of the time, Pallas kernels for 2%

profile of v3, /device:TPU:2, one launch (start us, length us, event | category | flops | bytes accessed | tf_op | source)
XLA Modules:
  0.0 145.4 jit_solution(4991460329236983628)
XLA Ops:
  0.6 2.1 %shard_map.113 = (f32[8,16,128]{2,1,0:T(8,128)}, f32[8,232,128]{2,1,0:T(8,128)}) custom-call(f32[9]{0:T(128)} %weight_ref.2, bf16[9,2048]{1,0:T(8,128)(2,1)} %flux_ref.1, s32[6,2048]{1,0:T(8,128)} %neighbor_ref.1, f32[6,2048]{1,0:T(8,128)} %conduct_ref.1, f32[16,128]{1,0:T(8,128)} %bitcast.12, f32[16,128]{1,0:T(8,128)} %bitcast.13, s32[2,256]{1,0:T(2,128)} %lists_ref.1, ...), custom_call_target="tpu_custom_call" | custom-call | tf_op jit(solution)/shard_map/pallas_call | solution.py:279
  2.7 11.9 %all_to_all.30.shares_ref = f32[8,16,128]{2,1,0:T(8,128)} all-to-all(f32[8,16,128]{2,1,0:T(8,128)} %get-tuple-element.9), channel_id=1, replica_groups=mesh['comp'=8,'cells'=32] {'comp'}, dimensions={0} | all-to-all | bytes 131072 | tf_op jit(solution)/shard_map/all_to_all | solution.py:294
  14.6 5.8 %all-to-all-start.2 = ((f32[8,232,128]{2,1,0:T(8,128)}), f32[8,232,128]{2,1,0:T(8,128)S(1)}, u32[]{:S(2)}, u32[]{:S(2)}) async-start(f32[8,232,128]{2,1,0:T(8,128)} %get-tuple-element.10), calls=%async_computation.2 | async-start | bytes 1900544 | tf_op jit(solution)/shard_map/all_to_all | solution.py:44
  20.5 1.6 %slice_bitcast_fusion.packed_ref = f32[232,128]{1,0:T(8,128)} fusion(f32[8,232,128]{2,1,0:T(8,128)} %get-tuple-element.10), kind=kLoop, calls=%fused_computation.2 | loop fusion | bytes 237568 | tf_op jit(solution)/shard_map/squeeze | solution.py:302
  22.1 3.3 %shard_map.114 = f32[32,40,128]{2,1,0:T(8,128)} custom-call(s32[64]{0:T(128)} %source_ref.1, f32[8,16,128]{2,1,0:T(8,128)} %all_to_all.30.shares_ref, f32[232,128]{1,0:T(8,128)} %slice_bitcast_fusion.packed_ref, bf16[64,128,128]{2,1,0:T(8,128)(2,1)} %weight_ref.3), custom_call_target="tpu_custom_call" | custom-call | tf_op jit(solution)/shard_map/pallas_call | solution.py:297
  25.4 8.4 %all-to-all-done.2.group_ref = f32[8,232,128]{2,1,0:T(8,128)S(1)} async-done(((f32[8,232,128]{2,1,0:T(8,128)}), f32[8,232,128]{2,1,0:T(8,128)S(1)}, u32[]{:S(2)}, u32[]{:S(2)}) %all-to-all-start.2) | async-done | bytes 950304 | tf_op jit(solution)/shard_map/all_to_all | solution.py:44
  33.8 0.0 copy-start
  33.8 28.1 %all_to_all.31.arrived_ref = f32[32,40,128]{2,1,0:T(8,128)} all-to-all(f32[32,40,128]{2,1,0:T(8,128)} %shard_map.114), channel_id=1, replica_groups={{0,1,2,3,4,5,6,7,8,9,10,11,12,13,14,15,208,209,210,211,212,213,214,215,..., dimensions={0} | all-to-all | bytes 1310720 | tf_op jit(solution)/shard_map/all_to_all | solution.py:44
  61.9 8.7 %all-to-all-start.3 = ((f32[8,232,128]{2,1,0:T(8,128)}), f32[8,232,128]{2,1,0:T(8,128)S(1)}, u32[]{:S(2)}, u32[]{:S(2)}) async-start(f32[8,232,128]{2,1,0:T(8,128)} %get-tuple-element.10), calls=%async_computation.3 | async-start | bytes 1900544 | tf_op jit(solution)/shard_map/all_to_all | solution.py:44
  70.6 18.5 %all-to-all-done.3.staggered_ref = f32[8,232,128]{2,1,0:T(8,128)S(1)} async-done(((f32[8,232,128]{2,1,0:T(8,128)}), f32[8,232,128]{2,1,0:T(8,128)S(1)}, u32[]{:S(2)}, u32[]{:S(2)}) %all-to-all-start.3) | async-done | bytes 950304 | tf_op jit(solution)/shard_map/all_to_all | solution.py:44
  89.1 0.0 copy-start.1
  89.1 0.0 copy-done
  89.1 1.0 copy-done.1
  90.1 10.8 %shard_map.115 = (f32[32,16,128]{2,1,0:T(8,128)}, f32[13,8,128]{2,1,0:T(8,128)}, f32[9,16,128]{2,1,0:T(8,128)}) custom-call(s32[1]{0:T(128)} %bitcast.owner_ref, f32[32,40,128]{2,1,0:T(8,128)} %all_to_all.31.arrived_ref, f32[8,232,128]{2,1,0:T(8,128)} %copy-done, f32[8,232,128]{2,1,0:T(8,128)} %copy-done.1), custom_call_target="tpu_custom_call" | custom-call | tf_op jit(solution)/shard_map/pallas_call | solution.py:304
  100.9 0.0 copy-start.2
  100.9 18.2 %all_to_all.32.surfaces_ref = f32[32,16,128]{2,1,0:T(8,128)} all-to-all(f32[32,16,128]{2,1,0:T(8,128)} %get-tuple-element.11), channel_id=1, replica_groups={{0,1,2,3,4,5,6,7,8,9,10,11,12,13,14,15,208,209,210,211,212,213,214,215,..., dimensions={0} | all-to-all | bytes 524288 | tf_op jit(solution)/shard_map/all_to_all | solution.py:44
  119.1 0.0 copy-start.3
  119.1 10.5 %shard_map.116 = (f32[16,128]{1,0:T(8,128)}, f32[32,2,128]{2,1,0:T(2,128)}) custom-call(s32[1]{0:T(128)} %bitcast.owner_ref, s32[64]{0:T(128)} %target_ref.1, f32[32,16,128]{2,1,0:T(8,128)} %all_to_all.32.surfaces_ref, f32[8,232,128]{2,1,0:T(8,128)} %copy-done, f32[8,232,128]{2,1,0:T(8,128)} %copy-done.1, f32[13,8,128]{2,1,0:T(8,128)} %get-tuple-element.12.lists_ref, ...), custom_call_target="tpu_custom_call" | custom-call | tf_op jit(solution)/shard_map/pallas_call | solution.py:311
  129.7 13.6 %all_to_all.33 = f32[32,2,128]{2,1,0:T(2,128)S(1)} all-to-all(f32[32,2,128]{2,1,0:T(2,128)} %get-tuple-element.15), channel_id=1, replica_groups={{0,1,2,3,4,5,6,7,8,9,10,11,12,13,14,15,208,209,210,211,212,213,214,215,..., dimensions={0} | all-to-all | bytes 65536 | tf_op jit(solution)/shard_map/all_to_all | solution.py:44
  143.3 0.0 copy-done.2
  143.3 1.2 multiply_reduce_fusion
  144.5 0.0 copy-done.3
  144.5 0.9 convolution_bitcast_fusion
Async XLA Ops:
  14.6 19.1 %all-to-all-start.2 = ((f32[8,232,128]{2,1,0:T(8,128)}), f32[8,232,128]{2,1,0:T(8,128)S(1)}, u32[]{:S(2)}, u32[]{:S(2)}) async-start(f32[8,232,128]{2,1,0:T(8,128)} %get-tuple-element.10), calls=%async_computation.2 | async-start | bytes 1900544 | tf_op jit(solution)/shard_map/all_to_all | solution.py:44
  33.8 55.3 %copy-start = (f32[8,232,128]{2,1,0:T(8,128)}, f32[8,232,128]{2,1,0:T(8,128)S(1)}, u32[]{:S(2)}) copy-start(f32[8,232,128]{2,1,0:T(8,128)S(1)} %all-to-all-done.2.group_ref) | copy-start | bytes 2850820
  61.9 27.2 %all-to-all-start.3 = ((f32[8,232,128]{2,1,0:T(8,128)}), f32[8,232,128]{2,1,0:T(8,128)S(1)}, u32[]{:S(2)}, u32[]{:S(2)}) async-start(f32[8,232,128]{2,1,0:T(8,128)} %get-tuple-element.10), calls=%async_computation.3 | async-start | bytes 1900544 | tf_op jit(solution)/shard_map/all_to_all | solution.py:44
  89.1 1.0 copy-start.1
  100.9 42.4 %copy-start.2 = (bf16[64,128,128]{2,1,0:T(8,128)(2,1)S(1)}, bf16[64,128,128]{2,1,0:T(8,128)(2,1)}, u32[]{:S(2)}) copy-start(bf16[64,128,128]{2,1,0:T(8,128)(2,1)} %weight_ref.3) | copy-start | bytes 6291460
  119.1 25.4 %copy-start.3 = (s32[64]{0:T(128)S(1)}, s32[64]{0:T(128)}, u32[]{:S(2)}) copy-start(s32[64]{0:T(128)} %source_ref.1) | copy-start | bytes 772

commit v4 on v3

--- a/solution.py
+++ b/solution.py
@@ -34,14 +34,17 @@
 ALL = [[device_of(owner, *copy) for owner in range(OWNERS)] for copy in COPIES]
 
 
-def eights(first):
-    return [
-        [device_of((8 * g + first + i) % OWNERS, *copy) for i in range(8)] for copy in COPIES for g in range(4)
+def from_owner(block, offset):
+    route = [
+        (device_of((owner + offset) % OWNERS, *copy), device_of(owner, *copy))
+        for copy in COPIES
+        for owner in range(OWNERS)
     ]
-
-
-def exchange(blocks, groups):
-    return lax.all_to_all(blocks, BOTH, split_axis=0, concat_axis=0, tiled=True, axis_index_groups=groups)
+    return lax.ppermute(block, BOTH, route)
+
+
+def exchange(blocks):
+    return lax.all_to_all(blocks, BOTH, split_axis=0, concat_axis=0, tiled=True, axis_index_groups=ALL)
 
 
 def lane_pick(rows, lane):
@@ -89,7 +92,7 @@
         block = flux_ref[:, lanes].astype(F32)
         row_ref[j : j + 1] = sum(weight_ref[level] * block[level : level + 1] for level in range(block.shape[0]))
     shares_ref[...] = jnp.broadcast_to(row_ref[...][None], shares_ref.shape)
-    own = packed_ref.at[0]
+    own = packed_ref
     for j in range(16):
         lanes = slice(LANES * j, LANES * j + LANES)
         own[pl.ds(j, 6, stride=16), :] = coded(neighbor_ref[:, lanes]).astype(F32)
@@ -104,8 +107,6 @@
         own[LISTS + 2 + j : LISTS + 3 + j] = lists[1:2]
     own[TARGET:PART] = jnp.zeros((PART - TARGET, LANES), F32)
     own[TARGET : TARGET + 1, 0:TILES] = target_ref[...].astype(F32)
-    for copy in range(1, 8):
-        packed_ref[copy] = packed_ref[0]
 
 
 def terms_kernel(source_ref, shares_ref, packed_ref, weight_ref, out_ref, parts_ref, terms_ref):
@@ -140,21 +141,6 @@
 
     if left:
         lax.fori_loop(1, left + 1, pair, 0)
-
-
-def load_window(owner_ref, group_ref, staggered_ref, window_ref):
-    owner = owner_ref[0]
-    for k in range(WINDOW):
-        other = (owner + (k - REACH + OWNERS)) % OWNERS
-        inside = other // 8 == owner // 8
-
-        @pl.when(inside)
-        def _(k=k, other=other):
-            window_ref[k] = group_ref[other % 8]
-
-        @pl.when(jnp.logical_not(inside))
-        def _(k=k, other=other):
-            window_ref[k] = staggered_ref[(other + 4) % 8]
 
 
 def run_steps(window_ref, lists_ref, forcing_ref, surface_ref, table_ref, scale_ref):
@@ -221,8 +207,7 @@
             spread(left)
 
 
-def first_kernel(owner_ref, arrived_ref, group_ref, staggered_ref, out_ref, lists_ref, forcing_ref, window_ref, terms_ref, surface_ref, table_ref, scale_ref):
-    load_window(owner_ref, group_ref, staggered_ref, window_ref)
+def first_kernel(owner_ref, arrived_ref, window_ref, out_ref, lists_ref, forcing_ref, terms_ref, surface_ref, table_ref, scale_ref):
     owner = owner_ref[0]
     for slot in range(1, WINDOW + 3):
         other = (owner + (slot - CENTER + OWNERS)) % OWNERS
@@ -241,8 +226,7 @@
     out_ref[...] = jnp.broadcast_to(surface_ref[CENTER][None], out_ref.shape)
 
 
-def last_kernel(owner_ref, target_ref, surfaces_ref, group_ref, staggered_ref, lists_ref, forcing_ref, out_ref, values_ref, window_ref, surface_ref, table_ref, scale_ref):
-    load_window(owner_ref, group_ref, staggered_ref, window_ref)
+def last_kernel(owner_ref, target_ref, surfaces_ref, window_ref, lists_ref, forcing_ref, out_ref, values_ref, surface_ref, table_ref, scale_ref):
     owner = owner_ref[0]
     for slot in range(1, WINDOW + 3):
         surface_ref[slot] = surfaces_ref[(owner + (slot - CENTER + OWNERS)) % OWNERS]
@@ -269,7 +253,6 @@
     send_lists,
 ):
     owner = lax.axis_index("cells").astype(I32).reshape(1)
-    window = pltpu.VMEM((WINDOW, PART, LANES), F32)
     scratch = [
         pltpu.VMEM((SLOTS, 16, LANES), F32),
         pltpu.VMEM((SLOTS, 16, LANES), I32),
@@ -278,7 +261,7 @@
 
     partials, packed = pl.pallas_call(
         prepare_kernel,
-        out_shape=(shape(8, 16, LANES), shape(8, PART, LANES)),
+        out_shape=(shape(8, 16, LANES), shape(PART, LANES)),
         in_specs=[SMEM] + [VMEM] * 7,
         scratch_shapes=[pltpu.VMEM((16, LANES), F32)],
     )(
@@ -291,30 +274,36 @@
         send_lists,
         tile_target.reshape(1, TILES),
     )
-    shares = lax.all_to_all(partials, "comp", split_axis=0, concat_axis=0, tiled=True)
-    group = exchange(packed, eights(0))
-    staggered = exchange(packed, eights(4))
+    with jax.named_scope("levels"):
+        shares = lax.all_to_all(partials, "comp", split_axis=0, concat_axis=0, tiled=True)
+    with jax.named_scope("near"):
+        lower, higher = from_owner(packed, -1), from_owner(packed, 1)
+    three = jnp.concatenate([lower, packed, higher], axis=0)
     terms = pl.pallas_call(
         terms_kernel,
         out_shape=shape(OWNERS, SENT, LANES),
         in_specs=[SMEM] + [VMEM] * 3,
         scratch_shapes=[pltpu.VMEM((16, 8, LANES), F32), pltpu.VMEM((TILES + 2 * WINDOW, LANES), F32)],
-    )(tile_source, shares, packed[0], tile_weight)
-    arrived = exchange(terms, ALL)
+    )(tile_source, shares, packed, tile_weight)
+    with jax.named_scope("send"):
+        arrived = exchange(terms)
+    with jax.named_scope("far"):
+        lower, higher = from_owner(three, -3), from_owner(three, 3)
+    window = jnp.concatenate([lower, three, higher], axis=0).reshape(WINDOW, PART, LANES)
     surface, lists, forcing = pl.pallas_call(
         first_kernel,
         out_shape=(shape(OWNERS, 16, LANES), shape(SLOTS, 8, LANES), shape(WINDOW, 16, LANES)),
-        in_specs=[SMEM] + [VMEM] * 3,
-        scratch_shapes=[window, pltpu.VMEM((TILES, LANES), F32)] + scratch,
-    )(owner, arrived, group, staggered)
-    surfaces = exchange(surface, ALL)
+        in_specs=[SMEM] + [VMEM] * 2,
+        scratch_shapes=[pltpu.VMEM((TILES, LANES), F32)] + scratch,
+    )(owner, arrived, window)
+    surfaces = exchange(surface)
     ocean_end, values = pl.pallas_call(
         last_kernel,
         out_shape=(shape(16, LANES), shape(OWNERS, 2, LANES)),
-        in_specs=[SMEM] * 2 + [VMEM] * 5,
-        scratch_shapes=[window] + scratch,
-    )(owner, tile_target, surfaces, group, staggered, lists, forcing)
-    returned = exchange(values, ALL).reshape(TILES, LANES)
+        in_specs=[SMEM] * 2 + [VMEM] * 4,
+        scratch_shapes=scratch,
+    )(owner, tile_target, surfaces, window, lists, forcing)
+    returned = exchange(values).reshape(TILES, LANES)
     pulled = jnp.sum(returned[:, None, :] * tile_weight.astype(F32), axis=2)
     source_hot = (tile_source[:, None] == jnp.arange(16, dtype=I32)[None, :]).astype(F32)
     atm_back = jnp.einsum("ra,rb->ab", source_hot, pulled, precision=HIGHEST).reshape(-1)

time: 146 us -> 116 us (0.79)
  blocking collectives: 71.9 us -> 27.3 us
  starting transfers between devices: 14.6 us -> 23.3 us
  waiting for transfers between devices: 26.9 us -> 34.2 us
    all_to_all x3 -> x2, blocking collectives: 60 us -> 27.3 us  [exchange(): lax.all_to_all(blocks, BOTH, split_axis=0, concat_axis=0, tiled=True, axi...]
    ppermute x0 -> x4, waiting for transfers between devices: none -> 28.8 us  [from_owner(): return lax.ppermute(block, BOTH, route)]
    all_to_all x2 -> x1, waiting for transfers between devices: 26.9 us -> 0.01 us  [exchange(): lax.all_to_all(blocks, BOTH, split_axis=0, concat_axis=0, tiled=True, axi...]
    all_to_all x1 -> x0, blocking collectives: 11.9 us -> none  [local(): lax.all_to_all(partials, 'comp', split_axis=0, concat_axis=0, tiled=True)]
    ppermute x0 -> x4, starting transfers between devices: none -> 8.35 us  [from_owner(): return lax.ppermute(block, BOTH, route)]
    all_to_all x0 -> x1, starting transfers between devices: none -> 5.9 us  [local(): lax.all_to_all(partials, 'comp', split_axis=0, concat_axis=0, tiled=True)]
    all_to_all x2 -> x1, starting transfers between devices: 14.6 us -> 9.05 us  [exchange(): lax.all_to_all(blocks, BOTH, split_axis=0, concat_axis=0, tiled=True, axi...]
    all_to_all x0 -> x1, waiting for transfers between devices: none -> 5.38 us  [local(): lax.all_to_all(partials, 'comp', split_axis=0, concat_axis=0, tiled=True)]
  transfers between devices with their start and end apart: 2 -> 6, of which waited for: 2 -> 2; matrix products, arithmetic and copies ran while one was open for 1% -> 0% of each run, Pallas kernels for 2% -> 3%
where the time goes in v4:
time: 116 us; the launch traced here: 115 us
  waiting for transfers between devices  34.2 us (29%)
  blocking collectives  27.3 us (24%)
  Pallas kernels  25.5 us (22%)
  starting transfers between devices  23.3 us (20%)
  local copies, waits for them, and re-layouts  1.93 us (2%)
  other arithmetic  1.18 us (1%)
    ppermute x4, waiting for transfers between devices, from_owner(): return lax.ppermute(block, BOTH, route)  28.8 us
    all_to_all x2, blocking collectives, exchange(): lax.all_to_all(blocks, BOTH, split_axis=0, concat_axis=0, tiled=True, axi...  27.3 us
    pallas_call x1, Pallas kernels, local(): pl.pallas_call(first_kernel, out_shape=(shape(OWNERS, 16, LANES), shape(S...  10.5 us
    pallas_call x1, Pallas kernels, local(): pl.pallas_call(last_kernel, out_shape=(shape(16, LANES), shape(OWNERS, 2,...  9.97 us
    all_to_all x1, starting transfers between devices, exchange(): lax.all_to_all(blocks, BOTH, split_axis=0, concat_axis=0, tiled=True, axi...  9.05 us
    ppermute x4, starting transfers between devices, from_owner(): return lax.ppermute(block, BOTH, route)  8.35 us
    all_to_all x1, starting transfers between devices, local(): lax.all_to_all(partials, 'comp', split_axis=0, concat_axis=0, tiled=True)  5.9 us
    all_to_all x1, waiting for transfers between devices, local(): lax.all_to_all(partials, 'comp', split_axis=0, concat_axis=0, tiled=True)  5.38 us
  transfers between devices with their start and end apart: 6, of which 2 were waited for; matrix products, arithmetic and copies ran while one was open for 0% of the time, Pallas kernels for 3%

profile of v4, /device:TPU:2, one launch (start us, length us, event | category | flops | bytes accessed | tf_op | source)
XLA Modules:
  0.0 115.1 jit_solution(11606751143202030477)
XLA Ops:
  0.6 1.7 %shard_map.113 = (f32[8,16,128]{2,1,0:T(8,128)}, f32[232,128]{1,0:T(8,128)}) custom-call(f32[9]{0:T(128)} %weight_ref.2, bf16[9,2048]{1,0:T(8,128)(2,1)} %flux_ref.1, s32[6,2048]{1,0:T(8,128)} %neighbor_ref.1, f32[6,2048]{1,0:T(8,128)} %conduct_ref.1, f32[16,128]{1,0:T(8,128)} %bitcast.13, f32[16,128]{1,0:T(8,128)} %bitcast.14, s32[2,256]{1,0:T(2,128)} %lists_ref.1, ...), custom_call_target="tpu_custom_call" | custom-call | tf_op jit(solution)/shard_map/pallas_call | solution.py:262
  2.4 1.5 %collective-permute-start = (f32[232,128]{1,0:T(8,128)}, f32[232,128]{1,0:T(8,128)S(1)}, u32[]{:S(2)}, u32[]{:S(2)}) collective-permute-start(f32[232,128]{1,0:T(8,128)} %get-tuple-element.10.packed_ref), channel_id=1, source_target_pairs={{223,0},{0,1},{1,2},{2,3},{3,4},{4,5},{5,6},{6,7},{7,8},{8,9},{9,1... | collective-permute-start | bytes 356360 | tf_op jit(solution)/shard_map/near/ppermute | solution.py:43
  3.9 5.9 %all-to-all-start = ((f32[8,16,128]{2,1,0:T(8,128)}), f32[8,16,128]{2,1,0:T(8,128)S(1)}, u32[]{:S(2)}, u32[]{:S(2)}) async-start(f32[8,16,128]{2,1,0:T(8,128)} %get-tuple-element.9), calls=%async_computation | async-start | bytes 131072 | tf_op jit(solution)/shard_map/levels/all_to_all | solution.py:278
  9.8 0.5 collective-permute-start.1
  10.3 5.4 %all-to-all-done.shares_ref = f32[8,16,128]{2,1,0:T(8,128)S(1)} async-done(((f32[8,16,128]{2,1,0:T(8,128)}), f32[8,16,128]{2,1,0:T(8,128)S(1)}, u32[]{:S(2)}, u32[]{:S(2)}) %all-to-all-start) | async-done | bytes 65568 | tf_op jit(solution)/shard_map/levels/all_to_all | solution.py:278
  15.7 0.0 copy-start.4
  15.7 0.6 copy-done.4
  16.3 3.3 %shard_map.114 = f32[32,40,128]{2,1,0:T(8,128)} custom-call(s32[64]{0:T(128)} %source_ref.1, f32[8,16,128]{2,1,0:T(8,128)} %copy-done.4, f32[232,128]{1,0:T(8,128)} %get-tuple-element.10.packed_ref, bf16[64,128,128]{2,1,0:T(8,128)(2,1)} %weight_ref.3), custom_call_target="tpu_custom_call" | custom-call | tf_op jit(solution)/shard_map/pallas_call | solution.py:282
  19.6 0.0 copy-start.3
  19.6 9.0 %all-to-all-start.1 = ((f32[32,40,128]{2,1,0:T(8,128)}), f32[32,40,128]{2,1,0:T(8,128)S(1)}, u32[]{:S(2)}, u32[]{:S(2)}) async-start(f32[32,40,128]{2,1,0:T(8,128)} %shard_map.114), calls=%async_computation.1 | async-start | bytes 1310720 | tf_op jit(solution)/shard_map/send/all_to_all | solution.py:47
  28.7 0.0 collective-permute-done
  28.7 0.0 copy-done.3
  28.7 0.0 collective-permute-done.1
  28.7 1.5 %collective-permute-start.2 = (f32[696,128]{1,0:T(8,128)S(1)}, f32[696,128]{1,0:T(8,128)S(1)}, u32[]{:S(2)}, u32[]{:S(2)}) collective-permute-start(f32[696,128]{1,0:T(8,128)S(1)} %constant_dynamic-update-slice_fusion), channel_id=1, source_target_pairs={{221,0},{222,1},{223,2},{0,3},{1,4},{2,5},{3,6},{4,7},{5,8},{6,9},... | collective-permute-start | bytes 1069064 | tf_op jit(solution)/shard_map/far/ppermute | solution.py:43
  30.3 4.8 %collective-permute-start.3 = (f32[696,128]{1,0:T(8,128)S(1)}, f32[696,128]{1,0:T(8,128)S(1)}, u32[]{:S(2)}, u32[]{:S(2)}) collective-permute-start(f32[696,128]{1,0:T(8,128)S(1)} %constant_dynamic-update-slice_fusion), channel_id=1, source_target_pairs={{3,0},{4,1},{5,2},{6,3},{7,4},{8,5},{9,6},{10,7},{11,8},{12,9},{13... | collective-permute-start | bytes 1069064 | tf_op jit(solution)/shard_map/far/ppermute | solution.py:43
  35.1 28.8 %collective-permute-done.2 = f32[696,128]{1,0:T(8,128)S(1)} collective-permute-done((f32[696,128]{1,0:T(8,128)S(1)}, f32[696,128]{1,0:T(8,128)S(1)}, u32[]{:S(2)}, u32[]{:S(2)}) %collective-permute-start.2) | collective-permute-done | bytes 356384 | tf_op jit(solution)/shard_map/far/ppermute | solution.py:43
  63.9 0.0 collective-permute-done.3
  64.0 0.0 copy-start.1
  64.0 0.0 all-to-all-done.1.arrived_ref
  64.0 0.0 copy-start.2
  64.0 0.9 copy-done.2
  64.9 0.3 copy-done.1
  65.2 0.0 copy-start
  65.2 10.5 %shard_map.115 = (f32[32,16,128]{2,1,0:T(8,128)}, f32[13,8,128]{2,1,0:T(8,128)}, f32[9,16,128]{2,1,0:T(8,128)}) custom-call(s32[1]{0:T(128)} %bitcast.owner_ref, f32[32,40,128]{2,1,0:T(8,128)} %copy-done.2, f32[9,232,128]{2,1,0:T(8,128)} %bitcast.10), custom_call_target="tpu_custom_call" | custom-call | tf_op jit(solution)/shard_map/pallas_call | solution.py:293
  75.7 13.7 %all_to_all.20.surfaces_ref = f32[32,16,128]{2,1,0:T(8,128)} all-to-all(f32[32,16,128]{2,1,0:T(8,128)} %get-tuple-element.11), channel_id=1, replica_groups={{0,1,2,3,4,5,6,7,8,9,10,11,12,13,14,15,208,209,210,211,212,213,214,215,..., dimensions={0} | all-to-all | bytes 524288 | tf_op jit(solution)/shard_map/all_to_all | solution.py:47
  89.4 10.0 %shard_map.116 = (f32[16,128]{1,0:T(8,128)}, f32[32,2,128]{2,1,0:T(2,128)}) custom-call(s32[1]{0:T(128)} %bitcast.owner_ref, s32[64]{0:T(128)} %target_ref.1, f32[32,16,128]{2,1,0:T(8,128)} %all_to_all.20.surfaces_ref, f32[9,232,128]{2,1,0:T(8,128)} %bitcast.11, f32[13,8,128]{2,1,0:T(8,128)} %get-tuple-element.12.lists_ref, ...), custom_call_target="tpu_custom_call" | custom-call | tf_op jit(solution)/shard_map/pallas_call | solution.py:300
  99.4 13.6 %all_to_all.21 = f32[32,2,128]{2,1,0:T(2,128)S(1)} all-to-all(f32[32,2,128]{2,1,0:T(2,128)} %get-tuple-element.15), channel_id=1, replica_groups={{0,1,2,3,4,5,6,7,8,9,10,11,12,13,14,15,208,209,210,211,212,213,214,215,..., dimensions={0} | all-to-all | bytes 65536 | tf_op jit(solution)/shard_map/all_to_all | solution.py:47
  113.0 0.0 copy-done
  113.0 0.0 copy-start.5
  113.0 1.2 %multiply_reduce_fusion = f32[64,128]{1,0:T(8,128)S(1)} fusion(bf16[64,128,128]{2,1,0:T(8,128)(2,1)S(1)} %copy-done, f32[64,128]{1,0:T(8,128)S(1)} %bitcast.12), kind=kLoop, calls=%fused_computation | loop fusion | flops 3137536 | bytes 2162688 | tf_op jit(solution)/shard_map/reduce_sum | solution.py:307
  114.2 0.0 copy-done.5
  114.2 0.9 convolution_bitcast_fusion
  (8 shorter events, 0.1 us)
Async XLA Ops:
  2.4 26.3 %collective-permute-start = (f32[232,128]{1,0:T(8,128)}, f32[232,128]{1,0:T(8,128)S(1)}, u32[]{:S(2)}, u32[]{:S(2)}) collective-permute-start(f32[232,128]{1,0:T(8,128)} %get-tuple-element.10.packed_ref), channel_id=1, source_target_pairs={{223,0},{0,1},{1,2},{2,3},{3,4},{4,5},{5,6},{6,7},{7,8},{8,9},{9,1... | collective-permute-start | bytes 356360 | tf_op jit(solution)/shard_map/near/ppermute | solution.py:43
  3.9 11.8 %all-to-all-start = ((f32[8,16,128]{2,1,0:T(8,128)}), f32[8,16,128]{2,1,0:T(8,128)S(1)}, u32[]{:S(2)}, u32[]{:S(2)}) async-start(f32[8,16,128]{2,1,0:T(8,128)} %get-tuple-element.9), calls=%async_computation | async-start | bytes 131072 | tf_op jit(solution)/shard_map/levels/all_to_all | solution.py:278
  9.8 19.0 %collective-permute-start.1 = (f32[232,128]{1,0:T(8,128)}, f32[232,128]{1,0:T(8,128)S(1)}, u32[]{:S(2)}, u32[]{:S(2)}) collective-permute-start(f32[232,128]{1,0:T(8,128)} %get-tuple-element.10.packed_ref), channel_id=1, source_target_pairs={{1,0},{2,1},{3,2},{4,3},{5,4},{6,5},{7,6},{8,7},{9,8},{10,9},{11,1... | collective-permute-start | bytes 356360 | tf_op jit(solution)/shard_map/near/ppermute | solution.py:43
  15.7 0.6 copy-start.4
  19.6 9.1 %copy-start.3 = (f32[232,128]{1,0:T(8,128)S(1)}, f32[232,128]{1,0:T(8,128)}, u32[]{:S(2)}) copy-start(f32[232,128]{1,0:T(8,128)} %get-tuple-element.10.packed_ref) | copy-start | bytes 356356
  19.6 44.4 %all-to-all-start.1 = ((f32[32,40,128]{2,1,0:T(8,128)}), f32[32,40,128]{2,1,0:T(8,128)S(1)}, u32[]{:S(2)}, u32[]{:S(2)}) async-start(f32[32,40,128]{2,1,0:T(8,128)} %shard_map.114), calls=%async_computation.1 | async-start | bytes 1310720 | tf_op jit(solution)/shard_map/send/all_to_all | solution.py:47
  28.7 35.1 %collective-permute-start.2 = (f32[696,128]{1,0:T(8,128)S(1)}, f32[696,128]{1,0:T(8,128)S(1)}, u32[]{:S(2)}, u32[]{:S(2)}) collective-permute-start(f32[696,128]{1,0:T(8,128)S(1)} %constant_dynamic-update-slice_fusion), channel_id=1, source_target_pairs={{221,0},{222,1},{223,2},{0,3},{1,4},{2,5},{3,6},{4,7},{5,8},{6,9},... | collective-permute-start | bytes 1069064 | tf_op jit(solution)/shard_map/far/ppermute | solution.py:43
  30.3 33.7 %collective-permute-start.3 = (f32[696,128]{1,0:T(8,128)S(1)}, f32[696,128]{1,0:T(8,128)S(1)}, u32[]{:S(2)}, u32[]{:S(2)}) collective-permute-start(f32[696,128]{1,0:T(8,128)S(1)} %constant_dynamic-update-slice_fusion), channel_id=1, source_target_pairs={{3,0},{4,1},{5,2},{6,3},{7,4},{8,5},{9,6},{10,7},{11,8},{12,9},{13... | collective-permute-start | bytes 1069064 | tf_op jit(solution)/shard_map/far/ppermute | solution.py:43
  64.0 1.2 %copy-start.1 = (f32[2088,128]{1,0:T(8,128)}, f32[2088,128]{1,0:T(8,128)S(1)}, u32[]{:S(2)}) copy-start(f32[2088,128]{1,0:T(8,128)S(1)} %constant_dynamic-update-slice_fusion.3) | copy-start | bytes 3207172
  64.0 0.9 copy-start.2
  65.2 47.8 %copy-start = (bf16[64,128,128]{2,1,0:T(8,128)(2,1)S(1)}, bf16[64,128,128]{2,1,0:T(8,128)(2,1)}, u32[]{:S(2)}) copy-start(bf16[64,128,128]{2,1,0:T(8,128)(2,1)} %weight_ref.3) | copy-start | bytes 6291460
  113.0 1.2 %copy-start.5 = (s32[64]{0:T(128)S(1)}, s32[64]{0:T(128)}, u32[]{:S(2)}) copy-start(s32[64]{0:T(128)} %source_ref.1) | copy-start | bytes 772

commit v5 on v4

--- a/solution.py
+++ b/solution.py
@@ -16,8 +16,7 @@
 SLOTS = WINDOW + 4
 PART = 232
 CONDUCT, KEEP, START, LISTS, TARGET = 96, 192, 208, 224, 228
-SENT = 40
-TERMS = 22
+SENT = 24
 BOTH = ("comp", "cells")
 HIGHEST = lax.Precision.HIGHEST
 F32, I32 = jnp.float32, jnp.int32
@@ -30,8 +29,13 @@
     return (2 * z_low + core) * OWNERS + owner
 
 
-COPIES = [(copy, core) for copy in range(4) for core in range(2)]
-ALL = [[device_of(owner, *copy) for owner in range(OWNERS)] for copy in COPIES]
+COPIES = [(copy, core) for copy in (0, 3) for core in range(2)]
+IDLE = [
+    [(2 * z_low + core) * OWNERS + half * HALF + i for core in range(2) for i in range(HALF)]
+    for z_low in (1, 2)
+    for half in range(2)
+]
+ALL = [[device_of(owner, *copy) for owner in range(OWNERS)] for copy in COPIES] + IDLE
 
 
 def from_owner(block, offset):
@@ -41,6 +45,17 @@
         for owner in range(OWNERS)
     ]
     return lax.ppermute(block, BOTH, route)
+
+
+def to_idle(block):
+    route = [
+        ((2 * here + core) * OWNERS + owner, (2 * there + core) * OWNERS + owner)
+        for here, there in ((0, 1), (3, 2))
+        for core in range(2)
+        for owner in range(OWNERS)
+    ]
+    z_low = lax.axis_index("comp") // 2
+    return jnp.where((z_low == 0) | (z_low == 3), block, lax.ppermute(block, BOTH, route))
 
 
 def exchange(blocks):
@@ -109,7 +124,7 @@
     own[TARGET : TARGET + 1, 0:TILES] = target_ref[...].astype(F32)
 
 
-def terms_kernel(source_ref, shares_ref, packed_ref, weight_ref, out_ref, parts_ref, terms_ref):
+def terms_kernel(source_ref, shares_ref, weight_ref, out_ref, parts_ref, terms_ref):
     flux = jnp.sum(shares_ref[...], axis=0)
     high = flux.astype(jnp.bfloat16).astype(F32)
     rest = flux - high
@@ -126,10 +141,8 @@
         while place < TILES + 2 * WINDOW:
             terms_ref[place : place + 1] = term
             place += TILES
-    fixed = packed_ref[START : START + 24]
     for p in range(OWNERS):
-        out_ref[p, 0:24] = fixed
-        out_ref[p, TERMS:SENT] = terms_ref[2 * p : 2 * p + 2 * WINDOW]
+        out_ref[p, 0 : 2 * WINDOW] = terms_ref[2 * p : 2 * p + 2 * WINDOW]
 
 
 def by_distance(left, work):
@@ -207,18 +220,17 @@
             spread(left)
 
 
-def first_kernel(owner_ref, arrived_ref, window_ref, out_ref, lists_ref, forcing_ref, terms_ref, surface_ref, table_ref, scale_ref):
-    owner = owner_ref[0]
-    for slot in range(1, WINDOW + 3):
-        other = (owner + (slot - CENTER + OWNERS)) % OWNERS
-        surface_ref[slot] = arrived_ref[other, 0:16]
-        lists_ref[slot] = arrived_ref[other, 16:24]
-    for slot in range(1, WINDOW + 3):
-        lists_ref[slot, 4:8] = jnp.zeros((4, LANES), F32)
+def first_kernel(arrived_ref, below_ref, above_ref, window_ref, out_ref, lists_ref, forcing_ref, terms_ref, surface_ref, table_ref, scale_ref):
+    for slot, ref in ((1, below_ref), (WINDOW + 2, above_ref)):
+        surface_ref[slot] = ref[0:16]
+        lists_ref[slot] = ref[16:24]
+    for slot in range(2, WINDOW + 2):
+        surface_ref[slot] = window_ref[slot - 2, START:LISTS]
+        lists_ref[slot] = window_ref[slot - 2, LISTS:PART]
     blocks = lax.broadcasted_iota(I32, (16, TILES), 0)
     for k in range(WINDOW):
         for j in range(2):
-            terms_ref[pl.ds(j, OWNERS, stride=2), :] = arrived_ref[:, TERMS + 2 * k + j, :]
+            terms_ref[pl.ds(j, OWNERS, stride=2), :] = arrived_ref[:, 2 * k + j, :]
         target = window_ref[k, TARGET : TARGET + 1, 0:TILES].astype(I32)
         hot = (blocks == target).astype(F32)
         forcing_ref[k] = jnp.dot(hot, terms_ref[...], precision=HIGHEST, preferred_element_type=F32)
@@ -282,20 +294,21 @@
     terms = pl.pallas_call(
         terms_kernel,
         out_shape=shape(OWNERS, SENT, LANES),
-        in_specs=[SMEM] + [VMEM] * 3,
+        in_specs=[SMEM] + [VMEM] * 2,
         scratch_shapes=[pltpu.VMEM((16, 8, LANES), F32), pltpu.VMEM((TILES + 2 * WINDOW, LANES), F32)],
-    )(tile_source, shares, packed, tile_weight)
+    )(tile_source, shares, tile_weight)
     with jax.named_scope("send"):
         arrived = exchange(terms)
     with jax.named_scope("far"):
         lower, higher = from_owner(three, -3), from_owner(three, 3)
+        outer = packed[START : START + 24]
+        below, above = from_owner(outer, -STEPS), from_owner(outer, STEPS)
     window = jnp.concatenate([lower, three, higher], axis=0).reshape(WINDOW, PART, LANES)
     surface, lists, forcing = pl.pallas_call(
         first_kernel,
         out_shape=(shape(OWNERS, 16, LANES), shape(SLOTS, 8, LANES), shape(WINDOW, 16, LANES)),
-        in_specs=[SMEM] + [VMEM] * 2,
         scratch_shapes=[pltpu.VMEM((TILES, LANES), F32)] + scratch,
-    )(owner, arrived, window)
+    )(arrived, below, above, window)
     surfaces = exchange(surface)
     ocean_end, values = pl.pallas_call(
         last_kernel,
@@ -303,11 +316,12 @@
         in_specs=[SMEM] * 2 + [VMEM] * 4,
         scratch_shapes=scratch,
     )(owner, tile_target, surfaces, window, lists, forcing)
+    ocean_end = to_idle(ocean_end)
     returned = exchange(values).reshape(TILES, LANES)
     pulled = jnp.sum(returned[:, None, :] * tile_weight.astype(F32), axis=2)
     source_hot = (tile_source[:, None] == jnp.arange(16, dtype=I32)[None, :]).astype(F32)
     atm_back = jnp.einsum("ra,rb->ab", source_hot, pulled, precision=HIGHEST).reshape(-1)
-    return (ocean_end.reshape(-1), atm_back)
+    return (ocean_end.reshape(-1), to_idle(atm_back))
 
 
 def solution(mesh):

time: 116 us -> 127 us (1.095)
  starting transfers between devices: 23.3 us -> 54.5 us
  blocking collectives: 27.3 us -> 11.9 us
  waiting for transfers between devices: 34.2 us -> 27.3 us
    all_to_all x1 -> x3, starting transfers between devices: 9.05 us -> 27.7 us  [exchange(): lax.all_to_all(blocks, BOTH, split_axis=0, concat_axis=0, tiled=True, axi...]
    ppermute x4 -> x6, waiting for transfers between devices: 28.8 us -> 10.8 us  [from_owner(): return lax.ppermute(block, BOTH, route)]
    ppermute x4 -> x6, starting transfers between devices: 8.35 us -> 24.3 us  [from_owner(): return lax.ppermute(block, BOTH, route)]
    all_to_all x1 -> x3, waiting for transfers between devices: 0.01 us -> 15.8 us  [exchange(): lax.all_to_all(blocks, BOTH, split_axis=0, concat_axis=0, tiled=True, axi...]
    all_to_all x2 -> x1, blocking collectives: 27.3 us -> 11.9 us  [local(): lax.all_to_all(partials, 'comp', split_axis=0, concat_axis=0, tiled=True)]
    all_to_all x1 -> x0, starting transfers between devices: 5.9 us -> none  [local(): lax.all_to_all(partials, 'comp', split_axis=0, concat_axis=0, tiled=True)]
    all_to_all x1 -> x0, waiting for transfers between devices: 5.38 us -> none  [local(): lax.all_to_all(partials, 'comp', split_axis=0, concat_axis=0, tiled=True)]
    ppermute x0 -> x2, starting transfers between devices: none -> 2.58 us  [to_idle(): lax.ppermute(block, BOTH, route)]
  transfers between devices with their start and end apart: 6 -> 11, of which waited for: 2 -> 6; matrix products, arithmetic and copies ran while one was open for 0% -> 2% of each run, Pallas kernels for 3% -> 3%
where the time goes in v5:
time: 127 us; the launch traced here: 125 us
  starting transfers between devices  54.5 us (43%)
  waiting for transfers between devices  27.3 us (21%)
  Pallas kernels  25.2 us (20%)
  blocking collectives  11.9 us (9%)
  local copies, waits for them, and re-layouts  2.79 us (2%)
  other arithmetic  2.38 us (2%)
    all_to_all x3, starting transfers between devices, exchange(): lax.all_to_all(blocks, BOTH, split_axis=0, concat_axis=0, tiled=True, axi...  27.7 us
    ppermute x6, starting transfers between devices, from_owner(): return lax.ppermute(block, BOTH, route)  24.3 us
    all_to_all x3, waiting for transfers between devices, exchange(): lax.all_to_all(blocks, BOTH, split_axis=0, concat_axis=0, tiled=True, axi...  15.8 us
    all_to_all x1, blocking collectives, local(): lax.all_to_all(partials, 'comp', split_axis=0, concat_axis=0, tiled=True)  11.9 us
    ppermute x6, waiting for transfers between devices, from_owner(): return lax.ppermute(block, BOTH, route)  10.8 us
    pallas_call x1, Pallas kernels, local(): pl.pallas_call(first_kernel, out_shape=(shape(OWNERS, 16, LANES), shape(S...  10.3 us
    pallas_call x1, Pallas kernels, local(): pl.pallas_call(last_kernel, out_shape=(shape(16, LANES), shape(OWNERS, 2,...  9.96 us
    pallas_call x1, Pallas kernels, local(): pl.pallas_call(terms_kernel, out_shape=shape(OWNERS, SENT, LANES), in_spe...  3.15 us
  transfers between devices with their start and end apart: 11, of which 6 were waited for; matrix products, arithmetic and copies ran while one was open for 2% of the time, Pallas kernels for 3%

profile of v5, /device:TPU:2, one launch (start us, length us, event | category | flops | bytes accessed | tf_op | source)
XLA Modules:
  0.0 125.2 jit_solution(11672026844055824878)
XLA Ops:
  0.6 1.7 %shard_map.113 = (f32[8,16,128]{2,1,0:T(8,128)}, f32[232,128]{1,0:T(8,128)}) custom-call(f32[9]{0:T(128)} %weight_ref.2, bf16[9,2048]{1,0:T(8,128)(2,1)} %flux_ref.1, s32[6,2048]{1,0:T(8,128)} %neighbor_ref.1, f32[6,2048]{1,0:T(8,128)} %conduct_ref.1, f32[16,128]{1,0:T(8,128)} %bitcast.14, f32[16,128]{1,0:T(8,128)} %bitcast.15, s32[2,256]{1,0:T(2,128)} %lists_ref.1, ...), custom_call_target="tpu_custom_call" | custom-call | tf_op jit(solution)/shard_map/pallas_call | solution.py:274
  2.4 3.4 %collective-permute-start.2 = (f32[232,128]{1,0:T(8,128)}, f32[232,128]{1,0:T(8,128)S(1)}, u32[]{:S(2)}, u32[]{:S(2)}) collective-permute-start(f32[232,128]{1,0:T(8,128)} %get-tuple-element.10), channel_id=1, source_target_pairs={{223,0},{0,1},{1,2},{2,3},{3,4},{4,5},{5,6},{6,7},{7,8},{8,9},{9,1... | collective-permute-start | bytes 356360 | tf_op jit(solution)/shard_map/near/ppermute | solution.py:47
  5.8 2.7 %collective-permute-start.3 = (f32[232,128]{1,0:T(8,128)}, f32[232,128]{1,0:T(8,128)S(1)}, u32[]{:S(2)}, u32[]{:S(2)}) collective-permute-start(f32[232,128]{1,0:T(8,128)} %get-tuple-element.10), channel_id=1, source_target_pairs={{1,0},{2,1},{3,2},{4,3},{5,4},{6,5},{7,6},{8,7},{9,8},{10,9},{11,1... | collective-permute-start | bytes 356360 | tf_op jit(solution)/shard_map/near/ppermute | solution.py:47
  8.4 1.1 collective-permute-done.2
  9.5 0.9 constant_dynamic-update-slice_fusion.1
  10.4 2.3 %collective-permute-done.3 = f32[232,128]{1,0:T(8,128)S(1)} collective-permute-done((f32[232,128]{1,0:T(8,128)}, f32[232,128]{1,0:T(8,128)S(1)}, u32[]{:S(2)}, u32[]{:S(2)}) %collective-permute-start.3) | collective-permute-done | bytes 118816 | tf_op jit(solution)/shard_map/near/ppermute | solution.py:47
  12.7 3.8 %collective-permute-start.4 = (f32[696,128]{1,0:T(8,128)S(1)}, f32[696,128]{1,0:T(8,128)S(1)}, u32[]{:S(2)}, u32[]{:S(2)}) collective-permute-start(f32[696,128]{1,0:T(8,128)S(1)} %constant_dynamic-update-slice_fusion), channel_id=1, source_target_pairs={{221,0},{222,1},{223,2},{0,3},{1,4},{2,5},{3,6},{4,7},{5,8},{6,9},... | collective-permute-start | bytes 1069064 | tf_op jit(solution)/shard_map/far/ppermute | solution.py:47
  16.5 11.9 %all_to_all.20.shares_ref = f32[8,16,128]{2,1,0:T(8,128)} all-to-all(f32[8,16,128]{2,1,0:T(8,128)} %get-tuple-element.9), channel_id=1, replica_groups=mesh['comp'=8,'cells'=32] {'comp'}, dimensions={0} | all-to-all | bytes 131072 | tf_op jit(solution)/shard_map/levels/all_to_all | solution.py:290
  28.4 3.2 %shard_map.114 = f32[32,24,128]{2,1,0:T(8,128)} custom-call(s32[64]{0:T(128)} %source_ref.1, f32[8,16,128]{2,1,0:T(8,128)} %all_to_all.20.shares_ref, bf16[64,128,128]{2,1,0:T(8,128)(2,1)} %weight_ref.3), custom_call_target="tpu_custom_call" | custom-call | tf_op jit(solution)/shard_map/pallas_call | solution.py:294
  31.6 13.3 %all-to-all-start.1 = ((f32[32,24,128]{2,1,0:T(8,128)}), f32[32,24,128]{2,1,0:T(8,128)S(1)}, u32[]{:S(2)}, u32[]{:S(2)}) async-start(f32[32,24,128]{2,1,0:T(8,128)} %shard_map.114), calls=%async_computation.1 | async-start | bytes 786432 | tf_op jit(solution)/shard_map/send/all_to_all | solution.py:62
  44.9 4.3 %collective-permute-start = (f32[24,128]{1,0:T(8,128)S(1)}, f32[24,128]{1,0:T(8,128)S(1)}, u32[]{:S(2)}, u32[]{:S(2)}) collective-permute-start(f32[24,128]{1,0:T(8,128)S(1)} %slice.3), channel_id=1, source_target_pairs={{219,0},{220,1},{221,2},{222,3},{223,4},{0,5},{1,6},{2,7},{3,8},{4... | collective-permute-start | bytes 36872 | tf_op jit(solution)/shard_map/far/ppermute | solution.py:47
  49.2 5.8 %collective-permute-start.1 = (f32[24,128]{1,0:T(8,128)S(1)}, f32[24,128]{1,0:T(8,128)S(1)}, u32[]{:S(2)}, u32[]{:S(2)}) collective-permute-start(f32[24,128]{1,0:T(8,128)S(1)} %slice.3), channel_id=1, source_target_pairs={{5,0},{6,1},{7,2},{8,3},{9,4},{10,5},{11,6},{12,7},{13,8},{14,9},{... | collective-permute-start | bytes 36872 | tf_op jit(solution)/shard_map/far/ppermute | solution.py:47
  54.9 4.4 %collective-permute-start.5 = (f32[696,128]{1,0:T(8,128)S(1)}, f32[696,128]{1,0:T(8,128)S(1)}, u32[]{:S(2)}, u32[]{:S(2)}) collective-permute-start(f32[696,128]{1,0:T(8,128)S(1)} %constant_dynamic-update-slice_fusion), channel_id=1, source_target_pairs={{3,0},{4,1},{5,2},{6,3},{7,4},{8,5},{9,6},{10,7},{11,8},{12,9},{13... | collective-permute-start | bytes 1069064 | tf_op jit(solution)/shard_map/far/ppermute | solution.py:47
  59.4 7.4 %collective-permute-done.5 = f32[696,128]{1,0:T(8,128)S(1)} collective-permute-done((f32[696,128]{1,0:T(8,128)S(1)}, f32[696,128]{1,0:T(8,128)S(1)}, u32[]{:S(2)}, u32[]{:S(2)}) %collective-permute-start.5) | collective-permute-done | bytes 356384 | tf_op jit(solution)/shard_map/far/ppermute | solution.py:47
  66.9 0.0 collective-permute-done.below_ref
  66.9 0.9 copy-done.1
  67.9 0.0 copy-done.6
  67.9 0.1 copy-done.2
  68.0 10.3 %shard_map.115 = (f32[32,16,128]{2,1,0:T(8,128)}, f32[13,8,128]{2,1,0:T(8,128)}, f32[9,16,128]{2,1,0:T(8,128)}) custom-call(f32[32,24,128]{2,1,0:T(8,128)} %copy-done.2, f32[24,128]{1,0:T(8,128)} %copy-done.5, f32[24,128]{1,0:T(8,128)} %copy-done.6, f32[9,232,128]{2,1,0:T(8,128)} %bitcast.11), custom_call_target="tpu_custom_call" | custom-call | tf_op jit(solution)/shard_map/pallas_call | solution.py:307
  78.3 9.1 %all-to-all-start.2 = ((f32[32,16,128]{2,1,0:T(8,128)}), f32[32,16,128]{2,1,0:T(8,128)S(1)}, u32[]{:S(2)}, u32[]{:S(2)}) async-start(f32[32,16,128]{2,1,0:T(8,128)} %get-tuple-element.11), calls=%async_computation.2 | async-start | bytes 524288 | tf_op jit(solution)/shard_map/all_to_all | solution.py:62
  87.4 8.8 %all-to-all-done.2.surfaces_ref = f32[32,16,128]{2,1,0:T(8,128)S(1)} async-done(((f32[32,16,128]{2,1,0:T(8,128)}), f32[32,16,128]{2,1,0:T(8,128)S(1)}, u32[]{:S(2)}, u32[]{:S(2)}) %all-to-all-start.2) | async-done | bytes 262176 | tf_op jit(solution)/shard_map/all_to_all | solution.py:62
  96.2 0.7 copy-done.3
  96.9 10.0 %shard_map.116 = (f32[16,128]{1,0:T(8,128)}, f32[32,2,128]{2,1,0:T(2,128)}) custom-call(s32[1]{0:T(128)} %bitcast.owner_ref, s32[64]{0:T(128)} %target_ref.1, f32[32,16,128]{2,1,0:T(8,128)} %copy-done.3, f32[9,232,128]{2,1,0:T(8,128)} %bitcast.12, f32[13,8,128]{2,1,0:T(8,128)} %get-tuple-element.12.lists_ref, f32[9,16,128]{2,1,0:T(8,128)} %get-tuple-element.13.forcing_ref), custom_call_target="tpu_custom_call" | custom-call | tf_op jit(solution)/shard_map/pallas_call | solution.py:313
  106.9 5.3 %all-to-all-start.3 = ((f32[32,2,128]{2,1,0:T(2,128)}), f32[32,2,128]{2,1,0:T(2,128)S(1)}, u32[]{:S(2)}, u32[]{:S(2)}) async-start(f32[32,2,128]{2,1,0:T(2,128)} %get-tuple-element.15), calls=%async_computation.3 | async-start | bytes 65536 | tf_op jit(solution)/shard_map/all_to_all | solution.py:62
  112.2 1.3 %collective-permute-start.6 = (f32[16,128]{1,0:T(8,128)}, f32[16,128]{1,0:T(8,128)S(1)}, u32[]{:S(2)}, u32[]{:S(2)}) collective-permute-start(f32[16,128]{1,0:T(8,128)} %get-tuple-element.14), channel_id=1, source_target_pairs={{0,64},{1,65},{2,66},{3,67},{4,68},{5,69},{6,70},{7,71},{8,72},{9,... | collective-permute-start | bytes 24584 | tf_op jit(solution)/shard_map/ppermute | solution.py:58
  113.5 7.0 %all-to-all-done.3 = f32[32,2,128]{2,1,0:T(2,128)S(1)} async-done(((f32[32,2,128]{2,1,0:T(2,128)}), f32[32,2,128]{2,1,0:T(2,128)S(1)}, u32[]{:S(2)}, u32[]{:S(2)}) %all-to-all-start.3) | async-done | bytes 32800 | tf_op jit(solution)/shard_map/all_to_all | solution.py:62
  120.5 1.2 multiply_reduce_fusion
  121.7 0.3 convolution_bitcast_fusion
  122.0 1.3 %collective-permute-start.7 = (f32[2048]{0:T(1024)S(1)}, f32[2048]{0:T(1024)S(1)}, u32[]{:S(2)}, u32[]{:S(2)}) collective-permute-start(f32[2048]{0:T(1024)S(1)} %convolution_bitcast_fusion), channel_id=1, source_target_pairs={{0,64},{1,65},{2,66},{3,67},{4,68},{5,69},{6,70},{7,71},{8,72},{9,... | collective-permute-start | bytes 24584 | tf_op jit(solution)/shard_map/ppermute | solution.py:58
  123.3 0.6 select_bitcast_fusion
  123.9 0.7 collective-permute-done.7
  124.6 0.6 broadcast_select_fusion
  (26 shorter events, 0.1 us)
Async XLA Ops:
  2.4 7.2 %collective-permute-start.2 = (f32[232,128]{1,0:T(8,128)}, f32[232,128]{1,0:T(8,128)S(1)}, u32[]{:S(2)}, u32[]{:S(2)}) collective-permute-start(f32[232,128]{1,0:T(8,128)} %get-tuple-element.10), channel_id=1, source_target_pairs={{223,0},{0,1},{1,2},{2,3},{3,4},{4,5},{5,6},{6,7},{7,8},{8,9},{9,1... | collective-permute-start | bytes 356360 | tf_op jit(solution)/shard_map/near/ppermute | solution.py:47
  5.8 6.9 %collective-permute-start.3 = (f32[232,128]{1,0:T(8,128)}, f32[232,128]{1,0:T(8,128)S(1)}, u32[]{:S(2)}, u32[]{:S(2)}) collective-permute-start(f32[232,128]{1,0:T(8,128)} %get-tuple-element.10), channel_id=1, source_target_pairs={{1,0},{2,1},{3,2},{4,3},{5,4},{6,5},{7,6},{8,7},{9,8},{10,9},{11,1... | collective-permute-start | bytes 356360 | tf_op jit(solution)/shard_map/near/ppermute | solution.py:47
  12.7 46.6 %collective-permute-start.4 = (f32[696,128]{1,0:T(8,128)S(1)}, f32[696,128]{1,0:T(8,128)S(1)}, u32[]{:S(2)}, u32[]{:S(2)}) collective-permute-start(f32[696,128]{1,0:T(8,128)S(1)} %constant_dynamic-update-slice_fusion), channel_id=1, source_target_pairs={{221,0},{222,1},{223,2},{0,3},{1,4},{2,5},{3,6},{4,7},{5,8},{6,9},... | collective-permute-start | bytes 1069064 | tf_op jit(solution)/shard_map/far/ppermute | solution.py:47
  28.4 16.4 %copy-start.4 = (f32[232,128]{1,0:T(8,128)S(1)}, f32[232,128]{1,0:T(8,128)}, u32[]{:S(2)}) copy-start(f32[232,128]{1,0:T(8,128)} %get-tuple-element.10) | copy-start | bytes 356356
  31.6 35.3 %all-to-all-start.1 = ((f32[32,24,128]{2,1,0:T(8,128)}), f32[32,24,128]{2,1,0:T(8,128)S(1)}, u32[]{:S(2)}, u32[]{:S(2)}) async-start(f32[32,24,128]{2,1,0:T(8,128)} %shard_map.114), calls=%async_computation.1 | async-start | bytes 786432 | tf_op jit(solution)/shard_map/send/all_to_all | solution.py:62
  44.9 22.0 %collective-permute-start = (f32[24,128]{1,0:T(8,128)S(1)}, f32[24,128]{1,0:T(8,128)S(1)}, u32[]{:S(2)}, u32[]{:S(2)}) collective-permute-start(f32[24,128]{1,0:T(8,128)S(1)} %slice.3), channel_id=1, source_target_pairs={{219,0},{220,1},{221,2},{222,3},{223,4},{0,5},{1,6},{2,7},{3,8},{4... | collective-permute-start | bytes 36872 | tf_op jit(solution)/shard_map/far/ppermute | solution.py:47
  49.2 17.7 %collective-permute-start.1 = (f32[24,128]{1,0:T(8,128)S(1)}, f32[24,128]{1,0:T(8,128)S(1)}, u32[]{:S(2)}, u32[]{:S(2)}) collective-permute-start(f32[24,128]{1,0:T(8,128)S(1)} %slice.3), channel_id=1, source_target_pairs={{5,0},{6,1},{7,2},{8,3},{9,4},{10,5},{11,6},{12,7},{13,8},{14,9},{... | collective-permute-start | bytes 36872 | tf_op jit(solution)/shard_map/far/ppermute | solution.py:47
  54.9 11.9 %collective-permute-start.5 = (f32[696,128]{1,0:T(8,128)S(1)}, f32[696,128]{1,0:T(8,128)S(1)}, u32[]{:S(2)}, u32[]{:S(2)}) collective-permute-start(f32[696,128]{1,0:T(8,128)S(1)} %constant_dynamic-update-slice_fusion), channel_id=1, source_target_pairs={{3,0},{4,1},{5,2},{6,3},{7,4},{8,5},{9,6},{10,7},{11,8},{12,9},{13... | collective-permute-start | bytes 1069064 | tf_op jit(solution)/shard_map/far/ppermute | solution.py:47
  66.9 1.0 copy-start.1
  66.9 1.0 copy-start.5
  66.9 1.0 copy-start.6
  66.9 1.1 copy-start.2
  78.3 42.2 %copy-start = (bf16[64,128,128]{2,1,0:T(8,128)(2,1)S(1)}, bf16[64,128,128]{2,1,0:T(8,128)(2,1)}, u32[]{:S(2)}) copy-start(bf16[64,128,128]{2,1,0:T(8,128)(2,1)} %weight_ref.3) | copy-start | bytes 6291460
  78.3 17.9 %all-to-all-start.2 = ((f32[32,16,128]{2,1,0:T(8,128)}), f32[32,16,128]{2,1,0:T(8,128)S(1)}, u32[]{:S(2)}, u32[]{:S(2)}) async-start(f32[32,16,128]{2,1,0:T(8,128)} %get-tuple-element.11), calls=%async_computation.2 | async-start | bytes 524288 | tf_op jit(solution)/shard_map/all_to_all | solution.py:62
  96.2 0.7 copy-start.3
  106.9 13.6 %all-to-all-start.3 = ((f32[32,2,128]{2,1,0:T(2,128)}), f32[32,2,128]{2,1,0:T(2,128)S(1)}, u32[]{:S(2)}, u32[]{:S(2)}) async-start(f32[32,2,128]{2,1,0:T(2,128)} %get-tuple-element.15), calls=%async_computation.3 | async-start | bytes 65536 | tf_op jit(solution)/shard_map/all_to_all | solution.py:62
  112.2 11.0 %collective-permute-start.6 = (f32[16,128]{1,0:T(8,128)}, f32[16,128]{1,0:T(8,128)S(1)}, u32[]{:S(2)}, u32[]{:S(2)}) collective-permute-start(f32[16,128]{1,0:T(8,128)} %get-tuple-element.14), channel_id=1, source_target_pairs={{0,64},{1,65},{2,66},{3,67},{4,68},{5,69},{6,70},{7,71},{8,72},{9,... | collective-permute-start | bytes 24584 | tf_op jit(solution)/shard_map/ppermute | solution.py:58
  120.5 1.2 copy-start.8
  120.5 2.8 %copy-start.7 = (f32[16,128]{1,0:T(8,128)S(1)}, f32[16,128]{1,0:T(8,128)}, u32[]{:S(2)}) copy-start(f32[16,128]{1,0:T(8,128)} %get-tuple-element.14) | copy-start | bytes 24580
  122.0 2.6 %collective-permute-start.7 = (f32[2048]{0:T(1024)S(1)}, f32[2048]{0:T(1024)S(1)}, u32[]{:S(2)}, u32[]{:S(2)}) collective-permute-start(f32[2048]{0:T(1024)S(1)} %convolution_bitcast_fusion), channel_id=1, source_target_pairs={{0,64},{1,65},{2,66},{3,67},{4,68},{5,69},{6,70},{7,71},{8,72},{9,... | collective-permute-start | bytes 24584 | tf_op jit(solution)/shard_map/ppermute | solution.py:58

commit v6 on v4

--- a/solution.py
+++ b/solution.py
@@ -30,8 +30,13 @@
     return (2 * z_low + core) * OWNERS + owner
 
 
-COPIES = [(copy, core) for copy in range(4) for core in range(2)]
-ALL = [[device_of(owner, *copy) for owner in range(OWNERS)] for copy in COPIES]
+COPIES = [(copy, core) for copy in (0, 3) for core in range(2)]
+IDLE = [
+    [(2 * z_low + core) * OWNERS + half * HALF + i for core in range(2) for i in range(HALF)]
+    for z_low in (1, 2)
+    for half in range(2)
+]
+ALL = [[device_of(owner, *copy) for owner in range(OWNERS)] for copy in COPIES] + IDLE
 
 
 def from_owner(block, offset):
@@ -41,6 +46,17 @@
         for owner in range(OWNERS)
     ]
     return lax.ppermute(block, BOTH, route)
+
+
+def to_idle(block):
+    route = [
+        ((2 * here + core) * OWNERS + owner, (2 * there + core) * OWNERS + owner)
+        for here, there in ((0, 1), (3, 2))
+        for core in range(2)
+        for owner in range(OWNERS)
+    ]
+    z_low = lax.axis_index("comp") // 2
+    return jnp.where((z_low == 0) | (z_low == 3), block, lax.ppermute(block, BOTH, route))
 
 
 def exchange(blocks):
@@ -303,11 +319,12 @@
         in_specs=[SMEM] * 2 + [VMEM] * 4,
         scratch_shapes=scratch,
     )(owner, tile_target, surfaces, window, lists, forcing)
+    ocean_end = to_idle(ocean_end)
     returned = exchange(values).reshape(TILES, LANES)
     pulled = jnp.sum(returned[:, None, :] * tile_weight.astype(F32), axis=2)
     source_hot = (tile_source[:, None] == jnp.arange(16, dtype=I32)[None, :]).astype(F32)
     atm_back = jnp.einsum("ra,rb->ab", source_hot, pulled, precision=HIGHEST).reshape(-1)
-    return (ocean_end.reshape(-1), atm_back)
+    return (ocean_end.reshape(-1), to_idle(atm_back))
 
 
 def solution(mesh):

time: 116 us -> 109 us (0.940); the launches traced: 115 us -> 107 us
  starting transfers between devices: 23.3 us -> 38.8 us
  waiting for transfers between devices: 34.2 us -> 21.6 us
  blocking collectives: 27.3 us -> 15.4 us
  other arithmetic: 1.18 us -> 2.38 us
    ppermute x4, waiting for transfers between devices: 28.8 us -> 10.4 us  [from_owner(): return lax.ppermute(block, BOTH, route)]
    all_to_all x2 -> x1, blocking collectives: 27.3 us -> 15.4 us  [exchange(): lax.all_to_all(blocks, BOTH, split_axis=0, concat_axis=0, tiled=True, axi...]
    ppermute x4, starting transfers between devices: 8.35 us -> 15.9 us  [from_owner(): return lax.ppermute(block, BOTH, route)]
    all_to_all x1 -> x2, waiting for transfers between devices: 0.01 us -> 6.99 us  [exchange(): lax.all_to_all(blocks, BOTH, split_axis=0, concat_axis=0, tiled=True, axi...]
    all_to_all x1 -> x2, starting transfers between devices: 9.05 us -> 14.4 us  [exchange(): lax.all_to_all(blocks, BOTH, split_axis=0, concat_axis=0, tiled=True, axi...]
    ppermute x0 -> x2, starting transfers between devices: none -> 2.58 us  [to_idle(): lax.ppermute(block, BOTH, route)]
    all_to_all x1, waiting for transfers between devices: 5.38 us -> 3.48 us  [local(): lax.all_to_all(partials, 'comp', split_axis=0, concat_axis=0, tiled=True)]
  transfers between devices with their start and end apart: 6 -> 9, of which waited for: 2 -> 4; matrix products, arithmetic and copies ran while one was open for 0% -> 2% of each run, Pallas kernels for 3% -> 3%
where the time goes in v6:
time: 109 us; the launch traced here: 107 us
  starting transfers between devices  38.8 us (36%)
  Pallas kernels  25.4 us (23%)
  waiting for transfers between devices  21.6 us (20%)
  blocking collectives  15.4 us (14%)
  other arithmetic  2.38 us (2%)
  local copies, waits for them, and re-layouts  1.95 us (2%)
    ppermute x4, starting transfers between devices, from_owner(): return lax.ppermute(block, BOTH, route)  15.9 us
    all_to_all x1, blocking collectives, exchange(): lax.all_to_all(blocks, BOTH, split_axis=0, concat_axis=0, tiled=True, axi...  15.4 us
    all_to_all x2, starting transfers between devices, exchange(): lax.all_to_all(blocks, BOTH, split_axis=0, concat_axis=0, tiled=True, axi...  14.4 us
    pallas_call x1, Pallas kernels, local(): pl.pallas_call(first_kernel, out_shape=(shape(OWNERS, 16, LANES), shape(S...  10.4 us
    ppermute x4, waiting for transfers between devices, from_owner(): return lax.ppermute(block, BOTH, route)  10.4 us
    pallas_call x1, Pallas kernels, local(): pl.pallas_call(last_kernel, out_shape=(shape(16, LANES), shape(OWNERS, 2,...  9.96 us
    all_to_all x2, waiting for transfers between devices, exchange(): lax.all_to_all(blocks, BOTH, split_axis=0, concat_axis=0, tiled=True, axi...  6.99 us
    all_to_all x1, starting transfers between devices, local(): lax.all_to_all(partials, 'comp', split_axis=0, concat_axis=0, tiled=True)  5.91 us
  transfers between devices with their start and end apart: 9, of which 4 were waited for; matrix products, arithmetic and copies ran while one was open for 2% of the time, Pallas kernels for 3%

profile of v6, /device:TPU:2, one launch (start us, length us, event | category | flops | bytes accessed | tf_op | source)
XLA Modules:
  0.0 106.6 jit_solution(1565819918169866534)
XLA Ops:
  0.6 1.7 %shard_map.113 = (f32[8,16,128]{2,1,0:T(8,128)}, f32[232,128]{1,0:T(8,128)}) custom-call(f32[9]{0:T(128)} %weight_ref.2, bf16[9,2048]{1,0:T(8,128)(2,1)} %flux_ref.1, s32[6,2048]{1,0:T(8,128)} %neighbor_ref.1, f32[6,2048]{1,0:T(8,128)} %conduct_ref.1, f32[16,128]{1,0:T(8,128)} %bitcast.14, f32[16,128]{1,0:T(8,128)} %bitcast.15, s32[2,256]{1,0:T(2,128)} %lists_ref.1, ...), custom_call_target="tpu_custom_call" | custom-call | tf_op jit(solution)/shard_map/pallas_call | solution.py:278
  2.4 3.4 %collective-permute-start = (f32[232,128]{1,0:T(8,128)}, f32[232,128]{1,0:T(8,128)S(1)}, u32[]{:S(2)}, u32[]{:S(2)}) collective-permute-start(f32[232,128]{1,0:T(8,128)} %get-tuple-element.10.packed_ref), channel_id=1, source_target_pairs={{223,0},{0,1},{1,2},{2,3},{3,4},{4,5},{5,6},{6,7},{7,8},{8,9},{9,1... | collective-permute-start | bytes 356360 | tf_op jit(solution)/shard_map/near/ppermute | solution.py:48
  5.8 5.9 %all-to-all-start = ((f32[8,16,128]{2,1,0:T(8,128)}), f32[8,16,128]{2,1,0:T(8,128)S(1)}, u32[]{:S(2)}, u32[]{:S(2)}) async-start(f32[8,16,128]{2,1,0:T(8,128)} %get-tuple-element.9), calls=%async_computation | async-start | bytes 131072 | tf_op jit(solution)/shard_map/levels/all_to_all | solution.py:294
  11.7 2.4 %collective-permute-start.1 = (f32[232,128]{1,0:T(8,128)}, f32[232,128]{1,0:T(8,128)S(1)}, u32[]{:S(2)}, u32[]{:S(2)}) collective-permute-start(f32[232,128]{1,0:T(8,128)} %get-tuple-element.10.packed_ref), channel_id=1, source_target_pairs={{1,0},{2,1},{3,2},{4,3},{5,4},{6,5},{7,6},{8,7},{9,8},{10,9},{11,1... | collective-permute-start | bytes 356360 | tf_op jit(solution)/shard_map/near/ppermute | solution.py:48
  14.1 3.5 %all-to-all-done.shares_ref = f32[8,16,128]{2,1,0:T(8,128)S(1)} async-done(((f32[8,16,128]{2,1,0:T(8,128)}), f32[8,16,128]{2,1,0:T(8,128)S(1)}, u32[]{:S(2)}, u32[]{:S(2)}) %all-to-all-start) | async-done | bytes 65568 | tf_op jit(solution)/shard_map/levels/all_to_all | solution.py:294
  17.6 0.6 copy-done.4
  18.2 3.3 %shard_map.114 = f32[32,40,128]{2,1,0:T(8,128)} custom-call(s32[64]{0:T(128)} %source_ref.1, f32[8,16,128]{2,1,0:T(8,128)} %copy-done.4, f32[232,128]{1,0:T(8,128)} %get-tuple-element.10.packed_ref, bf16[64,128,128]{2,1,0:T(8,128)(2,1)} %weight_ref.3), custom_call_target="tpu_custom_call" | custom-call | tf_op jit(solution)/shard_map/pallas_call | solution.py:298
  21.5 9.1 %all-to-all-start.1 = ((f32[32,40,128]{2,1,0:T(8,128)}), f32[32,40,128]{2,1,0:T(8,128)S(1)}, u32[]{:S(2)}, u32[]{:S(2)}) async-start(f32[32,40,128]{2,1,0:T(8,128)} %shard_map.114), calls=%async_computation.1 | async-start | bytes 1310720 | tf_op jit(solution)/shard_map/send/all_to_all | solution.py:63
  30.6 0.0 collective-permute-done
  30.6 0.0 copy-done.3
  30.6 0.0 collective-permute-done.1
  30.7 3.4 %collective-permute-start.2 = (f32[696,128]{1,0:T(8,128)S(1)}, f32[696,128]{1,0:T(8,128)S(1)}, u32[]{:S(2)}, u32[]{:S(2)}) collective-permute-start(f32[696,128]{1,0:T(8,128)S(1)} %constant_dynamic-update-slice_fusion), channel_id=1, source_target_pairs={{221,0},{222,1},{223,2},{0,3},{1,4},{2,5},{3,6},{4,7},{5,8},{6,9},... | collective-permute-start | bytes 1069064 | tf_op jit(solution)/shard_map/far/ppermute | solution.py:48
  34.1 6.7 %collective-permute-start.3 = (f32[696,128]{1,0:T(8,128)S(1)}, f32[696,128]{1,0:T(8,128)S(1)}, u32[]{:S(2)}, u32[]{:S(2)}) collective-permute-start(f32[696,128]{1,0:T(8,128)S(1)} %constant_dynamic-update-slice_fusion), channel_id=1, source_target_pairs={{3,0},{4,1},{5,2},{6,3},{7,4},{8,5},{9,6},{10,7},{11,8},{12,9},{13... | collective-permute-start | bytes 1069064 | tf_op jit(solution)/shard_map/far/ppermute | solution.py:48
  40.8 10.4 %collective-permute-done.2 = f32[696,128]{1,0:T(8,128)S(1)} collective-permute-done((f32[696,128]{1,0:T(8,128)S(1)}, f32[696,128]{1,0:T(8,128)S(1)}, u32[]{:S(2)}, u32[]{:S(2)}) %collective-permute-start.2) | collective-permute-done | bytes 356384 | tf_op jit(solution)/shard_map/far/ppermute | solution.py:48
  51.2 0.0 collective-permute-done.3
  51.3 0.0 all-to-all-done.1.arrived_ref
  51.3 0.0 copy-start.2
  51.3 1.0 copy-done.1
  52.3 0.2 copy-done.2
  52.5 10.4 %shard_map.115 = (f32[32,16,128]{2,1,0:T(8,128)}, f32[13,8,128]{2,1,0:T(8,128)}, f32[9,16,128]{2,1,0:T(8,128)}) custom-call(s32[1]{0:T(128)} %bitcast.owner_ref, f32[32,40,128]{2,1,0:T(8,128)} %copy-done.2, f32[9,232,128]{2,1,0:T(8,128)} %bitcast.11), custom_call_target="tpu_custom_call" | custom-call | tf_op jit(solution)/shard_map/pallas_call | solution.py:309
  62.9 15.4 %all_to_all.20.surfaces_ref = f32[32,16,128]{2,1,0:T(8,128)} all-to-all(f32[32,16,128]{2,1,0:T(8,128)} %get-tuple-element.11), channel_id=1, replica_groups={{0,1,2,3,4,5,6,7,8,9,10,11,12,13,14,15,208,209,210,211,212,213,214,215,..., dimensions={0} | all-to-all | bytes 524288 | tf_op jit(solution)/shard_map/all_to_all | solution.py:63
  78.3 10.0 %shard_map.116 = (f32[16,128]{1,0:T(8,128)}, f32[32,2,128]{2,1,0:T(2,128)}) custom-call(s32[1]{0:T(128)} %bitcast.owner_ref, s32[64]{0:T(128)} %target_ref.1, f32[32,16,128]{2,1,0:T(8,128)} %all_to_all.20.surfaces_ref, f32[9,232,128]{2,1,0:T(8,128)} %bitcast.12, f32[13,8,128]{2,1,0:T(8,128)} %get-tuple-element.12.lists_ref, ...), custom_call_target="tpu_custom_call" | custom-call | tf_op jit(solution)/shard_map/pallas_call | solution.py:316
  88.3 5.3 %all-to-all-start.3 = ((f32[32,2,128]{2,1,0:T(2,128)}), f32[32,2,128]{2,1,0:T(2,128)S(1)}, u32[]{:S(2)}, u32[]{:S(2)}) async-start(f32[32,2,128]{2,1,0:T(2,128)} %get-tuple-element.15), calls=%async_computation.3 | async-start | bytes 65536 | tf_op jit(solution)/shard_map/all_to_all | solution.py:63
  93.6 1.3 %collective-permute-start.4 = (f32[16,128]{1,0:T(8,128)}, f32[16,128]{1,0:T(8,128)S(1)}, u32[]{:S(2)}, u32[]{:S(2)}) collective-permute-start(f32[16,128]{1,0:T(8,128)} %get-tuple-element.14), channel_id=1, source_target_pairs={{0,64},{1,65},{2,66},{3,67},{4,68},{5,69},{6,70},{7,71},{8,72},{9,... | collective-permute-start | bytes 24584 | tf_op jit(solution)/shard_map/ppermute | solution.py:59
  94.9 7.0 %all-to-all-done.3 = f32[32,2,128]{2,1,0:T(2,128)S(1)} async-done(((f32[32,2,128]{2,1,0:T(2,128)}), f32[32,2,128]{2,1,0:T(2,128)S(1)}, u32[]{:S(2)}, u32[]{:S(2)}) %all-to-all-start.3) | async-done | bytes 32800 | tf_op jit(solution)/shard_map/all_to_all | solution.py:63
  101.9 1.2 %multiply_reduce_fusion = f32[64,128]{1,0:T(8,128)S(1)} fusion(bf16[64,128,128]{2,1,0:T(8,128)(2,1)S(1)} %copy-done, f32[64,128]{1,0:T(8,128)S(1)} %bitcast.13), kind=kLoop, calls=%fused_computation | loop fusion | flops 3137536 | bytes 2162688 | tf_op jit(solution)/shard_map/reduce_sum | solution.py:324
  103.1 0.3 convolution_bitcast_fusion
  103.4 1.3 %collective-permute-start.5 = (f32[2048]{0:T(1024)S(1)}, f32[2048]{0:T(1024)S(1)}, u32[]{:S(2)}, u32[]{:S(2)}) collective-permute-start(f32[2048]{0:T(1024)S(1)} %convolution_bitcast_fusion), channel_id=1, source_target_pairs={{0,64},{1,65},{2,66},{3,67},{4,68},{5,69},{6,70},{7,71},{8,72},{9,... | collective-permute-start | bytes 24584 | tf_op jit(solution)/shard_map/ppermute | solution.py:59
  104.7 0.0 collective-permute-done.4
  104.7 0.6 select_bitcast_fusion
  105.3 0.7 collective-permute-done.5
  106.0 0.6 broadcast_select_fusion
  (17 shorter events, 0.1 us)
Async XLA Ops:
  2.4 28.2 %collective-permute-start = (f32[232,128]{1,0:T(8,128)}, f32[232,128]{1,0:T(8,128)S(1)}, u32[]{:S(2)}, u32[]{:S(2)}) collective-permute-start(f32[232,128]{1,0:T(8,128)} %get-tuple-element.10.packed_ref), channel_id=1, source_target_pairs={{223,0},{0,1},{1,2},{2,3},{3,4},{4,5},{5,6},{6,7},{7,8},{8,9},{9,1... | collective-permute-start | bytes 356360 | tf_op jit(solution)/shard_map/near/ppermute | solution.py:48
  5.8 11.8 %all-to-all-start = ((f32[8,16,128]{2,1,0:T(8,128)}), f32[8,16,128]{2,1,0:T(8,128)S(1)}, u32[]{:S(2)}, u32[]{:S(2)}) async-start(f32[8,16,128]{2,1,0:T(8,128)} %get-tuple-element.9), calls=%async_computation | async-start | bytes 131072 | tf_op jit(solution)/shard_map/levels/all_to_all | solution.py:294
  11.7 19.0 %collective-permute-start.1 = (f32[232,128]{1,0:T(8,128)}, f32[232,128]{1,0:T(8,128)S(1)}, u32[]{:S(2)}, u32[]{:S(2)}) collective-permute-start(f32[232,128]{1,0:T(8,128)} %get-tuple-element.10.packed_ref), channel_id=1, source_target_pairs={{1,0},{2,1},{3,2},{4,3},{5,4},{6,5},{7,6},{8,7},{9,8},{10,9},{11,1... | collective-permute-start | bytes 356360 | tf_op jit(solution)/shard_map/near/ppermute | solution.py:48
  17.6 0.6 copy-start.4
  21.5 9.1 %copy-start.3 = (f32[232,128]{1,0:T(8,128)S(1)}, f32[232,128]{1,0:T(8,128)}, u32[]{:S(2)}) copy-start(f32[232,128]{1,0:T(8,128)} %get-tuple-element.10.packed_ref) | copy-start | bytes 356356
  21.5 29.7 %all-to-all-start.1 = ((f32[32,40,128]{2,1,0:T(8,128)}), f32[32,40,128]{2,1,0:T(8,128)S(1)}, u32[]{:S(2)}, u32[]{:S(2)}) async-start(f32[32,40,128]{2,1,0:T(8,128)} %shard_map.114), calls=%async_computation.1 | async-start | bytes 1310720 | tf_op jit(solution)/shard_map/send/all_to_all | solution.py:63
  30.7 20.5 %collective-permute-start.2 = (f32[696,128]{1,0:T(8,128)S(1)}, f32[696,128]{1,0:T(8,128)S(1)}, u32[]{:S(2)}, u32[]{:S(2)}) collective-permute-start(f32[696,128]{1,0:T(8,128)S(1)} %constant_dynamic-update-slice_fusion), channel_id=1, source_target_pairs={{221,0},{222,1},{223,2},{0,3},{1,4},{2,5},{3,6},{4,7},{5,8},{6,9},... | collective-permute-start | bytes 1069064 | tf_op jit(solution)/shard_map/far/ppermute | solution.py:48
  34.1 17.2 %collective-permute-start.3 = (f32[696,128]{1,0:T(8,128)S(1)}, f32[696,128]{1,0:T(8,128)S(1)}, u32[]{:S(2)}, u32[]{:S(2)}) collective-permute-start(f32[696,128]{1,0:T(8,128)S(1)} %constant_dynamic-update-slice_fusion), channel_id=1, source_target_pairs={{3,0},{4,1},{5,2},{6,3},{7,4},{8,5},{9,6},{10,7},{11,8},{12,9},{13... | collective-permute-start | bytes 1069064 | tf_op jit(solution)/shard_map/far/ppermute | solution.py:48
  51.3 1.0 copy-start.1
  51.3 1.2 %copy-start.2 = (f32[32,40,128]{2,1,0:T(8,128)}, f32[32,40,128]{2,1,0:T(8,128)S(1)}, u32[]{:S(2)}) copy-start(f32[32,40,128]{2,1,0:T(8,128)S(1)} %all-to-all-done.1.arrived_ref) | copy-start | bytes 1966084
  62.9 39.0 %copy-start = (bf16[64,128,128]{2,1,0:T(8,128)(2,1)S(1)}, bf16[64,128,128]{2,1,0:T(8,128)(2,1)}, u32[]{:S(2)}) copy-start(bf16[64,128,128]{2,1,0:T(8,128)(2,1)} %weight_ref.3) | copy-start | bytes 6291460
  88.3 13.6 %all-to-all-start.3 = ((f32[32,2,128]{2,1,0:T(2,128)}), f32[32,2,128]{2,1,0:T(2,128)S(1)}, u32[]{:S(2)}, u32[]{:S(2)}) async-start(f32[32,2,128]{2,1,0:T(2,128)} %get-tuple-element.15), calls=%async_computation.3 | async-start | bytes 65536 | tf_op jit(solution)/shard_map/all_to_all | solution.py:63
  93.6 11.0 %collective-permute-start.4 = (f32[16,128]{1,0:T(8,128)}, f32[16,128]{1,0:T(8,128)S(1)}, u32[]{:S(2)}, u32[]{:S(2)}) collective-permute-start(f32[16,128]{1,0:T(8,128)} %get-tuple-element.14), channel_id=1, source_target_pairs={{0,64},{1,65},{2,66},{3,67},{4,68},{5,69},{6,70},{7,71},{8,72},{9,... | collective-permute-start | bytes 24584 | tf_op jit(solution)/shard_map/ppermute | solution.py:59
  101.9 1.2 %copy-start.6 = (s32[64]{0:T(128)S(1)}, s32[64]{0:T(128)}, u32[]{:S(2)}) copy-start(s32[64]{0:T(128)} %source_ref.1) | copy-start | bytes 772
  101.9 2.8 %copy-start.5 = (f32[16,128]{1,0:T(8,128)S(1)}, f32[16,128]{1,0:T(8,128)}, u32[]{:S(2)}) copy-start(f32[16,128]{1,0:T(8,128)} %get-tuple-element.14) | copy-start | bytes 24580
  103.4 2.6 %collective-permute-start.5 = (f32[2048]{0:T(1024)S(1)}, f32[2048]{0:T(1024)S(1)}, u32[]{:S(2)}, u32[]{:S(2)}) collective-permute-start(f32[2048]{0:T(1024)S(1)} %convolution_bitcast_fusion), channel_id=1, source_target_pairs={{0,64},{1,65},{2,66},{3,67},{4,68},{5,69},{6,70},{7,71},{8,72},{9,... | collective-permute-start | bytes 24584 | tf_op jit(solution)/shard_map/ppermute | solution.py:59

commit v7 on v6

--- a/solution.py
+++ b/solution.py
@@ -4,6 +4,7 @@
 from jax.experimental import pallas as pl
 from jax.experimental.pallas import tpu as pltpu
 from jax.sharding import PartitionSpec as P
+
 
 LANES = 128
 OWNERS = 32
@@ -148,82 +149,67 @@
         out_ref[p, TERMS:SENT] = terms_ref[2 * p : 2 * p + 2 * WINDOW]
 
 
-def by_distance(left, work):
-    work([CENTER])
-
-    def pair(i, carry):
-        work([CENTER - i, CENTER + i])
-        return carry
-
-    if left:
-        lax.fori_loop(1, left + 1, pair, 0)
-
-
-def run_steps(window_ref, lists_ref, forcing_ref, surface_ref, table_ref, scale_ref):
-    def spread(left):
-        largest = jnp.max(jnp.max(scale_ref[0], axis=1, keepdims=True), axis=0, keepdims=True)
+def groups(left):
+    if left == 0:
+        return [[CENTER]]
+    pairs = [[CENTER - i, CENTER + i] for i in range(2, left + 1)]
+    return [[CENTER, CENTER - 1, CENTER + 1]] + pairs
+
+
+def run_steps(parts, lists_ref, forcing_ref, surface_ref, table_ref):
+    def part(slot):
+        return parts[(slot - 2) // 3].at[(slot - 2) % 3]
+
+    def spread(left, largest):
+        largest = jnp.max(jnp.max(largest, axis=1, keepdims=True), axis=0, keepdims=True)
         largest = jnp.maximum(largest, 1e-30)
-        scale_ref[1] = jnp.broadcast_to(32767.0 / largest, (8, LANES))
-        scale_ref[2] = jnp.broadcast_to(largest * (1.0 / 32767.0), (8, LANES))
-        scale_ref[0] = jnp.zeros((8, LANES), F32)
-
-        def work(slots):
+        scale = jnp.broadcast_to(32767.0 / largest, (8, LANES))
+        slots = range(CENTER - left, CENTER + left + 1)
+        for slot in slots:
+            whole = []
+            for h in range(2):
+                scaled = surface_ref[slot, 8 * h : 8 * h + 8] * scale
+                whole.append((scaled + jnp.where(scaled < 0, -0.5, 0.5)).astype(I32))
+            table_ref[slot, 0:8] = pair_of(*whole)
+        for slot in slots:
+            value = pick(table_ref.at[slot], 8, lists_ref[slot].astype(I32))
+            pairs = pair_of(value, pltpu.roll(value, 7, 0))
+            table_ref[slot - 1, 9:10] = pairs[0:1]
+            table_ref[slot + 1, 8:9] = pairs[2:3]
+        return jnp.broadcast_to(largest * (1.0 / 32767.0), (8, LANES))
+
+    def advance(left, unit):
+        largest = jnp.zeros((8, LANES), F32)
+        for slots in groups(left):
             for slot in slots:
-                whole = []
+                own_part = part(slot)
                 for h in range(2):
-                    scaled = surface_ref[slot, 8 * h : 8 * h + 8] * scale_ref[1]
-                    whole.append((scaled + jnp.where(scaled < 0, -0.5, 0.5)).astype(I32))
-                table_ref[slot, 0:8] = pair_of(*whole)
-            sent = []
-            for slot in slots:
-                value = pick(table_ref.at[slot], 8, lists_ref[slot].astype(I32))
-                sent.append(pair_of(value, pltpu.roll(value, 7, 0)))
-            for slot, pairs in zip(slots, sent):
-                table_ref[slot - 1, 9:10] = pairs[0:1]
-                table_ref[slot + 1, 8:9] = pairs[2:3]
-
-        by_distance(left, work)
-
-    def advance(left):
-        def work(slots):
-            totals = []
-            for slot in slots:
-                for h in range(2):
-                    part = slice(8 * h, 8 * h + 8)
+                    rows = slice(8 * h, 8 * h + 8)
                     flow = None
                     for m in range(6):
-                        rows = slice(16 * m + 8 * h, 16 * m + 8 * h + 8)
-                        code = window_ref[slot - 2, rows].astype(I32)
-                        near = pick(table_ref.at[slot], 10, code).astype(F32)
-                        near = window_ref[slot - 2, CONDUCT + 16 * m + 8 * h : CONDUCT + 16 * m + 8 * h + 8] * near
+                        first = 16 * m + 8 * h
+                        near = pick(table_ref.at[slot], 10, own_part[first : first + 8].astype(I32)).astype(F32)
+                        near = own_part[CONDUCT + first : CONDUCT + first + 8] * near
                         flow = near if flow is None else flow + near
-                    own = surface_ref[slot, part]
-                    keep = window_ref[slot - 2, KEEP + 8 * h : KEEP + 8 * h + 8]
-                    totals.append(keep * own + forcing_ref[slot - 2, part] + flow * scale_ref[2])
-            largest = scale_ref[0]
-            for i, slot in enumerate(slots):
-                for h in range(2):
-                    total = totals[2 * i + h]
-                    surface_ref[slot, 8 * h : 8 * h + 8] = total
+                    keep = own_part[KEEP + 8 * h : KEEP + 8 * h + 8]
+                    total = keep * surface_ref[slot, rows] + forcing_ref[slot - 2, rows] + flow * unit
+                    surface_ref[slot, rows] = total
                     largest = jnp.maximum(largest, jnp.abs(total))
-            scale_ref[0] = largest
-
-        by_distance(left, work)
+        return largest
 
     largest = jnp.zeros((8, LANES), F32)
     for slot in range(1, WINDOW + 3):
         for h in range(2):
             largest = jnp.maximum(largest, jnp.abs(surface_ref[slot, 8 * h : 8 * h + 8]))
-    scale_ref[0] = largest
-    spread(REACH + 1)
-    for step in range(STEPS):
-        left = STEPS - 1 - step
-        advance(left)
+    unit = spread(REACH + 1, largest)
+    for left in reversed(range(STEPS)):
+        largest = advance(left, unit)
         if left:
-            spread(left)
-
-
-def first_kernel(owner_ref, arrived_ref, window_ref, out_ref, lists_ref, forcing_ref, terms_ref, surface_ref, table_ref, scale_ref):
+            unit = spread(left, largest)
+
+
+def first_kernel(owner_ref, arrived_ref, low_ref, middle_ref, high_ref, out_ref, lists_ref, forcing_ref, terms_ref, surface_ref, table_ref):
+    parts = (low_ref, middle_ref, high_ref)
     owner = owner_ref[0]
     for slot in range(1, WINDOW + 3):
         other = (owner + (slot - CENTER + OWNERS)) % OWNERS
@@ -235,18 +221,19 @@
     for k in range(WINDOW):
         for j in range(2):
             terms_ref[pl.ds(j, OWNERS, stride=2), :] = arrived_ref[:, TERMS + 2 * k + j, :]
-        target = window_ref[k, TARGET : TARGET + 1, 0:TILES].astype(I32)
+        target = parts[k // 3][k % 3, TARGET : TARGET + 1, 0:TILES].astype(I32)
         hot = (blocks == target).astype(F32)
         forcing_ref[k] = jnp.dot(hot, terms_ref[...], precision=HIGHEST, preferred_element_type=F32)
-    run_steps(window_ref, lists_ref, forcing_ref, surface_ref, table_ref, scale_ref)
+    run_steps(parts, lists_ref, forcing_ref, surface_ref, table_ref)
     out_ref[...] = jnp.broadcast_to(surface_ref[CENTER][None], out_ref.shape)
 
 
-def last_kernel(owner_ref, target_ref, surfaces_ref, window_ref, lists_ref, forcing_ref, out_ref, values_ref, surface_ref, table_ref, scale_ref):
+def last_kernel(owner_ref, target_ref, surfaces_ref, low_ref, middle_ref, high_ref, lists_ref, forcing_ref, out_ref, values_ref, surface_ref, table_ref):
+    parts = (low_ref, middle_ref, high_ref)
     owner = owner_ref[0]
     for slot in range(1, WINDOW + 3):
         surface_ref[slot] = surfaces_ref[(owner + (slot - CENTER + OWNERS)) % OWNERS]
-    run_steps(window_ref, lists_ref, forcing_ref, surface_ref, table_ref, scale_ref)
+    run_steps(parts, lists_ref, forcing_ref, surface_ref, table_ref)
     out_ref[...] = surface_ref[CENTER]
     for t in range(TILES):
         values_ref[t // 2, t % 2 : t % 2 + 1] = surface_ref[CENTER, pl.ds(target_ref[t], 1), :]
@@ -272,7 +259,6 @@
     scratch = [
         pltpu.VMEM((SLOTS, 16, LANES), F32),
         pltpu.VMEM((SLOTS, 16, LANES), I32),
-        pltpu.VMEM((3, 8, LANES), F32),
     ]
 
     partials, packed = pl.pallas_call(
@@ -290,10 +276,8 @@
         send_lists,
         tile_target.reshape(1, TILES),
     )
-    with jax.named_scope("levels"):
-        shares = lax.all_to_all(partials, "comp", split_axis=0, concat_axis=0, tiled=True)
-    with jax.named_scope("near"):
-        lower, higher = from_owner(packed, -1), from_owner(packed, 1)
+    shares = lax.all_to_all(partials, "comp", split_axis=0, concat_axis=0, tiled=True)
+    lower, higher = from_owner(packed, -1), from_owner(packed, 1)
     three = jnp.concatenate([lower, packed, higher], axis=0)
     terms = pl.pallas_call(
         terms_kernel,
@@ -301,24 +285,22 @@
         in_specs=[SMEM] + [VMEM] * 3,
         scratch_shapes=[pltpu.VMEM((16, 8, LANES), F32), pltpu.VMEM((TILES + 2 * WINDOW, LANES), F32)],
     )(tile_source, shares, packed, tile_weight)
-    with jax.named_scope("send"):
-        arrived = exchange(terms)
-    with jax.named_scope("far"):
-        lower, higher = from_owner(three, -3), from_owner(three, 3)
-    window = jnp.concatenate([lower, three, higher], axis=0).reshape(WINDOW, PART, LANES)
+    arrived = exchange(terms)
+    lower, higher = from_owner(three, -3), from_owner(three, 3)
+    window = [block.reshape(3, PART, LANES) for block in (lower, three, higher)]
     surface, lists, forcing = pl.pallas_call(
         first_kernel,
         out_shape=(shape(OWNERS, 16, LANES), shape(SLOTS, 8, LANES), shape(WINDOW, 16, LANES)),
-        in_specs=[SMEM] + [VMEM] * 2,
+        in_specs=[SMEM] + [VMEM] * 4,
         scratch_shapes=[pltpu.VMEM((TILES, LANES), F32)] + scratch,
-    )(owner, arrived, window)
+    )(owner, arrived, *window)
     surfaces = exchange(surface)
     ocean_end, values = pl.pallas_call(
         last_kernel,
         out_shape=(shape(16, LANES), shape(OWNERS, 2, LANES)),
-        in_specs=[SMEM] * 2 + [VMEM] * 4,
+        in_specs=[SMEM] * 2 + [VMEM] * 6,
         scratch_shapes=scratch,
-    )(owner, tile_target, surfaces, window, lists, forcing)
+    )(owner, tile_target, surfaces, *window, lists, forcing)
     ocean_end = to_idle(ocean_end)
     returned = exchange(values).reshape(TILES, LANES)
     pulled = jnp.sum(returned[:, None, :] * tile_weight.astype(F32), axis=2)

time: 109 us -> 115 us (1.055)
  blocking collectives: 15.4 us -> 34.3 us
  starting transfers between devices: 38.8 us -> 33.7 us
  Pallas kernels: 25.4 us -> 20.7 us
  waiting for transfers between devices: 21.6 us -> 19.8 us
    all_to_all x0 -> x1, blocking collectives: none -> 11.9 us  [local(): lax.all_to_all(partials, 'comp', split_axis=0, concat_axis=0, tiled=True)]
    all_to_all x1, blocking collectives: 15.4 us -> 22.4 us  [exchange(): lax.all_to_all(blocks, BOTH, split_axis=0, concat_axis=0, tiled=True, axi...]
    all_to_all x1 -> x0, starting transfers between devices: 5.91 us -> none  [local(): lax.all_to_all(partials, 'comp', split_axis=0, concat_axis=0, tiled=True)]
    all_to_all x1 -> x0, waiting for transfers between devices: 3.48 us -> none  [local(): lax.all_to_all(partials, 'comp', split_axis=0, concat_axis=0, tiled=True)]
    pallas_call x1, Pallas kernels: 10.4 us -> 7.97 us  [local(): pl.pallas_call(first_kernel, out_shape=(shape(OWNERS, 16, LANES), shape(S...]
    pallas_call x1, Pallas kernels: 9.96 us -> 7.68 us  [local(): pl.pallas_call(last_kernel, out_shape=(shape(16, LANES), shape(OWNERS, 2,...]
    ppermute x4, waiting for transfers between devices: 10.4 us -> 12.1 us  [from_owner(): return lax.ppermute(block, BOTH, route)]
  transfers between devices with their start and end apart: 9 -> 8, of which waited for: 4 -> 6; matrix products, arithmetic and copies ran while one was open for 2% -> 2% of each run, Pallas kernels for 3% -> 0%
where the time goes in v7:
time: 115 us; the launch traced here: 113 us
  blocking collectives  34.3 us (30%)
  starting transfers between devices  33.7 us (29%)
  Pallas kernels  20.7 us (18%)
  waiting for transfers between devices  19.8 us (17%)
  other arithmetic  2.38 us (2%)
    all_to_all x1, blocking collectives, exchange(): lax.all_to_all(blocks, BOTH, split_axis=0, concat_axis=0, tiled=True, axi...  22.4 us
    ppermute x4, starting transfers between devices, from_owner(): return lax.ppermute(block, BOTH, route)  15.9 us
    all_to_all x2, starting transfers between devices, exchange(): lax.all_to_all(blocks, BOTH, split_axis=0, concat_axis=0, tiled=True, axi...  15.2 us
    ppermute x4, waiting for transfers between devices, from_owner(): return lax.ppermute(block, BOTH, route)  12.1 us
    all_to_all x1, blocking collectives, local(): lax.all_to_all(partials, 'comp', split_axis=0, concat_axis=0, tiled=True)  11.9 us
    pallas_call x1, Pallas kernels, local(): pl.pallas_call(first_kernel, out_shape=(shape(OWNERS, 16, LANES), shape(S...  7.97 us
    pallas_call x1, Pallas kernels, local(): pl.pallas_call(last_kernel, out_shape=(shape(16, LANES), shape(OWNERS, 2,...  7.68 us
    all_to_all x2, waiting for transfers between devices, exchange(): lax.all_to_all(blocks, BOTH, split_axis=0, concat_axis=0, tiled=True, axi...  6.99 us
  transfers between devices with their start and end apart: 8, of which 6 were waited for; matrix products, arithmetic and copies ran while one was open for 2% of the time, Pallas kernels for 0%

profile of v7, /device:TPU:2, one launch (start us, length us, event | category | flops | bytes accessed | tf_op | source)
XLA Modules:
  0.0 112.9 jit_solution(9473839216090284141)
XLA Ops:
  0.6 1.7 %shard_map.113 = (f32[8,16,128]{2,1,0:T(8,128)}, f32[232,128]{1,0:T(8,128)}) custom-call(f32[9]{0:T(128)} %weight_ref.2, bf16[9,2048]{1,0:T(8,128)(2,1)} %flux_ref.1, s32[6,2048]{1,0:T(8,128)} %neighbor_ref.1, f32[6,2048]{1,0:T(8,128)} %conduct_ref.1, f32[16,128]{1,0:T(8,128)} %bitcast.18, f32[16,128]{1,0:T(8,128)} %bitcast.19, s32[2,256]{1,0:T(2,128)} %lists_ref.1, ...), custom_call_target="tpu_custom_call" | custom-call | tf_op jit(solution)/shard_map/pallas_call | solution.py:264
  2.4 11.9 %all_to_all.20.shares_ref = f32[8,16,128]{2,1,0:T(8,128)} all-to-all(f32[8,16,128]{2,1,0:T(8,128)} %get-tuple-element.9), channel_id=1, replica_groups=mesh['comp'=8,'cells'=32] {'comp'}, dimensions={0} | all-to-all | bytes 131072 | tf_op jit(solution)/shard_map/all_to_all | solution.py:279
  14.3 3.3 %shard_map.114 = f32[32,40,128]{2,1,0:T(8,128)} custom-call(s32[64]{0:T(128)} %source_ref.1, f32[8,16,128]{2,1,0:T(8,128)} %all_to_all.20.shares_ref, f32[232,128]{1,0:T(8,128)} %get-tuple-element.10.packed_ref, bf16[64,128,128]{2,1,0:T(8,128)(2,1)} %weight_ref.3), custom_call_target="tpu_custom_call" | custom-call | tf_op jit(solution)/shard_map/pallas_call | solution.py:282
  17.6 9.8 %all-to-all-start.1 = ((f32[32,40,128]{2,1,0:T(8,128)}), f32[32,40,128]{2,1,0:T(8,128)S(1)}, u32[]{:S(2)}, u32[]{:S(2)}) async-start(f32[32,40,128]{2,1,0:T(8,128)} %shard_map.114), calls=%async_computation.1 | async-start | bytes 1310720 | tf_op jit(solution)/shard_map/all_to_all | solution.py:64
  27.4 0.0 copy-done.4
  27.4 3.4 %collective-permute-start = (f32[232,128]{1,0:T(8,128)S(1)}, f32[232,128]{1,0:T(8,128)S(1)}, u32[]{:S(2)}, u32[]{:S(2)}) collective-permute-start(f32[232,128]{1,0:T(8,128)S(1)} %copy-done.4), channel_id=1, source_target_pairs={{223,0},{0,1},{1,2},{2,3},{3,4},{4,5},{5,6},{6,7},{7,8},{8,9},{9,1... | collective-permute-start | bytes 356360 | tf_op jit(solution)/shard_map/ppermute | solution.py:49
  30.8 2.5 %collective-permute-start.1 = (f32[232,128]{1,0:T(8,128)S(1)}, f32[232,128]{1,0:T(8,128)S(1)}, u32[]{:S(2)}, u32[]{:S(2)}) collective-permute-start(f32[232,128]{1,0:T(8,128)S(1)} %copy-done.4), channel_id=1, source_target_pairs={{1,0},{2,1},{3,2},{4,3},{5,4},{6,5},{7,6},{8,7},{9,8},{10,9},{11,1... | collective-permute-start | bytes 356360 | tf_op jit(solution)/shard_map/ppermute | solution.py:49
  33.3 4.2 %collective-permute-done = f32[232,128]{1,0:T(8,128)S(1)} collective-permute-done((f32[232,128]{1,0:T(8,128)S(1)}, f32[232,128]{1,0:T(8,128)S(1)}, u32[]{:S(2)}, u32[]{:S(2)}) %collective-permute-start) | collective-permute-done | bytes 118816 | tf_op jit(solution)/shard_map/ppermute | solution.py:49
  37.5 0.0 copy-start
  37.5 1.4 %collective-permute-done.1 = f32[232,128]{1,0:T(8,128)S(1)} collective-permute-done((f32[232,128]{1,0:T(8,128)S(1)}, f32[232,128]{1,0:T(8,128)S(1)}, u32[]{:S(2)}, u32[]{:S(2)}) %collective-permute-start.1) | collective-permute-done | bytes 118816 | tf_op jit(solution)/shard_map/ppermute | solution.py:49
  38.9 0.0 copy-start.2
  38.9 4.5 %collective-permute-start.2 = (f32[696,128]{1,0:T(8,128)S(1)}, f32[696,128]{1,0:T(8,128)S(1)}, u32[]{:S(2)}, u32[]{:S(2)}) collective-permute-start(f32[696,128]{1,0:T(8,128)S(1)} %constant_dynamic-update-slice_fusion), channel_id=1, source_target_pairs={{221,0},{222,1},{223,2},{0,3},{1,4},{2,5},{3,6},{4,7},{5,8},{6,9},... | collective-permute-start | bytes 1069064 | tf_op jit(solution)/shard_map/ppermute | solution.py:49
  43.4 5.6 %collective-permute-start.3 = (f32[696,128]{1,0:T(8,128)S(1)}, f32[696,128]{1,0:T(8,128)}, u32[]{:S(2)}, u32[]{:S(2)}) collective-permute-start(f32[696,128]{1,0:T(8,128)S(1)} %constant_dynamic-update-slice_fusion), channel_id=1, source_target_pairs={{3,0},{4,1},{5,2},{6,3},{7,4},{8,5},{9,6},{10,7},{11,8},{12,9},{13... | collective-permute-start | bytes 1069064 | tf_op jit(solution)/shard_map/ppermute | solution.py:49
  49.0 5.3 %collective-permute-done.2 = f32[696,128]{1,0:T(8,128)S(1)} collective-permute-done((f32[696,128]{1,0:T(8,128)S(1)}, f32[696,128]{1,0:T(8,128)S(1)}, u32[]{:S(2)}, u32[]{:S(2)}) %collective-permute-start.2) | collective-permute-done | bytes 356384 | tf_op jit(solution)/shard_map/ppermute | solution.py:49
  54.4 1.2 %collective-permute-done.3 = f32[696,128]{1,0:T(8,128)} collective-permute-done((f32[696,128]{1,0:T(8,128)S(1)}, f32[696,128]{1,0:T(8,128)}, u32[]{:S(2)}, u32[]{:S(2)}) %collective-permute-start.3) | collective-permute-done | bytes 356384 | tf_op jit(solution)/shard_map/ppermute | solution.py:49
  55.6 0.0 all-to-all-done.1.arrived_ref
  55.6 0.0 copy-done.2
  55.6 0.0 copy-done.3
  55.6 0.8 copy-done.1
  56.4 8.0 %shard_map.115 = (f32[32,16,128]{2,1,0:T(8,128)}, f32[13,8,128]{2,1,0:T(8,128)}, f32[9,16,128]{2,1,0:T(8,128)}) custom-call(s32[1]{0:T(128)} %bitcast.owner_ref, f32[32,40,128]{2,1,0:T(8,128)} %copy-done.1, f32[3,232,128]{2,1,0:T(8,128)} %bitcast.15, f32[3,232,128]{2,1,0:T(8,128)} %bitcast.13, f32[3,232,128]{2,1,0:T(8,128)} %bitcast.6.high_ref), custom_call_target="tpu_custom_call" | custom-call | tf_op jit(solution)/shard_map/pallas_call | solution.py:291
  64.4 22.4 %all_to_all.21.surfaces_ref = f32[32,16,128]{2,1,0:T(8,128)} all-to-all(f32[32,16,128]{2,1,0:T(8,128)} %get-tuple-element.11), channel_id=1, replica_groups={{0,1,2,3,4,5,6,7,8,9,10,11,12,13,14,15,208,209,210,211,212,213,214,215,..., dimensions={0} | all-to-all | bytes 524288 | tf_op jit(solution)/shard_map/all_to_all | solution.py:64
  86.8 7.7 %shard_map.116 = (f32[16,128]{1,0:T(8,128)}, f32[32,2,128]{2,1,0:T(2,128)}) custom-call(s32[1]{0:T(128)} %bitcast.owner_ref, s32[64]{0:T(128)} %target_ref.1, f32[32,16,128]{2,1,0:T(8,128)} %all_to_all.21.surfaces_ref, f32[3,232,128]{2,1,0:T(8,128)} %bitcast.16, f32[3,232,128]{2,1,0:T(8,128)} %bitcast.14, f32[3,232,128]{2,1,0:T(8,128)} %bitcast.6.high_ref, ...), custom_call_target="tpu_custom_call" | custom-call | tf_op jit(solution)/shard_map/pallas_call | solution.py:298
  94.5 5.5 %all-to-all-start.3 = ((f32[32,2,128]{2,1,0:T(2,128)}), f32[32,2,128]{2,1,0:T(2,128)S(1)}, u32[]{:S(2)}, u32[]{:S(2)}) async-start(f32[32,2,128]{2,1,0:T(2,128)} %get-tuple-element.15), calls=%async_computation.3 | async-start | bytes 65536 | tf_op jit(solution)/shard_map/all_to_all | solution.py:64
  99.9 1.3 %collective-permute-start.4 = (f32[16,128]{1,0:T(8,128)}, f32[16,128]{1,0:T(8,128)S(1)}, u32[]{:S(2)}, u32[]{:S(2)}) collective-permute-start(f32[16,128]{1,0:T(8,128)} %get-tuple-element.14), channel_id=1, source_target_pairs={{0,64},{1,65},{2,66},{3,67},{4,68},{5,69},{6,70},{7,71},{8,72},{9,... | collective-permute-start | bytes 24584 | tf_op jit(solution)/shard_map/ppermute | solution.py:60
  101.2 7.0 %all-to-all-done.3 = f32[32,2,128]{2,1,0:T(2,128)S(1)} async-done(((f32[32,2,128]{2,1,0:T(2,128)}), f32[32,2,128]{2,1,0:T(2,128)S(1)}, u32[]{:S(2)}, u32[]{:S(2)}) %all-to-all-start.3) | async-done | bytes 32800 | tf_op jit(solution)/shard_map/all_to_all | solution.py:64
  108.2 1.2 %multiply_reduce_fusion = f32[64,128]{1,0:T(8,128)S(1)} fusion(bf16[64,128,128]{2,1,0:T(8,128)(2,1)S(1)} %copy-done, f32[64,128]{1,0:T(8,128)S(1)} %bitcast.17), kind=kLoop, calls=%fused_computation | loop fusion | flops 3137536 | bytes 2162688 | tf_op jit(solution)/shard_map/reduce_sum | solution.py:306
  109.4 0.3 convolution_bitcast_fusion
  109.7 1.3 %collective-permute-start.5 = (f32[2048]{0:T(1024)S(1)}, f32[2048]{0:T(1024)S(1)}, u32[]{:S(2)}, u32[]{:S(2)}) collective-permute-start(f32[2048]{0:T(1024)S(1)} %convolution_bitcast_fusion), channel_id=1, source_target_pairs={{0,64},{1,65},{2,66},{3,67},{4,68},{5,69},{6,70},{7,71},{8,72},{9,... | collective-permute-start | bytes 24584 | tf_op jit(solution)/shard_map/ppermute | solution.py:60
  111.0 0.0 collective-permute-done.4
  111.0 0.6 select_bitcast_fusion
  111.6 0.7 collective-permute-done.5
  112.3 0.6 broadcast_select_fusion
  (11 shorter events, 0.0 us)
Async XLA Ops:
  14.3 13.1 %copy-start.4 = (f32[232,128]{1,0:T(8,128)S(1)}, f32[232,128]{1,0:T(8,128)}, u32[]{:S(2)}) copy-start(f32[232,128]{1,0:T(8,128)} %get-tuple-element.10.packed_ref) | copy-start | bytes 356356
  17.6 37.9 %all-to-all-start.1 = ((f32[32,40,128]{2,1,0:T(8,128)}), f32[32,40,128]{2,1,0:T(8,128)S(1)}, u32[]{:S(2)}, u32[]{:S(2)}) async-start(f32[32,40,128]{2,1,0:T(8,128)} %shard_map.114), calls=%async_computation.1 | async-start | bytes 1310720 | tf_op jit(solution)/shard_map/all_to_all | solution.py:64
  27.4 10.1 %collective-permute-start = (f32[232,128]{1,0:T(8,128)S(1)}, f32[232,128]{1,0:T(8,128)S(1)}, u32[]{:S(2)}, u32[]{:S(2)}) collective-permute-start(f32[232,128]{1,0:T(8,128)S(1)} %copy-done.4), channel_id=1, source_target_pairs={{223,0},{0,1},{1,2},{2,3},{3,4},{4,5},{5,6},{6,7},{7,8},{8,9},{9,1... | collective-permute-start | bytes 356360 | tf_op jit(solution)/shard_map/ppermute | solution.py:49
  30.8 8.1 %collective-permute-start.1 = (f32[232,128]{1,0:T(8,128)S(1)}, f32[232,128]{1,0:T(8,128)S(1)}, u32[]{:S(2)}, u32[]{:S(2)}) collective-permute-start(f32[232,128]{1,0:T(8,128)S(1)} %copy-done.4), channel_id=1, source_target_pairs={{1,0},{2,1},{3,2},{4,3},{5,4},{6,5},{7,6},{8,7},{9,8},{10,9},{11,1... | collective-permute-start | bytes 356360 | tf_op jit(solution)/shard_map/ppermute | solution.py:49
  37.5 70.7 %copy-start = (bf16[64,128,128]{2,1,0:T(8,128)(2,1)S(1)}, bf16[64,128,128]{2,1,0:T(8,128)(2,1)}, u32[]{:S(2)}) copy-start(bf16[64,128,128]{2,1,0:T(8,128)(2,1)} %weight_ref.3) | copy-start | bytes 6291460
  38.9 16.6 %copy-start.2 = (f32[696,128]{1,0:T(8,128)}, f32[696,128]{1,0:T(8,128)S(1)}, u32[]{:S(2)}) copy-start(f32[696,128]{1,0:T(8,128)S(1)} %constant_dynamic-update-slice_fusion) | copy-start | bytes 1069060
  38.9 15.4 %collective-permute-start.2 = (f32[696,128]{1,0:T(8,128)S(1)}, f32[696,128]{1,0:T(8,128)S(1)}, u32[]{:S(2)}, u32[]{:S(2)}) collective-permute-start(f32[696,128]{1,0:T(8,128)S(1)} %constant_dynamic-update-slice_fusion), channel_id=1, source_target_pairs={{221,0},{222,1},{223,2},{0,3},{1,4},{2,5},{3,6},{4,7},{5,8},{6,9},... | collective-permute-start | bytes 1069064 | tf_op jit(solution)/shard_map/ppermute | solution.py:49
  43.4 12.1 %collective-permute-start.3 = (f32[696,128]{1,0:T(8,128)S(1)}, f32[696,128]{1,0:T(8,128)}, u32[]{:S(2)}, u32[]{:S(2)}) collective-permute-start(f32[696,128]{1,0:T(8,128)S(1)} %constant_dynamic-update-slice_fusion), channel_id=1, source_target_pairs={{3,0},{4,1},{5,2},{6,3},{7,4},{8,5},{9,6},{10,7},{11,8},{12,9},{13... | collective-permute-start | bytes 1069064 | tf_op jit(solution)/shard_map/ppermute | solution.py:49
  54.4 1.2 %copy-start.3 = (f32[696,128]{1,0:T(8,128)}, f32[696,128]{1,0:T(8,128)S(1)}, u32[]{:S(2)}) copy-start(f32[696,128]{1,0:T(8,128)S(1)} %collective-permute-done.2) | copy-start | bytes 1069060
  55.6 0.8 copy-start.1
  64.4 45.0 %copy-start.6 = (s32[64]{0:T(128)S(1)}, s32[64]{0:T(128)}, u32[]{:S(2)}) copy-start(s32[64]{0:T(128)} %source_ref.1) | copy-start | bytes 772
  94.5 16.5 %copy-start.5 = (f32[16,128]{1,0:T(8,128)S(1)}, f32[16,128]{1,0:T(8,128)}, u32[]{:S(2)}) copy-start(f32[16,128]{1,0:T(8,128)} %get-tuple-element.14) | copy-start | bytes 24580
  94.5 13.8 %all-to-all-start.3 = ((f32[32,2,128]{2,1,0:T(2,128)}), f32[32,2,128]{2,1,0:T(2,128)S(1)}, u32[]{:S(2)}, u32[]{:S(2)}) async-start(f32[32,2,128]{2,1,0:T(2,128)} %get-tuple-element.15), calls=%async_computation.3 | async-start | bytes 65536 | tf_op jit(solution)/shard_map/all_to_all | solution.py:64
  99.9 11.0 %collective-permute-start.4 = (f32[16,128]{1,0:T(8,128)}, f32[16,128]{1,0:T(8,128)S(1)}, u32[]{:S(2)}, u32[]{:S(2)}) collective-permute-start(f32[16,128]{1,0:T(8,128)} %get-tuple-element.14), channel_id=1, source_target_pairs={{0,64},{1,65},{2,66},{3,67},{4,68},{5,69},{6,70},{7,71},{8,72},{9,... | collective-permute-start | bytes 24584 | tf_op jit(solution)/shard_map/ppermute | solution.py:60
  109.7 2.6 %collective-permute-start.5 = (f32[2048]{0:T(1024)S(1)}, f32[2048]{0:T(1024)S(1)}, u32[]{:S(2)}, u32[]{:S(2)}) collective-permute-start(f32[2048]{0:T(1024)S(1)} %convolution_bitcast_fusion), channel_id=1, source_target_pairs={{0,64},{1,65},{2,66},{3,67},{4,68},{5,69},{6,70},{7,71},{8,72},{9,... | collective-permute-start | bytes 24584 | tf_op jit(solution)/shard_map/ppermute | solution.py:60

commit v8 on v7

--- a/solution.py
+++ b/solution.py
@@ -31,10 +31,11 @@
     return (2 * z_low + core) * OWNERS + owner
 
 
-COPIES = [(copy, core) for copy in (0, 3) for core in range(2)]
+COPIES = [(0, 0), (3, 0)]
+PLANES = [[(1, 0), (1, 1)], [(2, 0), (2, 1)], [(0, 1), (3, 1)]]
 IDLE = [
-    [(2 * z_low + core) * OWNERS + half * HALF + i for core in range(2) for i in range(HALF)]
-    for z_low in (1, 2)
+    [(2 * z_low + core) * OWNERS + half * HALF + i for z_low, core in planes for i in range(HALF)]
+    for planes in PLANES
     for half in range(2)
 ]
 ALL = [[device_of(owner, *copy) for owner in range(OWNERS)] for copy in COPIES] + IDLE
@@ -50,14 +51,16 @@
 
 
 def to_idle(block):
-    route = [
-        ((2 * here + core) * OWNERS + owner, (2 * there + core) * OWNERS + owner)
-        for here, there in ((0, 1), (3, 2))
-        for core in range(2)
-        for owner in range(OWNERS)
-    ]
-    z_low = lax.axis_index("comp") // 2
-    return jnp.where((z_low == 0) | (z_low == 3), block, lax.ppermute(block, BOTH, route))
+    arrived = []
+    for aside, core in ((1, 0), (1, 1), (0, 1)):
+        route = [
+            (2 * here * OWNERS + owner, (2 * (there if aside else here) + core) * OWNERS + owner)
+            for here, there in ((0, 1), (3, 2))
+            for owner in range(OWNERS)
+        ]
+        arrived.append(lax.ppermute(block, BOTH, route))
+    seat = lax.axis_index("comp")
+    return jnp.where((seat == 0) | (seat == 6), block, arrived[0] + arrived[1] + arrived[2])
 
 
 def exchange(blocks):
@@ -158,7 +161,7 @@
 
 def run_steps(parts, lists_ref, forcing_ref, surface_ref, table_ref):
     def part(slot):
-        return parts[(slot - 2) // 3].at[(slot - 2) % 3]
+        return parts[(slot - 2) % 3].at[(slot - 2) // 3]
 
     def spread(left, largest):
         largest = jnp.max(jnp.max(largest, axis=1, keepdims=True), axis=0, keepdims=True)
@@ -221,7 +224,7 @@
     for k in range(WINDOW):
         for j in range(2):
             terms_ref[pl.ds(j, OWNERS, stride=2), :] = arrived_ref[:, TERMS + 2 * k + j, :]
-        target = parts[k // 3][k % 3, TARGET : TARGET + 1, 0:TILES].astype(I32)
+        target = parts[k % 3][k // 3, TARGET : TARGET + 1, 0:TILES].astype(I32)
         hot = (blocks == target).astype(F32)
         forcing_ref[k] = jnp.dot(hot, terms_ref[...], precision=HIGHEST, preferred_element_type=F32)
     run_steps(parts, lists_ref, forcing_ref, surface_ref, table_ref)
@@ -277,7 +280,7 @@
         tile_target.reshape(1, TILES),
     )
     shares = lax.all_to_all(partials, "comp", split_axis=0, concat_axis=0, tiled=True)
-    lower, higher = from_owner(packed, -1), from_owner(packed, 1)
+    lower, higher = from_owner(packed, -3), from_owner(packed, 3)
     three = jnp.concatenate([lower, packed, higher], axis=0)
     terms = pl.pallas_call(
         terms_kernel,
@@ -286,7 +289,7 @@
         scratch_shapes=[pltpu.VMEM((16, 8, LANES), F32), pltpu.VMEM((TILES + 2 * WINDOW, LANES), F32)],
     )(tile_source, shares, packed, tile_weight)
     arrived = exchange(terms)
-    lower, higher = from_owner(three, -3), from_owner(three, 3)
+    lower, higher = from_owner(three, -1), from_owner(three, 1)
     window = [block.reshape(3, PART, LANES) for block in (lower, three, higher)]
     surface, lists, forcing = pl.pallas_call(
         first_kernel,

time: 115 us -> 116 us (level)
  the two profiles are of different devices: /device:TPU:2 before, /device:TPU:65 now
where the time goes in v8:
time: 116 us
  waiting for transfers between devices  46 us (40%)
  blocking collectives  23 us (20%)
  starting transfers between devices  21.6 us (19%)
  Pallas kernels  20.7 us (18%)
  other arithmetic  2.38 us (2%)
    ppermute x6, waiting for transfers between devices, to_idle(): arrived.append(lax.ppermute(block, BOTH, route))  33.1 us
    all_to_all x1, blocking collectives, exchange(): lax.all_to_all(blocks, BOTH, split_axis=0, concat_axis=0, tiled=True, axi...  14 us
    all_to_all x2, waiting for transfers between devices, exchange(): lax.all_to_all(blocks, BOTH, split_axis=0, concat_axis=0, tiled=True, axi...  12.9 us
    all_to_all x2, starting transfers between devices, exchange(): lax.all_to_all(blocks, BOTH, split_axis=0, concat_axis=0, tiled=True, axi...  12.8 us
    all_to_all x1, blocking collectives, local(): lax.all_to_all(partials, 'comp', split_axis=0, concat_axis=0, tiled=True)  8.93 us
    pallas_call x1, Pallas kernels, local(): pl.pallas_call(first_kernel, out_shape=(shape(OWNERS, 16, LANES), shape(S...  7.98 us
    pallas_call x1, Pallas kernels, local(): pl.pallas_call(last_kernel, out_shape=(shape(16, LANES), shape(OWNERS, 2,...  7.68 us
    ppermute x6, starting transfers between devices, to_idle(): arrived.append(lax.ppermute(block, BOTH, route))  5.23 us
  transfers between devices with their start and end apart: 12, of which 4 were waited for; matrix products, arithmetic and copies ran while one was open for 2% of the time, Pallas kernels for 0%

profile of v8, /device:TPU:65, one launch (start us, length us, event | category | flops | bytes accessed | tf_op | source)
XLA Modules:
  0.0 115.7 jit_solution(45236927761829948)
XLA Ops:
  0.6 1.7 %shard_map.113 = (f32[8,16,128]{2,1,0:T(8,128)}, f32[232,128]{1,0:T(8,128)}) custom-call(f32[9]{0:T(128)} %weight_ref.2, bf16[9,2048]{1,0:T(8,128)(2,1)} %flux_ref.1, s32[6,2048]{1,0:T(8,128)} %neighbor_ref.1, f32[6,2048]{1,0:T(8,128)} %conduct_ref.1, f32[16,128]{1,0:T(8,128)} %bitcast.18, f32[16,128]{1,0:T(8,128)} %bitcast.19, s32[2,256]{1,0:T(2,128)} %lists_ref.1, ...), custom_call_target="tpu_custom_call" | custom-call | tf_op jit(solution)/shard_map/pallas_call | solution.py:267
  2.4 8.9 %all_to_all.20.shares_ref = f32[8,16,128]{2,1,0:T(8,128)} all-to-all(f32[8,16,128]{2,1,0:T(8,128)} %get-tuple-element.9), channel_id=1, replica_groups=mesh['comp'=8,'cells'=32] {'comp'}, dimensions={0} | all-to-all | bytes 131072 | tf_op jit(solution)/shard_map/all_to_all | solution.py:282
  11.3 3.3 %shard_map.114 = f32[32,40,128]{2,1,0:T(8,128)} custom-call(s32[64]{0:T(128)} %source_ref.1, f32[8,16,128]{2,1,0:T(8,128)} %all_to_all.20.shares_ref, f32[232,128]{1,0:T(8,128)} %get-tuple-element.10.packed_ref, bf16[64,128,128]{2,1,0:T(8,128)(2,1)} %weight_ref.3), custom_call_target="tpu_custom_call" | custom-call | tf_op jit(solution)/shard_map/pallas_call | solution.py:285
  14.6 8.0 %all-to-all-start.1 = ((f32[32,40,128]{2,1,0:T(8,128)}), f32[32,40,128]{2,1,0:T(8,128)S(1)}, u32[]{:S(2)}, u32[]{:S(2)}) async-start(f32[32,40,128]{2,1,0:T(8,128)} %shard_map.114), calls=%async_computation.1 | async-start | bytes 1310720 | tf_op jit(solution)/shard_map/all_to_all | solution.py:67
  22.6 0.7 collective-permute-start
  23.3 0.7 collective-permute-start.1
  24.0 0.0 collective-permute-done
  24.0 0.0 copy-start
  24.1 0.8 collective-permute-start.2
  24.9 1.4 %collective-permute-start.3 = (f32[696,128]{1,0:T(8,128)S(1)}, f32[696,128]{1,0:T(8,128)}, u32[]{:S(2)}, u32[]{:S(2)}) collective-permute-start(f32[696,128]{1,0:T(8,128)S(1)} %constant_dynamic-update-slice_fusion), channel_id=1, source_target_pairs={{1,0},{2,1},{3,2},{4,3},{5,4},{6,5},{7,6},{8,7},{9,8},{10,9},{11,1... | collective-permute-start | bytes 1069064 | tf_op jit(solution)/shard_map/ppermute | solution.py:50
  26.3 0.0 collective-permute-done.2
  26.3 8.6 %all-to-all-done.1.arrived_ref = f32[32,40,128]{2,1,0:T(8,128)S(1)} async-done(((f32[32,40,128]{2,1,0:T(8,128)}), f32[32,40,128]{2,1,0:T(8,128)S(1)}, u32[]{:S(2)}, u32[]{:S(2)}) %all-to-all-start.1) | async-done | bytes 655392 | tf_op jit(solution)/shard_map/all_to_all | solution.py:67
  34.9 0.9 copy-done.1
  35.8 8.0 %shard_map.115 = (f32[32,16,128]{2,1,0:T(8,128)}, f32[13,8,128]{2,1,0:T(8,128)}, f32[9,16,128]{2,1,0:T(8,128)}) custom-call(s32[1]{0:T(128)} %bitcast.owner_ref, f32[32,40,128]{2,1,0:T(8,128)} %copy-done.1, f32[3,232,128]{2,1,0:T(8,128)} %bitcast.15, f32[3,232,128]{2,1,0:T(8,128)} %bitcast.13, f32[3,232,128]{2,1,0:T(8,128)} %bitcast.6.high_ref), custom_call_target="tpu_custom_call" | custom-call | tf_op jit(solution)/shard_map/pallas_call | solution.py:294
  43.7 14.0 %all_to_all.21.surfaces_ref = f32[32,16,128]{2,1,0:T(8,128)} all-to-all(f32[32,16,128]{2,1,0:T(8,128)} %get-tuple-element.11), channel_id=1, replica_groups={{0,1,2,3,4,5,6,7,8,9,10,11,12,13,14,15,208,209,210,211,212,213,214,215,..., dimensions={0} | all-to-all | bytes 524288 | tf_op jit(solution)/shard_map/all_to_all | solution.py:67
  57.8 7.7 %shard_map.116 = (f32[16,128]{1,0:T(8,128)}, f32[32,2,128]{2,1,0:T(2,128)}) custom-call(s32[1]{0:T(128)} %bitcast.owner_ref, s32[64]{0:T(128)} %target_ref.1, f32[32,16,128]{2,1,0:T(8,128)} %all_to_all.21.surfaces_ref, f32[3,232,128]{2,1,0:T(8,128)} %bitcast.16, f32[3,232,128]{2,1,0:T(8,128)} %bitcast.14, f32[3,232,128]{2,1,0:T(8,128)} %bitcast.6.high_ref, ...), custom_call_target="tpu_custom_call" | custom-call | tf_op jit(solution)/shard_map/pallas_call | solution.py:301
  65.5 4.8 %all-to-all-start.3 = ((f32[32,2,128]{2,1,0:T(2,128)}), f32[32,2,128]{2,1,0:T(2,128)S(1)}, u32[]{:S(2)}, u32[]{:S(2)}) async-start(f32[32,2,128]{2,1,0:T(2,128)} %get-tuple-element.15), calls=%async_computation.3 | async-start | bytes 65536 | tf_op jit(solution)/shard_map/all_to_all | solution.py:67
  70.3 0.7 collective-permute-start.6
  71.0 0.7 collective-permute-start.4
  71.6 1.3 %collective-permute-start.5 = (f32[16,128]{1,0:T(8,128)}, f32[16,128]{1,0:T(8,128)S(1)}, u32[]{:S(2)}, u32[]{:S(2)}) collective-permute-start(f32[16,128]{1,0:T(8,128)} %get-tuple-element.14), channel_id=1, source_target_pairs={{0,96},{1,97},{2,98},{3,99},{4,100},{5,101},{6,102},{7,103},{8,104... | collective-permute-start | bytes 24584 | tf_op jit(solution)/shard_map/ppermute | solution.py:61
  72.9 4.3 %all-to-all-done.3 = f32[32,2,128]{2,1,0:T(2,128)S(1)} async-done(((f32[32,2,128]{2,1,0:T(2,128)}), f32[32,2,128]{2,1,0:T(2,128)S(1)}, u32[]{:S(2)}, u32[]{:S(2)}) %all-to-all-start.3) | async-done | bytes 32800 | tf_op jit(solution)/shard_map/all_to_all | solution.py:67
  77.3 1.2 %multiply_reduce_fusion = f32[64,128]{1,0:T(8,128)S(1)} fusion(bf16[64,128,128]{2,1,0:T(8,128)(2,1)S(1)} %copy-done, f32[64,128]{1,0:T(8,128)S(1)} %bitcast.17), kind=kLoop, calls=%fused_computation | loop fusion | flops 3137536 | bytes 2162688 | tf_op jit(solution)/shard_map/reduce_sum | solution.py:309
  78.4 0.3 convolution_bitcast_fusion
  78.7 0.7 collective-permute-start.9
  79.4 0.7 collective-permute-start.7
  80.1 1.3 %collective-permute-start.8 = (f32[2048]{0:T(1024)S(1)}, f32[2048]{0:T(1024)S(1)}, u32[]{:S(2)}, u32[]{:S(2)}) collective-permute-start(f32[2048]{0:T(1024)S(1)} %convolution_bitcast_fusion), channel_id=1, source_target_pairs={{0,96},{1,97},{2,98},{3,99},{4,100},{5,101},{6,102},{7,103},{8,104... | collective-permute-start | bytes 24584 | tf_op jit(solution)/shard_map/ppermute | solution.py:61
  81.4 0.0 collective-permute-done.4
  81.4 22.9 %collective-permute-done.5 = f32[16,128]{1,0:T(8,128)S(1)} collective-permute-done((f32[16,128]{1,0:T(8,128)}, f32[16,128]{1,0:T(8,128)S(1)}, u32[]{:S(2)}, u32[]{:S(2)}) %collective-permute-start.5) | collective-permute-done | bytes 8224 | tf_op jit(solution)/shard_map/ppermute | solution.py:61
  104.3 0.6 select_bitcast_fusion
  104.9 0.0 collective-permute-done.7
  104.9 10.2 %collective-permute-done.8 = f32[2048]{0:T(1024)S(1)} collective-permute-done((f32[2048]{0:T(1024)S(1)}, f32[2048]{0:T(1024)S(1)}, u32[]{:S(2)}, u32[]{:S(2)}) %collective-permute-start.8) | collective-permute-done | bytes 8224 | tf_op jit(solution)/shard_map/ppermute | solution.py:61
  115.1 0.6 add_select_fusion
  (19 shorter events, 0.1 us)
Async XLA Ops:
  11.3 11.3 %copy-start.4 = (f32[232,128]{1,0:T(8,128)S(1)}, f32[232,128]{1,0:T(8,128)}, u32[]{:S(2)}) copy-start(f32[232,128]{1,0:T(8,128)} %get-tuple-element.10.packed_ref) | copy-start | bytes 356356
  14.6 20.3 %all-to-all-start.1 = ((f32[32,40,128]{2,1,0:T(8,128)}), f32[32,40,128]{2,1,0:T(8,128)S(1)}, u32[]{:S(2)}, u32[]{:S(2)}) async-start(f32[32,40,128]{2,1,0:T(8,128)} %shard_map.114), calls=%async_computation.1 | async-start | bytes 1310720 | tf_op jit(solution)/shard_map/all_to_all | solution.py:67
  22.6 1.4 %collective-permute-start = (f32[232,128]{1,0:T(8,128)S(1)}, f32[232,128]{1,0:T(8,128)S(1)}, u32[]{:S(2)}, u32[]{:S(2)}) collective-permute-start(f32[232,128]{1,0:T(8,128)S(1)} %copy-done.4), channel_id=1, source_target_pairs={{221,0},{222,1},{223,2},{0,3},{1,4},{2,5},{3,6},{4,7},{5,8},{6,9},... | collective-permute-start | bytes 356360 | tf_op jit(solution)/shard_map/ppermute | solution.py:50
  23.3 0.7 collective-permute-start.1
  24.0 53.3 %copy-start = (bf16[64,128,128]{2,1,0:T(8,128)(2,1)S(1)}, bf16[64,128,128]{2,1,0:T(8,128)(2,1)}, u32[]{:S(2)}) copy-start(bf16[64,128,128]{2,1,0:T(8,128)(2,1)} %weight_ref.3) | copy-start | bytes 6291460
  24.1 10.8 %copy-start.2 = (f32[696,128]{1,0:T(8,128)}, f32[696,128]{1,0:T(8,128)S(1)}, u32[]{:S(2)}) copy-start(f32[696,128]{1,0:T(8,128)S(1)} %constant_dynamic-update-slice_fusion) | copy-start | bytes 1069060
  24.1 2.2 %collective-permute-start.2 = (f32[696,128]{1,0:T(8,128)S(1)}, f32[696,128]{1,0:T(8,128)S(1)}, u32[]{:S(2)}, u32[]{:S(2)}) collective-permute-start(f32[696,128]{1,0:T(8,128)S(1)} %constant_dynamic-update-slice_fusion), channel_id=1, source_target_pairs={{223,0},{0,1},{1,2},{2,3},{3,4},{4,5},{5,6},{6,7},{7,8},{8,9},{9,1... | collective-permute-start | bytes 1069064 | tf_op jit(solution)/shard_map/ppermute | solution.py:50
  24.9 1.4 %collective-permute-start.3 = (f32[696,128]{1,0:T(8,128)S(1)}, f32[696,128]{1,0:T(8,128)}, u32[]{:S(2)}, u32[]{:S(2)}) collective-permute-start(f32[696,128]{1,0:T(8,128)S(1)} %constant_dynamic-update-slice_fusion), channel_id=1, source_target_pairs={{1,0},{2,1},{3,2},{4,3},{5,4},{6,5},{7,6},{8,7},{9,8},{10,9},{11,1... | collective-permute-start | bytes 1069064 | tf_op jit(solution)/shard_map/ppermute | solution.py:50
  26.3 8.6 %copy-start.3 = (f32[696,128]{1,0:T(8,128)}, f32[696,128]{1,0:T(8,128)S(1)}, u32[]{:S(2)}) copy-start(f32[696,128]{1,0:T(8,128)S(1)} %collective-permute-done.2) | copy-start | bytes 1069060
  34.9 0.9 copy-start.1
  43.7 34.7 %copy-start.6 = (s32[64]{0:T(128)S(1)}, s32[64]{0:T(128)}, u32[]{:S(2)}) copy-start(s32[64]{0:T(128)} %source_ref.1) | copy-start | bytes 772
  65.5 38.8 %copy-start.5 = (f32[16,128]{1,0:T(8,128)S(1)}, f32[16,128]{1,0:T(8,128)}, u32[]{:S(2)}) copy-start(f32[16,128]{1,0:T(8,128)} %get-tuple-element.14) | copy-start | bytes 24580
  65.5 11.8 %all-to-all-start.3 = ((f32[32,2,128]{2,1,0:T(2,128)}), f32[32,2,128]{2,1,0:T(2,128)S(1)}, u32[]{:S(2)}, u32[]{:S(2)}) async-start(f32[32,2,128]{2,1,0:T(2,128)} %get-tuple-element.15), calls=%async_computation.3 | async-start | bytes 65536 | tf_op jit(solution)/shard_map/all_to_all | solution.py:67
  70.3 9.8 %collective-permute-start.6 = (f32[16,128]{1,0:T(8,128)}, f32[16,128]{1,0:T(8,128)S(1)}, u32[]{:S(2)}, u32[]{:S(2)}) collective-permute-start(f32[16,128]{1,0:T(8,128)} %get-tuple-element.14), channel_id=1, source_target_pairs={{0,32},{1,33},{2,34},{3,35},{4,36},{5,37},{6,38},{7,39},{8,40},{9,... | collective-permute-start | bytes 24584 | tf_op jit(solution)/shard_map/ppermute | solution.py:61
  71.0 10.4 %collective-permute-start.4 = (f32[16,128]{1,0:T(8,128)}, f32[16,128]{1,0:T(8,128)S(1)}, u32[]{:S(2)}, u32[]{:S(2)}) collective-permute-start(f32[16,128]{1,0:T(8,128)} %get-tuple-element.14), channel_id=1, source_target_pairs={{0,64},{1,65},{2,66},{3,67},{4,68},{5,69},{6,70},{7,71},{8,72},{9,... | collective-permute-start | bytes 24584 | tf_op jit(solution)/shard_map/ppermute | solution.py:61
  71.6 32.7 %collective-permute-start.5 = (f32[16,128]{1,0:T(8,128)}, f32[16,128]{1,0:T(8,128)S(1)}, u32[]{:S(2)}, u32[]{:S(2)}) collective-permute-start(f32[16,128]{1,0:T(8,128)} %get-tuple-element.14), channel_id=1, source_target_pairs={{0,96},{1,97},{2,98},{3,99},{4,100},{5,101},{6,102},{7,103},{8,104... | collective-permute-start | bytes 24584 | tf_op jit(solution)/shard_map/ppermute | solution.py:61
  78.7 26.2 %collective-permute-start.9 = (f32[2048]{0:T(1024)S(1)}, f32[2048]{0:T(1024)S(1)}, u32[]{:S(2)}, u32[]{:S(2)}) collective-permute-start(f32[2048]{0:T(1024)S(1)} %convolution_bitcast_fusion), channel_id=1, source_target_pairs={{0,32},{1,33},{2,34},{3,35},{4,36},{5,37},{6,38},{7,39},{8,40},{9,... | collective-permute-start | bytes 24584 | tf_op jit(solution)/shard_map/ppermute | solution.py:61
  79.4 25.5 %collective-permute-start.7 = (f32[2048]{0:T(1024)S(1)}, f32[2048]{0:T(1024)S(1)}, u32[]{:S(2)}, u32[]{:S(2)}) collective-permute-start(f32[2048]{0:T(1024)S(1)} %convolution_bitcast_fusion), channel_id=1, source_target_pairs={{0,64},{1,65},{2,66},{3,67},{4,68},{5,69},{6,70},{7,71},{8,72},{9,... | collective-permute-start | bytes 24584 | tf_op jit(solution)/shard_map/ppermute | solution.py:61
  80.1 35.0 %collective-permute-start.8 = (f32[2048]{0:T(1024)S(1)}, f32[2048]{0:T(1024)S(1)}, u32[]{:S(2)}, u32[]{:S(2)}) collective-permute-start(f32[2048]{0:T(1024)S(1)} %convolution_bitcast_fusion), channel_id=1, source_target_pairs={{0,96},{1,97},{2,98},{3,99},{4,100},{5,101},{6,102},{7,103},{8,104... | collective-permute-start | bytes 24584 | tf_op jit(solution)/shard_map/ppermute | solution.py:61

commit v9 on v8

--- a/solution.py
+++ b/solution.py
@@ -161,7 +161,7 @@
 
 def run_steps(parts, lists_ref, forcing_ref, surface_ref, table_ref):
     def part(slot):
-        return parts[(slot - 2) % 3].at[(slot - 2) // 3]
+        return parts[(slot - 2) // 3].at[(slot - 2) % 3]
 
     def spread(left, largest):
         largest = jnp.max(jnp.max(largest, axis=1, keepdims=True), axis=0, keepdims=True)
@@ -224,7 +224,7 @@
     for k in range(WINDOW):
         for j in range(2):
             terms_ref[pl.ds(j, OWNERS, stride=2), :] = arrived_ref[:, TERMS + 2 * k + j, :]
-        target = parts[k % 3][k // 3, TARGET : TARGET + 1, 0:TILES].astype(I32)
+        target = parts[k // 3][k % 3, TARGET : TARGET + 1, 0:TILES].astype(I32)
         hot = (blocks == target).astype(F32)
         forcing_ref[k] = jnp.dot(hot, terms_ref[...], precision=HIGHEST, preferred_element_type=F32)
     run_steps(parts, lists_ref, forcing_ref, surface_ref, table_ref)
@@ -280,7 +280,7 @@
         tile_target.reshape(1, TILES),
     )
     shares = lax.all_to_all(partials, "comp", split_axis=0, concat_axis=0, tiled=True)
-    lower, higher = from_owner(packed, -3), from_owner(packed, 3)
+    lower, higher = from_owner(packed, -1), from_owner(packed, 1)
     three = jnp.concatenate([lower, packed, higher], axis=0)
     terms = pl.pallas_call(
         terms_kernel,
@@ -289,7 +289,7 @@
         scratch_shapes=[pltpu.VMEM((16, 8, LANES), F32), pltpu.VMEM((TILES + 2 * WINDOW, LANES), F32)],
     )(tile_source, shares, packed, tile_weight)
     arrived = exchange(terms)
-    lower, higher = from_owner(three, -1), from_owner(three, 1)
+    lower, higher = from_owner(three, -3), from_owner(three, 3)
     window = [block.reshape(3, PART, LANES) for block in (lower, three, higher)]
     surface, lists, forcing = pl.pallas_call(
         first_kernel,

time: 116 us -> 116 us (level)
  no operation moved by 1% of the time
where the time goes in v9:
time: 116 us; the launch traced here: 115 us
  waiting for transfers between devices  45.5 us (39%)
  blocking collectives  23 us (20%)
  starting transfers between devices  21.6 us (19%)
  Pallas kernels  20.7 us (18%)
  other arithmetic  2.38 us (2%)
    ppermute x6, waiting for transfers between devices, to_idle(): arrived.append(lax.ppermute(block, BOTH, route))  32.5 us
    all_to_all x1, blocking collectives, exchange(): lax.all_to_all(blocks, BOTH, split_axis=0, concat_axis=0, tiled=True, axi...  14 us
    all_to_all x2, waiting for transfers between devices, exchange(): lax.all_to_all(blocks, BOTH, split_axis=0, concat_axis=0, tiled=True, axi...  12.9 us
    all_to_all x2, starting transfers between devices, exchange(): lax.all_to_all(blocks, BOTH, split_axis=0, concat_axis=0, tiled=True, axi...  12.8 us
    all_to_all x1, blocking collectives, local(): lax.all_to_all(partials, 'comp', split_axis=0, concat_axis=0, tiled=True)  8.93 us
    pallas_call x1, Pallas kernels, local(): pl.pallas_call(first_kernel, out_shape=(shape(OWNERS, 16, LANES), shape(S...  7.99 us
    pallas_call x1, Pallas kernels, local(): pl.pallas_call(last_kernel, out_shape=(shape(16, LANES), shape(OWNERS, 2,...  7.68 us
    ppermute x6, starting transfers between devices, to_idle(): arrived.append(lax.ppermute(block, BOTH, route))  5.23 us
  transfers between devices with their start and end apart: 12, of which 4 were waited for; matrix products, arithmetic and copies ran while one was open for 2% of the time, Pallas kernels for 0%

profile of v9, /device:TPU:65, one launch (start us, length us, event | category | flops | bytes accessed | tf_op | source)
XLA Modules:
  0.0 115.1 jit_solution(8698187859640458258)
XLA Ops:
  0.6 1.7 %shard_map.113 = (f32[8,16,128]{2,1,0:T(8,128)}, f32[232,128]{1,0:T(8,128)}) custom-call(f32[9]{0:T(128)} %weight_ref.2, bf16[9,2048]{1,0:T(8,128)(2,1)} %flux_ref.1, s32[6,2048]{1,0:T(8,128)} %neighbor_ref.1, f32[6,2048]{1,0:T(8,128)} %conduct_ref.1, f32[16,128]{1,0:T(8,128)} %bitcast.18, f32[16,128]{1,0:T(8,128)} %bitcast.19, s32[2,256]{1,0:T(2,128)} %lists_ref.1, ...), custom_call_target="tpu_custom_call" | custom-call | tf_op jit(solution)/shard_map/pallas_call | solution.py:267
  2.4 8.9 %all_to_all.20.shares_ref = f32[8,16,128]{2,1,0:T(8,128)} all-to-all(f32[8,16,128]{2,1,0:T(8,128)} %get-tuple-element.9), channel_id=1, replica_groups=mesh['comp'=8,'cells'=32] {'comp'}, dimensions={0} | all-to-all | bytes 131072 | tf_op jit(solution)/shard_map/all_to_all | solution.py:282
  11.3 3.3 %shard_map.114 = f32[32,40,128]{2,1,0:T(8,128)} custom-call(s32[64]{0:T(128)} %source_ref.1, f32[8,16,128]{2,1,0:T(8,128)} %all_to_all.20.shares_ref, f32[232,128]{1,0:T(8,128)} %get-tuple-element.10.packed_ref, bf16[64,128,128]{2,1,0:T(8,128)(2,1)} %weight_ref.3), custom_call_target="tpu_custom_call" | custom-call | tf_op jit(solution)/shard_map/pallas_call | solution.py:285
  14.6 8.0 %all-to-all-start.1 = ((f32[32,40,128]{2,1,0:T(8,128)}), f32[32,40,128]{2,1,0:T(8,128)S(1)}, u32[]{:S(2)}, u32[]{:S(2)}) async-start(f32[32,40,128]{2,1,0:T(8,128)} %shard_map.114), calls=%async_computation.1 | async-start | bytes 1310720 | tf_op jit(solution)/shard_map/all_to_all | solution.py:67
  22.6 0.7 collective-permute-start
  23.3 0.7 collective-permute-start.1
  24.0 0.0 collective-permute-done
  24.0 0.0 copy-start
  24.1 0.8 collective-permute-start.2
  24.9 1.4 %collective-permute-start.3 = (f32[696,128]{1,0:T(8,128)S(1)}, f32[696,128]{1,0:T(8,128)}, u32[]{:S(2)}, u32[]{:S(2)}) collective-permute-start(f32[696,128]{1,0:T(8,128)S(1)} %constant_dynamic-update-slice_fusion), channel_id=1, source_target_pairs={{3,0},{4,1},{5,2},{6,3},{7,4},{8,5},{9,6},{10,7},{11,8},{12,9},{13... | collective-permute-start | bytes 1069064 | tf_op jit(solution)/shard_map/ppermute | solution.py:50
  26.3 0.0 collective-permute-done.2
  26.3 8.6 %all-to-all-done.1.arrived_ref = f32[32,40,128]{2,1,0:T(8,128)S(1)} async-done(((f32[32,40,128]{2,1,0:T(8,128)}), f32[32,40,128]{2,1,0:T(8,128)S(1)}, u32[]{:S(2)}, u32[]{:S(2)}) %all-to-all-start.1) | async-done | bytes 655392 | tf_op jit(solution)/shard_map/all_to_all | solution.py:67
  34.9 0.9 copy-done.1
  35.8 8.0 %shard_map.115 = (f32[32,16,128]{2,1,0:T(8,128)}, f32[13,8,128]{2,1,0:T(8,128)}, f32[9,16,128]{2,1,0:T(8,128)}) custom-call(s32[1]{0:T(128)} %bitcast.owner_ref, f32[32,40,128]{2,1,0:T(8,128)} %copy-done.1, f32[3,232,128]{2,1,0:T(8,128)} %bitcast.15, f32[3,232,128]{2,1,0:T(8,128)} %bitcast.13, f32[3,232,128]{2,1,0:T(8,128)} %bitcast.6.high_ref), custom_call_target="tpu_custom_call" | custom-call | tf_op jit(solution)/shard_map/pallas_call | solution.py:294
  43.7 14.0 %all_to_all.21.surfaces_ref = f32[32,16,128]{2,1,0:T(8,128)} all-to-all(f32[32,16,128]{2,1,0:T(8,128)} %get-tuple-element.11), channel_id=1, replica_groups={{0,1,2,3,4,5,6,7,8,9,10,11,12,13,14,15,208,209,210,211,212,213,214,215,..., dimensions={0} | all-to-all | bytes 524288 | tf_op jit(solution)/shard_map/all_to_all | solution.py:67
  57.8 7.7 %shard_map.116 = (f32[16,128]{1,0:T(8,128)}, f32[32,2,128]{2,1,0:T(2,128)}) custom-call(s32[1]{0:T(128)} %bitcast.owner_ref, s32[64]{0:T(128)} %target_ref.1, f32[32,16,128]{2,1,0:T(8,128)} %all_to_all.21.surfaces_ref, f32[3,232,128]{2,1,0:T(8,128)} %bitcast.16, f32[3,232,128]{2,1,0:T(8,128)} %bitcast.14, f32[3,232,128]{2,1,0:T(8,128)} %bitcast.6.high_ref, ...), custom_call_target="tpu_custom_call" | custom-call | tf_op jit(solution)/shard_map/pallas_call | solution.py:301
  65.5 4.8 %all-to-all-start.3 = ((f32[32,2,128]{2,1,0:T(2,128)}), f32[32,2,128]{2,1,0:T(2,128)S(1)}, u32[]{:S(2)}, u32[]{:S(2)}) async-start(f32[32,2,128]{2,1,0:T(2,128)} %get-tuple-element.15), calls=%async_computation.3 | async-start | bytes 65536 | tf_op jit(solution)/shard_map/all_to_all | solution.py:67
  70.3 0.7 collective-permute-start.6
  71.0 0.7 collective-permute-start.4
  71.6 1.3 %collective-permute-start.5 = (f32[16,128]{1,0:T(8,128)}, f32[16,128]{1,0:T(8,128)S(1)}, u32[]{:S(2)}, u32[]{:S(2)}) collective-permute-start(f32[16,128]{1,0:T(8,128)} %get-tuple-element.14), channel_id=1, source_target_pairs={{0,96},{1,97},{2,98},{3,99},{4,100},{5,101},{6,102},{7,103},{8,104... | collective-permute-start | bytes 24584 | tf_op jit(solution)/shard_map/ppermute | solution.py:61
  72.9 4.3 %all-to-all-done.3 = f32[32,2,128]{2,1,0:T(2,128)S(1)} async-done(((f32[32,2,128]{2,1,0:T(2,128)}), f32[32,2,128]{2,1,0:T(2,128)S(1)}, u32[]{:S(2)}, u32[]{:S(2)}) %all-to-all-start.3) | async-done | bytes 32800 | tf_op jit(solution)/shard_map/all_to_all | solution.py:67
  77.3 1.2 %multiply_reduce_fusion = f32[64,128]{1,0:T(8,128)S(1)} fusion(bf16[64,128,128]{2,1,0:T(8,128)(2,1)S(1)} %copy-done, f32[64,128]{1,0:T(8,128)S(1)} %bitcast.17), kind=kLoop, calls=%fused_computation | loop fusion | flops 3137536 | bytes 2162688 | tf_op jit(solution)/shard_map/reduce_sum | solution.py:309
  78.4 0.3 convolution_bitcast_fusion
  78.7 0.7 collective-permute-start.9
  79.4 0.7 collective-permute-start.7
  80.0 0.0 collective-permute-done.6
  80.1 1.3 %collective-permute-start.8 = (f32[2048]{0:T(1024)S(1)}, f32[2048]{0:T(1024)S(1)}, u32[]{:S(2)}, u32[]{:S(2)}) collective-permute-start(f32[2048]{0:T(1024)S(1)} %convolution_bitcast_fusion), channel_id=1, source_target_pairs={{0,96},{1,97},{2,98},{3,99},{4,100},{5,101},{6,102},{7,103},{8,104... | collective-permute-start | bytes 24584 | tf_op jit(solution)/shard_map/ppermute | solution.py:61
  81.4 0.0 collective-permute-done.4
  81.4 22.4 %collective-permute-done.5 = f32[16,128]{1,0:T(8,128)S(1)} collective-permute-done((f32[16,128]{1,0:T(8,128)}, f32[16,128]{1,0:T(8,128)S(1)}, u32[]{:S(2)}, u32[]{:S(2)}) %collective-permute-start.5) | collective-permute-done | bytes 8224 | tf_op jit(solution)/shard_map/ppermute | solution.py:61
  103.7 0.6 select_bitcast_fusion
  104.4 10.2 %collective-permute-done.8 = f32[2048]{0:T(1024)S(1)} collective-permute-done((f32[2048]{0:T(1024)S(1)}, f32[2048]{0:T(1024)S(1)}, u32[]{:S(2)}, u32[]{:S(2)}) %collective-permute-start.8) | collective-permute-done | bytes 8224 | tf_op jit(solution)/shard_map/ppermute | solution.py:61
  114.5 0.6 add_select_fusion
  (19 shorter events, 0.1 us)
Async XLA Ops:
  11.3 11.3 %copy-start.4 = (f32[232,128]{1,0:T(8,128)S(1)}, f32[232,128]{1,0:T(8,128)}, u32[]{:S(2)}) copy-start(f32[232,128]{1,0:T(8,128)} %get-tuple-element.10.packed_ref) | copy-start | bytes 356356
  14.6 20.3 %all-to-all-start.1 = ((f32[32,40,128]{2,1,0:T(8,128)}), f32[32,40,128]{2,1,0:T(8,128)S(1)}, u32[]{:S(2)}, u32[]{:S(2)}) async-start(f32[32,40,128]{2,1,0:T(8,128)} %shard_map.114), calls=%async_computation.1 | async-start | bytes 1310720 | tf_op jit(solution)/shard_map/all_to_all | solution.py:67
  22.6 1.4 %collective-permute-start = (f32[232,128]{1,0:T(8,128)S(1)}, f32[232,128]{1,0:T(8,128)S(1)}, u32[]{:S(2)}, u32[]{:S(2)}) collective-permute-start(f32[232,128]{1,0:T(8,128)S(1)} %copy-done.4), channel_id=1, source_target_pairs={{223,0},{0,1},{1,2},{2,3},{3,4},{4,5},{5,6},{6,7},{7,8},{8,9},{9,1... | collective-permute-start | bytes 356360 | tf_op jit(solution)/shard_map/ppermute | solution.py:50
  23.3 0.7 collective-permute-start.1
  24.0 53.3 %copy-start = (bf16[64,128,128]{2,1,0:T(8,128)(2,1)S(1)}, bf16[64,128,128]{2,1,0:T(8,128)(2,1)}, u32[]{:S(2)}) copy-start(bf16[64,128,128]{2,1,0:T(8,128)(2,1)} %weight_ref.3) | copy-start | bytes 6291460
  24.1 10.8 %copy-start.2 = (f32[696,128]{1,0:T(8,128)}, f32[696,128]{1,0:T(8,128)S(1)}, u32[]{:S(2)}) copy-start(f32[696,128]{1,0:T(8,128)S(1)} %constant_dynamic-update-slice_fusion) | copy-start | bytes 1069060
  24.1 2.2 %collective-permute-start.2 = (f32[696,128]{1,0:T(8,128)S(1)}, f32[696,128]{1,0:T(8,128)S(1)}, u32[]{:S(2)}, u32[]{:S(2)}) collective-permute-start(f32[696,128]{1,0:T(8,128)S(1)} %constant_dynamic-update-slice_fusion), channel_id=1, source_target_pairs={{221,0},{222,1},{223,2},{0,3},{1,4},{2,5},{3,6},{4,7},{5,8},{6,9},... | collective-permute-start | bytes 1069064 | tf_op jit(solution)/shard_map/ppermute | solution.py:50
  24.9 1.4 %collective-permute-start.3 = (f32[696,128]{1,0:T(8,128)S(1)}, f32[696,128]{1,0:T(8,128)}, u32[]{:S(2)}, u32[]{:S(2)}) collective-permute-start(f32[696,128]{1,0:T(8,128)S(1)} %constant_dynamic-update-slice_fusion), channel_id=1, source_target_pairs={{3,0},{4,1},{5,2},{6,3},{7,4},{8,5},{9,6},{10,7},{11,8},{12,9},{13... | collective-permute-start | bytes 1069064 | tf_op jit(solution)/shard_map/ppermute | solution.py:50
  26.3 8.6 %copy-start.3 = (f32[696,128]{1,0:T(8,128)}, f32[696,128]{1,0:T(8,128)S(1)}, u32[]{:S(2)}) copy-start(f32[696,128]{1,0:T(8,128)S(1)} %collective-permute-done.2) | copy-start | bytes 1069060
  34.9 0.9 copy-start.1
  43.7 34.7 %copy-start.6 = (s32[64]{0:T(128)S(1)}, s32[64]{0:T(128)}, u32[]{:S(2)}) copy-start(s32[64]{0:T(128)} %source_ref.1) | copy-start | bytes 772
  65.5 38.3 %copy-start.5 = (f32[16,128]{1,0:T(8,128)S(1)}, f32[16,128]{1,0:T(8,128)}, u32[]{:S(2)}) copy-start(f32[16,128]{1,0:T(8,128)} %get-tuple-element.14) | copy-start | bytes 24580
  65.5 11.8 %all-to-all-start.3 = ((f32[32,2,128]{2,1,0:T(2,128)}), f32[32,2,128]{2,1,0:T(2,128)S(1)}, u32[]{:S(2)}, u32[]{:S(2)}) async-start(f32[32,2,128]{2,1,0:T(2,128)} %get-tuple-element.15), calls=%async_computation.3 | async-start | bytes 65536 | tf_op jit(solution)/shard_map/all_to_all | solution.py:67
  70.3 9.8 %collective-permute-start.6 = (f32[16,128]{1,0:T(8,128)}, f32[16,128]{1,0:T(8,128)S(1)}, u32[]{:S(2)}, u32[]{:S(2)}) collective-permute-start(f32[16,128]{1,0:T(8,128)} %get-tuple-element.14), channel_id=1, source_target_pairs={{0,32},{1,33},{2,34},{3,35},{4,36},{5,37},{6,38},{7,39},{8,40},{9,... | collective-permute-start | bytes 24584 | tf_op jit(solution)/shard_map/ppermute | solution.py:61
  71.0 10.4 %collective-permute-start.4 = (f32[16,128]{1,0:T(8,128)}, f32[16,128]{1,0:T(8,128)S(1)}, u32[]{:S(2)}, u32[]{:S(2)}) collective-permute-start(f32[16,128]{1,0:T(8,128)} %get-tuple-element.14), channel_id=1, source_target_pairs={{0,64},{1,65},{2,66},{3,67},{4,68},{5,69},{6,70},{7,71},{8,72},{9,... | collective-permute-start | bytes 24584 | tf_op jit(solution)/shard_map/ppermute | solution.py:61
  71.6 32.1 %collective-permute-start.5 = (f32[16,128]{1,0:T(8,128)}, f32[16,128]{1,0:T(8,128)S(1)}, u32[]{:S(2)}, u32[]{:S(2)}) collective-permute-start(f32[16,128]{1,0:T(8,128)} %get-tuple-element.14), channel_id=1, source_target_pairs={{0,96},{1,97},{2,98},{3,99},{4,100},{5,101},{6,102},{7,103},{8,104... | collective-permute-start | bytes 24584 | tf_op jit(solution)/shard_map/ppermute | solution.py:61
  78.7 25.6 %collective-permute-start.9 = (f32[2048]{0:T(1024)S(1)}, f32[2048]{0:T(1024)S(1)}, u32[]{:S(2)}, u32[]{:S(2)}) collective-permute-start(f32[2048]{0:T(1024)S(1)} %convolution_bitcast_fusion), channel_id=1, source_target_pairs={{0,32},{1,33},{2,34},{3,35},{4,36},{5,37},{6,38},{7,39},{8,40},{9,... | collective-permute-start | bytes 24584 | tf_op jit(solution)/shard_map/ppermute | solution.py:61
  79.4 25.0 %collective-permute-start.7 = (f32[2048]{0:T(1024)S(1)}, f32[2048]{0:T(1024)S(1)}, u32[]{:S(2)}, u32[]{:S(2)}) collective-permute-start(f32[2048]{0:T(1024)S(1)} %convolution_bitcast_fusion), channel_id=1, source_target_pairs={{0,64},{1,65},{2,66},{3,67},{4,68},{5,69},{6,70},{7,71},{8,72},{9,... | collective-permute-start | bytes 24584 | tf_op jit(solution)/shard_map/ppermute | solution.py:61
  80.1 34.5 %collective-permute-start.8 = (f32[2048]{0:T(1024)S(1)}, f32[2048]{0:T(1024)S(1)}, u32[]{:S(2)}, u32[]{:S(2)}) collective-permute-start(f32[2048]{0:T(1024)S(1)} %convolution_bitcast_fusion), channel_id=1, source_target_pairs={{0,96},{1,97},{2,98},{3,99},{4,100},{5,101},{6,102},{7,103},{8,104... | collective-permute-start | bytes 24584 | tf_op jit(solution)/shard_map/ppermute | solution.py:61

commit v10 on v7

--- a/solution.py
+++ b/solution.py
@@ -15,8 +15,8 @@
 WINDOW = 2 * REACH + 1
 CENTER = REACH + 2
 SLOTS = WINDOW + 4
-PART = 232
-CONDUCT, KEEP, START, LISTS, TARGET = 96, 192, 208, 224, 228
+PART = 216
+CONDUCT, KEEP, TARGET = 96, 192, 208
 SENT = 40
 TERMS = 22
 BOTH = ("comp", "cells")
@@ -103,7 +103,7 @@
     return jnp.where((code & 128) == 0, total, total << 16) >> 16
 
 
-def prepare_kernel(weight_ref, flux_ref, neighbor_ref, conduct_ref, damping_ref, start_ref, lists_ref, target_ref, shares_ref, packed_ref, row_ref):
+def prepare_kernel(weight_ref, flux_ref, neighbor_ref, conduct_ref, damping_ref, start_ref, lists_ref, target_ref, shares_ref, packed_ref, fixed_ref, row_ref):
     for j in range(16):
         lanes = slice(LANES * j, LANES * j + LANES)
         block = flux_ref[:, lanes].astype(F32)
@@ -116,17 +116,18 @@
         conduct = conduct_ref[:, lanes]
         own[pl.ds(CONDUCT + j, 6, stride=16), :] = conduct
         own[KEEP + j : KEEP + j + 1] = 1.0 - jnp.sum(conduct, axis=0, keepdims=True) - damping_ref[j : j + 1]
-    own[START:LISTS] = start_ref[...]
+    fixed_ref[0:16] = start_ref[...]
     for j in range(2):
         lanes = slice(LANES * j, LANES * j + LANES)
         lists = coded(lists_ref[:, lanes]).astype(F32)
-        own[LISTS + j : LISTS + j + 1] = lists[0:1]
-        own[LISTS + 2 + j : LISTS + 3 + j] = lists[1:2]
+        fixed_ref[16 + j : 17 + j] = lists[0:1]
+        fixed_ref[18 + j : 19 + j] = lists[1:2]
+    fixed_ref[20:24] = jnp.zeros((4, LANES), F32)
     own[TARGET:PART] = jnp.zeros((PART - TARGET, LANES), F32)
     own[TARGET : TARGET + 1, 0:TILES] = target_ref[...].astype(F32)
 
 
-def terms_kernel(source_ref, shares_ref, packed_ref, weight_ref, out_ref, parts_ref, terms_ref):
+def terms_kernel(source_ref, shares_ref, fixed_ref, weight_ref, out_ref, parts_ref, terms_ref):
     flux = jnp.sum(shares_ref[...], axis=0)
     high = flux.astype(jnp.bfloat16).astype(F32)
     rest = flux - high
@@ -143,7 +144,7 @@
         while place < TILES + 2 * WINDOW:
             terms_ref[place : place + 1] = term
             place += TILES
-    fixed = packed_ref[START : START + 24]
+    fixed = fixed_ref[...]
     for p in range(OWNERS):
         out_ref[p, 0:24] = fixed
         out_ref[p, TERMS:SENT] = terms_ref[2 * p : 2 * p + 2 * WINDOW]
@@ -261,9 +262,9 @@
         pltpu.VMEM((SLOTS, 16, LANES), I32),
     ]
 
-    partials, packed = pl.pallas_call(
+    partials, packed, fixed = pl.pallas_call(
         prepare_kernel,
-        out_shape=(shape(8, 16, LANES), shape(PART, LANES)),
+        out_shape=(shape(8, 16, LANES), shape(PART, LANES), shape(24, LANES)),
         in_specs=[SMEM] + [VMEM] * 7,
         scratch_shapes=[pltpu.VMEM((16, LANES), F32)],
     )(
@@ -284,7 +285,7 @@
         out_shape=shape(OWNERS, SENT, LANES),
         in_specs=[SMEM] + [VMEM] * 3,
         scratch_shapes=[pltpu.VMEM((16, 8, LANES), F32), pltpu.VMEM((TILES + 2 * WINDOW, LANES), F32)],
-    )(tile_source, shares, packed, tile_weight)
+    )(tile_source, shares, fixed, tile_weight)
     arrived = exchange(terms)
     lower, higher = from_owner(three, -3), from_owner(three, 3)
     window = [block.reshape(3, PART, LANES) for block in (lower, three, higher)]
@@ -301,8 +302,10 @@
         in_specs=[SMEM] * 2 + [VMEM] * 6,
         scratch_shapes=scratch,
     )(owner, tile_target, surfaces, *window, lists, forcing)
+    returned = exchange(values)
     ocean_end = to_idle(ocean_end)
-    returned = exchange(values).reshape(TILES, LANES)
+    returned, ocean_end = lax.optimization_barrier((returned, ocean_end))
+    returned = returned.reshape(TILES, LANES)
     pulled = jnp.sum(returned[:, None, :] * tile_weight.astype(F32), axis=2)
     source_hot = (tile_source[:, None] == jnp.arange(16, dtype=I32)[None, :]).astype(F32)
     atm_back = jnp.einsum("ra,rb->ab", source_hot, pulled, precision=HIGHEST).reshape(-1)

time: 115 us -> 115 us (level)
    select_n x1 -> x2, other arithmetic: 0.6 us -> 1.91 us  [to_idle(): jnp.where((z_low == 0) | (z_low == 3), block, lax.ppermute(block, BOTH, r...]
  transfers between devices with their start and end apart: 8 -> 8, of which waited for: 6 -> 6; matrix products, arithmetic and copies ran while one was open for 2% -> 1% of each run, Pallas kernels for 0% -> 0%
where the time goes in v10:
time: 115 us; the launch traced here: 113 us
  blocking collectives  34.5 us (30%)
  starting transfers between devices  33.6 us (29%)
  Pallas kernels  20.6 us (18%)
  waiting for transfers between devices  19.5 us (17%)
  other arithmetic  3.08 us (3%)
    all_to_all x1, blocking collectives, exchange(): lax.all_to_all(blocks, BOTH, split_axis=0, concat_axis=0, tiled=True, axi...  22.6 us
    ppermute x4, starting transfers between devices, from_owner(): return lax.ppermute(block, BOTH, route)  15.9 us
    all_to_all x2, starting transfers between devices, exchange(): lax.all_to_all(blocks, BOTH, split_axis=0, concat_axis=0, tiled=True, axi...  15.1 us
    all_to_all x1, blocking collectives, local(): lax.all_to_all(partials, 'comp', split_axis=0, concat_axis=0, tiled=True)  11.9 us
    ppermute x4, waiting for transfers between devices, from_owner(): return lax.ppermute(block, BOTH, route)  11.2 us
    pallas_call x1, Pallas kernels, local(): pl.pallas_call(first_kernel, out_shape=(shape(OWNERS, 16, LANES), shape(S...  7.93 us
    pallas_call x1, Pallas kernels, local(): pl.pallas_call(last_kernel, out_shape=(shape(16, LANES), shape(OWNERS, 2,...  7.66 us
    all_to_all x2, waiting for transfers between devices, exchange(): lax.all_to_all(blocks, BOTH, split_axis=0, concat_axis=0, tiled=True, axi...  6.99 us
  transfers between devices with their start and end apart: 8, of which 6 were waited for; matrix products, arithmetic and copies ran while one was open for 1% of the time, Pallas kernels for 0%

profile of v10, /device:TPU:2, one launch (start us, length us, event | category | flops | bytes accessed | tf_op | source)
XLA Modules:
  0.0 113.3 jit_solution(14730284128425342183)
XLA Ops:
  0.6 1.7 %shard_map.113 = (f32[8,16,128]{2,1,0:T(8,128)}, f32[216,128]{1,0:T(8,128)}, f32[24,128]{1,0:T(8,128)}) custom-call(f32[9]{0:T(128)} %weight_ref.2, bf16[9,2048]{1,0:T(8,128)(2,1)} %flux_ref.1, s32[6,2048]{1,0:T(8,128)} %neighbor_ref.1, f32[6,2048]{1,0:T(8,128)} %conduct_ref.1, f32[16,128]{1,0:T(8,128)} %bitcast.18, f32[16,128]{1,0:T(8,128)} %bitcast.19, ...), custom_call_target="tpu_custom_call" | custom-call | tf_op jit(solution)/shard_map/pallas_call | solution.py:265
  2.4 11.9 %all_to_all.20.shares_ref = f32[8,16,128]{2,1,0:T(8,128)} all-to-all(f32[8,16,128]{2,1,0:T(8,128)} %get-tuple-element.12), channel_id=1, replica_groups=mesh['comp'=8,'cells'=32] {'comp'}, dimensions={0} | all-to-all | bytes 131072 | tf_op jit(solution)/shard_map/all_to_all | solution.py:280
  14.3 3.3 %shard_map.114 = f32[32,40,128]{2,1,0:T(8,128)} custom-call(s32[64]{0:T(128)} %source_ref.1, f32[8,16,128]{2,1,0:T(8,128)} %all_to_all.20.shares_ref, f32[24,128]{1,0:T(8,128)} %get-tuple-element.13.fixed_ref, bf16[64,128,128]{2,1,0:T(8,128)(2,1)} %weight_ref.3), custom_call_target="tpu_custom_call" | custom-call | tf_op jit(solution)/shard_map/pallas_call | solution.py:283
  17.5 9.8 %all-to-all-start.1 = ((f32[32,40,128]{2,1,0:T(8,128)}), f32[32,40,128]{2,1,0:T(8,128)S(1)}, u32[]{:S(2)}, u32[]{:S(2)}) async-start(f32[32,40,128]{2,1,0:T(8,128)} %shard_map.114), calls=%async_computation.1 | async-start | bytes 1310720 | tf_op jit(solution)/shard_map/all_to_all | solution.py:64
  27.3 0.0 copy-done.4
  27.4 3.4 %collective-permute-start = (f32[216,128]{1,0:T(8,128)S(1)}, f32[216,128]{1,0:T(8,128)S(1)}, u32[]{:S(2)}, u32[]{:S(2)}) collective-permute-start(f32[216,128]{1,0:T(8,128)S(1)} %copy-done.4), channel_id=1, source_target_pairs={{223,0},{0,1},{1,2},{2,3},{3,4},{4,5},{5,6},{6,7},{7,8},{8,9},{9,1... | collective-permute-start | bytes 331784 | tf_op jit(solution)/shard_map/ppermute | solution.py:49
  30.7 2.5 %collective-permute-start.1 = (f32[216,128]{1,0:T(8,128)S(1)}, f32[216,128]{1,0:T(8,128)S(1)}, u32[]{:S(2)}, u32[]{:S(2)}) collective-permute-start(f32[216,128]{1,0:T(8,128)S(1)} %copy-done.4), channel_id=1, source_target_pairs={{1,0},{2,1},{3,2},{4,3},{5,4},{6,5},{7,6},{8,7},{9,8},{10,9},{11,1... | collective-permute-start | bytes 331784 | tf_op jit(solution)/shard_map/ppermute | solution.py:49
  33.2 4.0 %collective-permute-done = f32[216,128]{1,0:T(8,128)S(1)} collective-permute-done((f32[216,128]{1,0:T(8,128)S(1)}, f32[216,128]{1,0:T(8,128)S(1)}, u32[]{:S(2)}, u32[]{:S(2)}) %collective-permute-start) | collective-permute-done | bytes 110624 | tf_op jit(solution)/shard_map/ppermute | solution.py:49
  37.3 0.0 copy-start
  37.3 1.4 %collective-permute-done.1 = f32[216,128]{1,0:T(8,128)S(1)} collective-permute-done((f32[216,128]{1,0:T(8,128)S(1)}, f32[216,128]{1,0:T(8,128)S(1)}, u32[]{:S(2)}, u32[]{:S(2)}) %collective-permute-start.1) | collective-permute-done | bytes 110624 | tf_op jit(solution)/shard_map/ppermute | solution.py:49
  38.7 0.0 copy-start.2
  38.7 4.5 %collective-permute-start.2 = (f32[648,128]{1,0:T(8,128)S(1)}, f32[648,128]{1,0:T(8,128)S(1)}, u32[]{:S(2)}, u32[]{:S(2)}) collective-permute-start(f32[648,128]{1,0:T(8,128)S(1)} %constant_dynamic-update-slice_fusion), channel_id=1, source_target_pairs={{221,0},{222,1},{223,2},{0,3},{1,4},{2,5},{3,6},{4,7},{5,8},{6,9},... | collective-permute-start | bytes 995336 | tf_op jit(solution)/shard_map/ppermute | solution.py:49
  43.2 5.6 %collective-permute-start.3 = (f32[648,128]{1,0:T(8,128)S(1)}, f32[648,128]{1,0:T(8,128)}, u32[]{:S(2)}, u32[]{:S(2)}) collective-permute-start(f32[648,128]{1,0:T(8,128)S(1)} %constant_dynamic-update-slice_fusion), channel_id=1, source_target_pairs={{3,0},{4,1},{5,2},{6,3},{7,4},{8,5},{9,6},{10,7},{11,8},{12,9},{13... | collective-permute-start | bytes 995336 | tf_op jit(solution)/shard_map/ppermute | solution.py:49
  48.8 4.6 %collective-permute-done.2 = f32[648,128]{1,0:T(8,128)S(1)} collective-permute-done((f32[648,128]{1,0:T(8,128)S(1)}, f32[648,128]{1,0:T(8,128)S(1)}, u32[]{:S(2)}, u32[]{:S(2)}) %collective-permute-start.2) | collective-permute-done | bytes 331808 | tf_op jit(solution)/shard_map/ppermute | solution.py:49
  53.4 1.2 %collective-permute-done.3 = f32[648,128]{1,0:T(8,128)} collective-permute-done((f32[648,128]{1,0:T(8,128)S(1)}, f32[648,128]{1,0:T(8,128)}, u32[]{:S(2)}, u32[]{:S(2)}) %collective-permute-start.3) | collective-permute-done | bytes 331808 | tf_op jit(solution)/shard_map/ppermute | solution.py:49
  54.6 0.0 all-to-all-done.1.arrived_ref
  54.6 0.0 copy-done.2
  54.6 0.0 copy-done.3
  54.6 0.8 copy-done.1
  55.4 7.9 %shard_map.115 = (f32[32,16,128]{2,1,0:T(8,128)}, f32[13,8,128]{2,1,0:T(8,128)}, f32[9,16,128]{2,1,0:T(8,128)}) custom-call(s32[1]{0:T(128)} %bitcast.owner_ref, f32[32,40,128]{2,1,0:T(8,128)} %copy-done.1, f32[3,216,128]{2,1,0:T(8,128)} %bitcast.14, f32[3,216,128]{2,1,0:T(8,128)} %bitcast.12, f32[3,216,128]{2,1,0:T(8,128)} %bitcast.6.high_ref), custom_call_target="tpu_custom_call" | custom-call | tf_op jit(solution)/shard_map/pallas_call | solution.py:292
  63.4 22.6 %all_to_all.21.surfaces_ref = f32[32,16,128]{2,1,0:T(8,128)} all-to-all(f32[32,16,128]{2,1,0:T(8,128)} %get-tuple-element.15), channel_id=1, replica_groups={{0,1,2,3,4,5,6,7,8,9,10,11,12,13,14,15,208,209,210,211,212,213,214,215,..., dimensions={0} | all-to-all | bytes 524288 | tf_op jit(solution)/shard_map/all_to_all | solution.py:64
  86.0 7.7 %shard_map.116 = (f32[16,128]{1,0:T(8,128)}, f32[32,2,128]{2,1,0:T(2,128)}) custom-call(s32[1]{0:T(128)} %bitcast.owner_ref, s32[64]{0:T(128)} %target_ref.1, f32[32,16,128]{2,1,0:T(8,128)} %all_to_all.21.surfaces_ref, f32[3,216,128]{2,1,0:T(8,128)} %bitcast.15, f32[3,216,128]{2,1,0:T(8,128)} %bitcast.13, f32[3,216,128]{2,1,0:T(8,128)} %bitcast.6.high_ref, ...), custom_call_target="tpu_custom_call" | custom-call | tf_op jit(solution)/shard_map/pallas_call | solution.py:299
  93.6 1.3 %collective-permute-start.4 = (f32[16,128]{1,0:T(8,128)}, f32[16,128]{1,0:T(8,128)S(1)}, u32[]{:S(2)}, u32[]{:S(2)}) collective-permute-start(f32[16,128]{1,0:T(8,128)} %get-tuple-element.19), channel_id=1, source_target_pairs={{0,64},{1,65},{2,66},{3,67},{4,68},{5,69},{6,70},{7,71},{8,72},{9,... | collective-permute-start | bytes 24584 | tf_op jit(solution)/shard_map/ppermute | solution.py:60
  94.9 5.3 %all-to-all-start.3 = ((f32[32,2,128]{2,1,0:T(2,128)}), f32[32,2,128]{2,1,0:T(2,128)S(1)}, u32[]{:S(2)}, u32[]{:S(2)}) async-start(f32[32,2,128]{2,1,0:T(2,128)} %get-tuple-element.18), calls=%async_computation.3 | async-start | bytes 65536 | tf_op jit(solution)/shard_map/all_to_all | solution.py:64
  100.3 0.0 collective-permute-done.4
  100.3 1.3 %broadcast_select_fusion.1 = f32[16,128]{1,0:T(8,128)} fusion(f32[16,128]{1,0:T(8,128)} %get-tuple-element.19, f32[16,128]{1,0:T(8,128)S(1)} %collective-permute-done.4, pred[]{:T(512)S(6)} %or.4), kind=kLoop, calls=%fused_computation.8 | loop fusion | flops 2048 | bytes 24577 | tf_op jit(solution)/shard_map/jit(_where)/select_n | solution.py:60
  101.6 7.0 %all-to-all-done.3 = f32[32,2,128]{2,1,0:T(2,128)S(1)} async-done(((f32[32,2,128]{2,1,0:T(2,128)}), f32[32,2,128]{2,1,0:T(2,128)S(1)}, u32[]{:S(2)}, u32[]{:S(2)}) %all-to-all-start.3) | async-done | bytes 32800 | tf_op jit(solution)/shard_map/all_to_all | solution.py:64
  108.6 1.2 %multiply_reduce_fusion = f32[64,128]{1,0:T(8,128)S(1)} fusion(bf16[64,128,128]{2,1,0:T(8,128)(2,1)S(1)} %copy-done, f32[64,128]{1,0:T(8,128)S(1)} %bitcast.16), kind=kLoop, calls=%fused_computation | loop fusion | flops 3137536 | bytes 2162688 | tf_op jit(solution)/shard_map/reduce_sum | solution.py:309
  109.8 0.3 convolution_bitcast_fusion
  110.0 1.3 %collective-permute-start.5 = (f32[2048]{0:T(1024)S(1)}, f32[2048]{0:T(1024)S(1)}, u32[]{:S(2)}, u32[]{:S(2)}) collective-permute-start(f32[2048]{0:T(1024)S(1)} %convolution_bitcast_fusion), channel_id=1, source_target_pairs={{0,64},{1,65},{2,66},{3,67},{4,68},{5,69},{6,70},{7,71},{8,72},{9,... | collective-permute-start | bytes 24584 | tf_op jit(solution)/shard_map/ppermute | solution.py:60
  111.3 1.3 %collective-permute-done.5 = f32[2048]{0:T(1024)S(1)} collective-permute-done((f32[2048]{0:T(1024)S(1)}, f32[2048]{0:T(1024)S(1)}, u32[]{:S(2)}, u32[]{:S(2)}) %collective-permute-start.5) | collective-permute-done | bytes 8224 | tf_op jit(solution)/shard_map/ppermute | solution.py:60
  112.7 0.6 broadcast_select_fusion
  (9 shorter events, 0.0 us)
Async XLA Ops:
  14.3 13.1 %copy-start.4 = (f32[216,128]{1,0:T(8,128)S(1)}, f32[216,128]{1,0:T(8,128)}, u32[]{:S(2)}) copy-start(f32[216,128]{1,0:T(8,128)} %get-tuple-element.14) | copy-start | bytes 331780
  17.5 37.0 %all-to-all-start.1 = ((f32[32,40,128]{2,1,0:T(8,128)}), f32[32,40,128]{2,1,0:T(8,128)S(1)}, u32[]{:S(2)}, u32[]{:S(2)}) async-start(f32[32,40,128]{2,1,0:T(8,128)} %shard_map.114), calls=%async_computation.1 | async-start | bytes 1310720 | tf_op jit(solution)/shard_map/all_to_all | solution.py:64
  27.4 9.9 %collective-permute-start = (f32[216,128]{1,0:T(8,128)S(1)}, f32[216,128]{1,0:T(8,128)S(1)}, u32[]{:S(2)}, u32[]{:S(2)}) collective-permute-start(f32[216,128]{1,0:T(8,128)S(1)} %copy-done.4), channel_id=1, source_target_pairs={{223,0},{0,1},{1,2},{2,3},{3,4},{4,5},{5,6},{6,7},{7,8},{8,9},{9,1... | collective-permute-start | bytes 331784 | tf_op jit(solution)/shard_map/ppermute | solution.py:49
  30.7 7.9 %collective-permute-start.1 = (f32[216,128]{1,0:T(8,128)S(1)}, f32[216,128]{1,0:T(8,128)S(1)}, u32[]{:S(2)}, u32[]{:S(2)}) collective-permute-start(f32[216,128]{1,0:T(8,128)S(1)} %copy-done.4), channel_id=1, source_target_pairs={{1,0},{2,1},{3,2},{4,3},{5,4},{6,5},{7,6},{8,7},{9,8},{10,9},{11,1... | collective-permute-start | bytes 331784 | tf_op jit(solution)/shard_map/ppermute | solution.py:49
  37.3 71.3 %copy-start = (bf16[64,128,128]{2,1,0:T(8,128)(2,1)S(1)}, bf16[64,128,128]{2,1,0:T(8,128)(2,1)}, u32[]{:S(2)}) copy-start(bf16[64,128,128]{2,1,0:T(8,128)(2,1)} %weight_ref.3) | copy-start | bytes 6291460
  38.7 15.9 %copy-start.2 = (f32[648,128]{1,0:T(8,128)}, f32[648,128]{1,0:T(8,128)S(1)}, u32[]{:S(2)}) copy-start(f32[648,128]{1,0:T(8,128)S(1)} %constant_dynamic-update-slice_fusion) | copy-start | bytes 995332
  38.7 14.7 %collective-permute-start.2 = (f32[648,128]{1,0:T(8,128)S(1)}, f32[648,128]{1,0:T(8,128)S(1)}, u32[]{:S(2)}, u32[]{:S(2)}) collective-permute-start(f32[648,128]{1,0:T(8,128)S(1)} %constant_dynamic-update-slice_fusion), channel_id=1, source_target_pairs={{221,0},{222,1},{223,2},{0,3},{1,4},{2,5},{3,6},{4,7},{5,8},{6,9},... | collective-permute-start | bytes 995336 | tf_op jit(solution)/shard_map/ppermute | solution.py:49
  43.2 11.4 %collective-permute-start.3 = (f32[648,128]{1,0:T(8,128)S(1)}, f32[648,128]{1,0:T(8,128)}, u32[]{:S(2)}, u32[]{:S(2)}) collective-permute-start(f32[648,128]{1,0:T(8,128)S(1)} %constant_dynamic-update-slice_fusion), channel_id=1, source_target_pairs={{3,0},{4,1},{5,2},{6,3},{7,4},{8,5},{9,6},{10,7},{11,8},{12,9},{13... | collective-permute-start | bytes 995336 | tf_op jit(solution)/shard_map/ppermute | solution.py:49
  53.4 1.2 %copy-start.3 = (f32[648,128]{1,0:T(8,128)}, f32[648,128]{1,0:T(8,128)S(1)}, u32[]{:S(2)}) copy-start(f32[648,128]{1,0:T(8,128)S(1)} %collective-permute-done.2) | copy-start | bytes 995332
  54.6 0.8 copy-start.1
  63.4 46.4 %copy-start.5 = (s32[64]{0:T(128)S(1)}, s32[64]{0:T(128)}, u32[]{:S(2)}) copy-start(s32[64]{0:T(128)} %source_ref.1) | copy-start | bytes 772
  93.6 6.7 %collective-permute-start.4 = (f32[16,128]{1,0:T(8,128)}, f32[16,128]{1,0:T(8,128)S(1)}, u32[]{:S(2)}, u32[]{:S(2)}) collective-permute-start(f32[16,128]{1,0:T(8,128)} %get-tuple-element.19), channel_id=1, source_target_pairs={{0,64},{1,65},{2,66},{3,67},{4,68},{5,69},{6,70},{7,71},{8,72},{9,... | collective-permute-start | bytes 24584 | tf_op jit(solution)/shard_map/ppermute | solution.py:60
  94.9 13.6 %all-to-all-start.3 = ((f32[32,2,128]{2,1,0:T(2,128)}), f32[32,2,128]{2,1,0:T(2,128)S(1)}, u32[]{:S(2)}, u32[]{:S(2)}) async-start(f32[32,2,128]{2,1,0:T(2,128)} %get-tuple-element.18), calls=%async_computation.3 | async-start | bytes 65536 | tf_op jit(solution)/shard_map/all_to_all | solution.py:64
  110.0 2.6 %collective-permute-start.5 = (f32[2048]{0:T(1024)S(1)}, f32[2048]{0:T(1024)S(1)}, u32[]{:S(2)}, u32[]{:S(2)}) collective-permute-start(f32[2048]{0:T(1024)S(1)} %convolution_bitcast_fusion), channel_id=1, source_target_pairs={{0,64},{1,65},{2,66},{3,67},{4,68},{5,69},{6,70},{7,71},{8,72},{9,... | collective-permute-start | bytes 24584 | tf_op jit(solution)/shard_map/ppermute | solution.py:60
